TPU v7x, 32 devices: a whole 2x2x4 slice. The times are simulated.
32 devices in a mesh: gx: 8 (over z, x), gy: 4 (over y, core).
Axes of the slice: x: 2, y: 2, z: 4, core: 2. Of those that a mesh axis runs over, the one named last changes fastest.
Arguments:
- vectors: float32 [2, 128, 128, 548], P(None, 'gx', 'gy'), may hold values from -6 to 6
- diffusivity: float32 [128, 128], P('gx', 'gy'), may hold values from 0.2 to 0.25
- vertical_factor: float32 [548, 548], replicated, may hold values from -4 to 4, as said below
- weight_first: float32 [548, 768], replicated, may hold values from -0.25 to 0.25
- bias_first: float32 [768], replicated, may hold values from -3 to 3
- weight_second: float32 [768, 768], replicated, may hold values from -0.21875 to 0.21875
- bias_second: float32 [768], replicated, may hold values from -3 to 3
- weight_out: float32 [768, 616], replicated, may hold values from -0.21875 to 0.21875
- error_inverse: float32 [616, 616], replicated, may hold values from -4 to 4, as said below
- observed_column: int32 [16384], P(('gx', 'gy')), may hold values from 0 to 16383, as said below
- owner_count: int32 [32], P(('gx', 'gy')), may hold values from 16 to 512
- observed_state: float32 [16384, 548], P(('gx', 'gy')), may hold values from -6 to 6
- channel_mask: int32 [32, 616], replicated, may hold values 0 or 1
Outputs:
- products: float32 [2, 128, 128, 548], P(None, 'gx', 'gy')
Inputs may be any that keep to these rules, and one draw needn't show every extreme that they name: `observed_column`: tile (a, b) holds the cells i with i // 16 = a and j with j // 32 = b. Among the used slots of one owner at most 16 lie in any one tile, and some tile receives exactly 16 from every owner. Unused slots hold valid columns. `vertical_factor`: the identity plus a dense random part; well conditioned. `error_inverse`: symmetric positive definite with a dominant diagonal.
All inputs are finite; a program needn't handle non-finite values.
Results may differ from a plain program's by a relative error of at most 0.0003.
Values sent between devices are 32-bit elements; how exact they have to be, the bound alone decides.
No kernel may reach another device: no remote copies, remote signals or barrier semaphores. Data moves between devices by JAX's collectives and lax.ppermute only.
A program may use at most 128 MiB of HBM per device.

v0:
```python
import functools

import jax
import jax.numpy as jnp
from jax import lax
from jax.experimental import pallas as pl
from jax.experimental.pallas import tpu as pltpu
from jax.sharding import PartitionSpec as P

SWEEPS = 4
WIDE = 256
LANES = 128
BF = jnp.bfloat16
F32 = jnp.float32
NN = ((1,), (0,))
NT = ((1,), (1,))


def up(size, unit):
    return -(-size // unit) * unit


def split(value):
    high = value.astype(BF)
    return high, (value - high.astype(F32)).astype(BF)


def mm(left, right, dims=NN):
    return lax.dot_general(left, right, (dims, ((), ())), preferred_element_type=F32)


def mm3(left_high, left_low, right_high, right_low, dims=NN):
    return mm(left_high, right_high, dims) + (
        mm(left_high, right_low, dims) + mm(left_low, right_high, dims)
    )


def halves(size):
    half = size // 2
    return [pl.ds(0, half), pl.ds(half, half)] if half % 16 == 0 else [pl.ds(0, size)]


def iota(shape, axis):
    return lax.broadcasted_iota(jnp.int32, shape, axis)


def call(kernel, out_shape, flops, moved, scratch=(), vmem=48, **more):
    return pl.pallas_call(
        kernel,
        out_shape=out_shape,
        scratch_shapes=list(scratch),
        compiler_params=pltpu.CompilerParams(vmem_limit_bytes=vmem * 1024 * 1024),
        cost_estimate=pl.CostEstimate(flops=flops, bytes_accessed=moved, transcendentals=0),
        **more,
    )


def shaped(shape, dtype=F32):
    return jax.ShapeDtypeStruct(shape, dtype)


def pack_kernel(bucket, dest_ref, cell_ref, state_ref, out_ref, high_ref, low_ref):
    levels, slots = state_ref.shape
    devices = slots // bucket
    dest = dest_ref[...]
    same = (iota((devices, slots), 0) == dest).astype(F32)
    before = (iota((slots, slots), 0) < iota((slots, slots), 1)).astype(BF)
    rank = jnp.sum(same * mm(same.astype(BF), before), axis=0, keepdims=True)
    place = dest * bucket + rank.astype(jnp.int32)
    pick = (iota((slots, slots), 0) == place).astype(BF)
    high_ref[...] = jnp.zeros_like(high_ref)
    low_ref[...] = jnp.zeros_like(low_ref)
    high, low = split(state_ref[...])
    high_ref[:levels, :] = high
    low_ref[:levels, :] = low
    mark = up(levels, 16)
    tall = jnp.where(iota((16, slots), 0) == 0, cell_ref[...], 0.0)
    high, low = split(tall)
    high_ref[mark : mark + 16, :] = high
    low_ref[mark : mark + 16, :] = low
    out_ref[...] = mm(pick, high_ref[...], NT) + mm(pick, low_ref[...], NT)


def prep_kernel(*refs):
    ins, (first_out, stack_out), refs = refs[:5], refs[5:7], refs[7:]
    raw, (first, stack, turned, in_sem, out_sem) = refs[:5], refs[5:]
    fetch = [
        pltpu.make_async_copy(ins[k], raw[k], in_sem.at[k]) for k in range(5)
    ]
    for copy in fetch:
        copy.start()
    sends = []

    def send(source, target):
        copy = pltpu.make_async_copy(source, target, out_sem.at[len(sends)])
        copy.start()
        sends.append(copy)

    def put(values, ref):
        rows, cols = values.shape
        if (rows, cols) != ref.shape[1:]:
            ref[...] = jnp.zeros_like(ref)
        ref[0, :rows, :cols], ref[1, :rows, :cols] = split(values)

    fetch[0].wait()
    put(raw[0][...].T, turned)
    fetch[1].wait()
    put(raw[1][...], first)
    send(first, first_out)
    deep = turned.shape[2]
    for part in halves(turned.shape[1]):
        got = mm3(turned[0, part, :], turned[1, part, :], first[0, :deep], first[1, :deep])
        stack[3, 0, part, :], stack[3, 1, part, :] = split(got)
    send(stack.at[3], stack_out.at[3])
    for k in range(3):
        fetch[k + 2].wait()
        put(raw[k + 2][...], stack.at[k])
        send(stack.at[k], stack_out.at[k])
    for copy in sends:
        copy.wait()


def cut_kernel(vectors_ref, coeff_ref, *outs):
    pairs, rows, wide, levels = vectors_ref.shape
    w = SWEEPS
    parts = (
        (slice(0, w), slice(None)), (slice(rows - w, rows), slice(None)),
        (slice(None), slice(0, w)), (slice(None), slice(wide - w, wide)),
    )
    for v in range(pairs):
        for k, part in enumerate(parts):
            out = outs[4 * v + k]
            out[:, :, :levels] = vectors_ref[(v,) + part]
            if v == 0:
                out[:, :, levels:] = coeff_ref[part][:, :, :1]


def fill(ext, tile, xlo, xhi, ylo, yhi):
    rows, wide, levels = tile.shape
    w = SWEEPS
    last = up(levels, LANES) - LANES
    ext[:, :, last:] = jnp.zeros((ext.shape[0], ext.shape[1], ext.shape[2] - last), F32)
    ext[w : w + rows, :wide, :levels] = tile
    ext[:w, :wide, :levels] = xlo[:, :, :levels]
    ext[w + rows :, :wide, :levels] = xhi[:, :, :levels]
    ext[:, wide : wide + w, :levels] = yhi[:, :, :levels]
    ext[:, wide + w :, :levels] = ylo[:, :, :levels]


def diffuse_kernel(given, tile_ref, coeff_ref, *refs):
    strips, stack_ref, refs = refs[:4], refs[4], refs[5:]
    ext, work, high_ref, low_ref, both, sem = refs[-6:]
    out_ref = refs[0]
    fetch = pltpu.make_async_copy(stack_ref.at[3], both, sem)
    fetch.start()
    w = SWEEPS
    rows, wide, levels = tile_ref.shape[1:]
    tall = rows + 2 * w
    around = wide + 2 * w
    fill(ext, tile_ref[0], *strips)
    if given:
        cb_ref = coeff_ref
    else:
        cb_ref = refs[1]

        def spread(ref):
            column = ref[:, :, levels : levels + 1]
            return jnp.broadcast_to(column, column.shape[:2] + (LANES,))

        xlo, xhi, ylo, yhi = strips
        cb_ref[w : w + rows, :wide, :] = coeff_ref[...]
        cb_ref[:w, :wide, :] = spread(xlo)
        cb_ref[w + rows :, :wide, :] = spread(xhi)
        cb_ref[:, wide : wide + w, :] = spread(yhi)
        cb_ref[:, wide + w :, :] = spread(ylo)

    def chunk(j, _):
        lanes = pl.ds(pl.multiple_of(j * LANES, LANES), LANES)
        for sweep in range(SWEEPS):
            for i in range(sweep + 1, tall - 1 - sweep):
                if sweep == 0:
                    above, mid, below = (ext[k, :, lanes] for k in (i - 1, i, i + 1))
                else:
                    above, mid, below = (work[(sweep + 1) % 2, k] for k in (i - 1, i, i + 1))
                beside = above + below + pltpu.roll(mid, 1, 0) + pltpu.roll(mid, around - 1, 0)
                new = mid + cb_ref[i] * (beside - 4.0 * mid)
                if sweep == SWEEPS - 1:
                    high, low = split(new[:wide])
                    here = pl.ds((i - w) * wide, wide)
                    high_ref[here, lanes] = high
                    low_ref[here, lanes] = low
                else:
                    work[sweep % 2, i] = new
        return 0

    lax.fori_loop(0, ext.shape[2] // LANES, chunk, 0)
    deep = ext.shape[2]
    fetch.wait()
    for part in halves(out_ref.shape[0]):
        out_ref[part, :] = mm3(
            high_ref[part, :], low_ref[part, :], both[0, :deep], both[1, :deep]
        )


def hidden_kernel(
    mark, bucket, x_ref, first_ref, b1_ref, stack_ref, b2_ref, mask_ref,
    scale_ref, one_ref, one_t_ref, high_ref, low_ref, first, second, sems,
):
    fetch_first = pltpu.make_async_copy(first_ref, first, sems.at[0])
    fetch_second = pltpu.make_async_copy(stack_ref.at[0], second, sems.at[1])
    fetch_first.start()
    fetch_second.start()
    s1_ref, s2_ref, gate_ref = (scale_ref.at[k] for k in range(3))
    slots, deep = x_ref.shape
    cells = one_ref.shape[1]
    devices, channels = mask_ref.shape
    index = x_ref[:, mark : mark + 1]
    cell = index.astype(jnp.int32) - 1
    live = index > 0.5
    one_ref[...] = (iota((slots, cells), 1) == cell).astype(BF)
    flat = jnp.broadcast_to(index, (slots, LANES)).T[0:1, :].astype(jnp.int32) - 1
    one_t_ref[...] = (iota((cells, slots), 0) == flat).astype(BF)
    begin = iota((slots, devices), 1) * bucket
    at = iota((slots, devices), 0)
    from_owner = ((at >= begin) & (at < begin + bucket) & live).astype(BF)
    gate_ref[...] = jnp.zeros_like(gate_ref)
    gate_ref[:, :channels] = mm(from_owner, mask_ref[...].astype(F32).astype(BF))
    high, low = split(x_ref[...])
    high_ref[:, :deep] = high
    low_ref[:, :deep] = low
    parts = halves(slots)
    fetch_first.wait()
    for part in parts:
        got = mm3(high_ref[part, :deep], low_ref[part, :deep], first[0, :deep], first[1, :deep])
        hidden = jnp.tanh(got + b1_ref[...])
        s1_ref[part, :] = 1.0 - hidden * hidden
        high, low = split(hidden)
        high_ref[part, :] = high
        low_ref[part, :] = low
    fetch_second.wait()
    for part in parts:
        got = mm3(high_ref[part, :], low_ref[part, :], second[0], second[1])
        hidden = jnp.tanh(got + b2_ref[...])
        s2_ref[part, :] = 1.0 - hidden * hidden


LAYERS = ((0, 0, 1), (1, 1, 2), (2, 0, 2), (1, 0, 1), (0, 1, 0))


def table(values, layer):
    value = jnp.int32(values[0])
    for k in range(1, len(values)):
        value = jnp.where(layer == k, values[k], value)
    return value


def net_kernel(
    q_ref, one_ref, one_t_ref, scale_ref, stack_ref,
    out_ref, xhead, xtail, yhead, ytail, x1, top, low, acc_top, acc_low, stack, sems,
):
    fetch = [
        pltpu.make_async_copy(stack_ref.at[k], stack.at[k], sems.at[k]) for k in range(4)
    ]
    for copy in fetch:
        copy.start()
    slots = q_ref.shape[0]
    half = slots // 2
    first, second = pl.ds(0, half), pl.ds(half, half)

    def pick(picker):
        return mm(picker, x1[0]) + mm(picker, x1[1])

    def close(acc, scale, part, target):
        target[0], target[1] = split(acc[...] * scale_ref[scale, part, :])

    x1[0], x1[1] = split(q_ref[...])
    acc_top[...] = pick(one_ref[first, :])
    acc_low[...] = pick(one_ref[second, :])
    close(acc_top, 0, first, top)
    fetch[0].wait()
    scales = [0] + [entry[2] for entry in LAYERS]

    def step(layer, _):
        for k in (1, 2):

            @pl.when(layer == k)
            def _():
                fetch[k].wait()

        weight = table([entry[0] for entry in LAYERS], layer)
        turned = table([entry[1] for entry in LAYERS], layer)
        before, after = table(scales[:-1], layer), table(scales[1:], layer)

        def run(dims):
            acc_top[...] = mm3(top[0], top[1], stack[weight, 0], stack[weight, 1], dims)
            close(acc_low, before, second, low)
            acc_low[...] = mm3(low[0], low[1], stack[weight, 0], stack[weight, 1], dims)
            close(acc_top, after, first, top)

        @pl.when(turned == 0)
        def _():
            run(NN)

        @pl.when(turned == 1)
        def _():
            run(NT)

        return 0

    lax.fori_loop(0, len(LAYERS), step, 0)
    close(acc_low, scales[-1], second, low)
    for part in halves(one_t_ref.shape[0]):
        got = mm(one_t_ref[part, :half], top[0]) + mm(one_t_ref[part, :half], top[1])
        got = got + mm(one_t_ref[part, half:], low[0]) + mm(one_t_ref[part, half:], low[1])
        x1[0, part, :], x1[1, part, :] = split(got)
    fetch[3].wait()
    rows, wide, levels = out_ref.shape
    for k, part in enumerate(halves(rows * wide)):
        got = mm3(x1[0, part, :], x1[1, part, :], stack[3, 0], stack[3, 1], NT)
        tall = got.shape[0] // wide
        got = got.reshape(tall, wide, got.shape[1])[:, :, :levels]
        here = pl.ds(k * tall, tall)
        out_ref[here] = got
        if k == 0:
            xhead[...] = got[:SWEEPS]
        if (k + 1) * tall == rows:
            xtail[...] = got[tall - SWEEPS :]
        yhead[here] = got[:, :SWEEPS]
        ytail[here] = got[:, wide - SWEEPS :]


def finish_kernel(field_ref, base_ref, cb_ref, *refs):
    out_ref, ext, work, total = refs[-4:]
    w = SWEEPS
    rows, wide, levels = field_ref.shape
    tall = rows + 2 * w
    fill(ext, field_ref[...], *refs[:4])
    around = wide + 2 * w

    def chunk(j, _):
        lanes = pl.ds(pl.multiple_of(j * LANES, LANES), LANES)
        for sweep in range(SWEEPS):

            def read(k):
                value = ext[k, :, lanes] if sweep == 0 else work[(sweep + 1) % 2, k]
                return value, cb_ref[k] * value

            above = read(sweep)
            mid = read(sweep + 1)
            for i in range(sweep + 1, tall - 1 - sweep):
                below = read(i + 1)
                scaled = mid[1]
                beside = (
                    above[1] + below[1]
                    + pltpu.roll(scaled, 1, 0) + pltpu.roll(scaled, around - 1, 0)
                )
                new = mid[0] + (beside - 4.0 * scaled)
                if sweep == SWEEPS - 1:
                    total[i - w, :, lanes] = new[:wide]
                else:
                    work[sweep % 2, i] = new
                above, mid = mid, below
        return 0

    lax.fori_loop(0, ext.shape[2] // LANES, chunk, 0)
    out_ref[0] = base_ref[0] + total[:, :, :levels]


def shift(value, axis, by):
    count = lax.axis_size(axis)
    return lax.ppermute(
        value, axis, [(i, i + by) for i in range(count) if 0 <= i + by < count]
    )


def halo(xhead, xtail, yhead, ytail):
    xlo = shift(xtail, "gx", 1)
    xhi = shift(xhead, "gx", -1)
    last = jnp.concatenate([xlo[:, -SWEEPS:], ytail, xhi[:, -SWEEPS:]], axis=0)
    head = jnp.concatenate([xlo[:, :SWEEPS], yhead, xhi[:, :SWEEPS]], axis=0)
    ylo = shift(last, "gy", 1)
    yhi = shift(head, "gy", -1)
    return xlo, xhi, ylo, yhi


def body(
    vectors, diffusivity, vertical_factor, weight_first, bias_first, weight_second,
    bias_second, weight_out, error_inverse, observed_column, owner_count,
    observed_state, channel_mask,
):
    pairs, tile_x, tile_y, levels = vectors.shape
    count_y = lax.axis_size("gy")
    devices = lax.axis_size("gx") * count_y
    slots = observed_column.shape[0]
    bucket = slots // devices
    cells = tile_x * tile_y
    grid_wide = tile_y * count_y
    units = weight_second.shape[0]
    deep = up(levels, LANES)
    tall, around = tile_x + 2 * SWEEPS, tile_y + 2 * SWEEPS
    full_l, full_u = up(levels, WIDE), up(units, WIDE)
    full_c = up(error_inverse.shape[0], WIDE)
    mark = up(levels, 16)

    coeff = jnp.broadcast_to(diffusivity[:, :, None], (tile_x, tile_y, LANES))
    shapes = []
    for v in range(pairs):
        deep_v = levels + (v == 0)
        shapes += [shaped((SWEEPS, tile_y, deep_v))] * 2 + [shaped((tile_x, SWEEPS, deep_v))] * 2
    cuts = call(cut_kernel, shapes, flops=0, moved=8 * vectors.size, vmem=16)(vectors, coeff)
    strips = [halo(*cuts[4 * v : 4 * v + 4]) for v in range(pairs)]

    position = jnp.arange(slots, dtype=jnp.int32)
    grid_row = observed_column // grid_wide
    grid_col = observed_column % grid_wide
    target = grid_row // tile_x * count_y + grid_col // tile_y
    dest = jnp.where(position < owner_count[0], target, -1)
    cell = (grid_row % tile_x * tile_y + grid_col % tile_y + 1).astype(F32)
    packed = call(
        functools.partial(pack_kernel, bucket),
        shaped((slots, deep)),
        flops=6 * slots * slots * deep,
        moved=8 * slots * deep,
        scratch=[pltpu.VMEM((deep, slots), BF)] * 2,
        vmem=12,
    )(dest[None, :], cell[None, :], observed_state.T)
    carried = lax.all_to_all(
        packed.reshape(devices, bucket, deep), ("gx", "gy"), split_axis=0,
        concat_axis=0, tiled=True,
    ).reshape(slots, deep)

    side = max(full_l, full_u, full_c)
    far = pl.BlockSpec(memory_space=pltpu.HBM)
    weights = (vertical_factor, weight_first, weight_second, weight_out.T, error_inverse)
    first, stack = call(
        prep_kernel,
        [pltpu.HBM((2, full_l, side), BF), pltpu.HBM((4, 2, side, side), BF)],
        flops=6 * full_l * full_l * full_u,
        moved=8 * 5 * full_u * full_u,
        scratch=[pltpu.VMEM(weight.shape, F32) for weight in weights]
        + [
            pltpu.VMEM((2, full_l, side), BF), pltpu.VMEM((4, 2, side, side), BF),
            pltpu.VMEM((2, side, full_l), BF),
            pltpu.SemaphoreType.DMA((5,)), pltpu.SemaphoreType.DMA((5,)),
        ],
        vmem=34,
        in_specs=[far] * 5,
        out_specs=[far] * 2,
    )(*[pltpu.with_memory_space_constraint(weight, pltpu.HBM) for weight in weights])
    first, stack = (pltpu.with_memory_space_constraint(x, pltpu.HBM) for x in (first, stack))

    whole = pl.BlockSpec(memory_space=pltpu.VMEM)

    def wide_bias(bias):
        return jnp.pad(bias, (0, side - bias.shape[0]))[None, :]

    def block(v):
        return pl.BlockSpec((1, tile_x, tile_y, levels), lambda i: (v, 0, 0, 0))

    queries = []
    for v in range(pairs):
        got = call(
            functools.partial(diffuse_kernel, v > 0),
            [shaped((cells, side))] + [shaped((tall, around, LANES))] * (v == 0),
            flops=6 * cells * deep * full_u,
            moved=8 * tall * around * deep,
            scratch=[
                pltpu.VMEM((tall, around, deep), F32),
                pltpu.VMEM((2, tall, around, LANES), F32),
                pltpu.VMEM((cells, deep), BF),
                pltpu.VMEM((cells, deep), BF),
                pltpu.VMEM((2, side, side), BF),
                pltpu.SemaphoreType.DMA,
            ],
            grid=(1,),
            vmem=18,
            in_specs=[block(v)] + [whole] * 5 + [far],
            out_specs=[whole] * (2 - (v > 0)),
        )(vectors, spread if v else coeff, *strips[v], stack)
        queries.append(got[0])
        if v == 0:
            spread = got[1]

    scale, one, one_t = call(
        functools.partial(hidden_kernel, mark, bucket),
        [shaped((3, slots, side)), shaped((slots, cells), BF), shaped((cells, slots), BF)],
        flops=12 * slots * full_u * full_u,
        moved=8 * slots * full_u,
        scratch=[pltpu.VMEM((slots, side), BF)] * 2
        + [
            pltpu.VMEM((2, full_l, side), BF), pltpu.VMEM((2, side, side), BF),
            pltpu.SemaphoreType.DMA((2,)),
        ],
        vmem=24,
        in_specs=[whole, far, whole, far, whole, whole],
    )(carried, first, wide_bias(bias_first), stack, wide_bias(bias_second), channel_mask)

    fields = []
    for v in range(pairs):
        fields.append(
            call(
                net_kernel,
                [shaped((tile_x, tile_y, levels))]
                + [shaped((SWEEPS, tile_y, levels))] * 2
                + [shaped((tile_x, SWEEPS, levels))] * 2,
                flops=36 * slots * full_u * full_u,
                moved=4 * 5 * full_u * full_u,
                scratch=[pltpu.VMEM((2, slots, side), BF)]
                + [pltpu.VMEM((2, slots // 2, side), BF)] * 2
                + [pltpu.VMEM((slots // 2, side), F32)] * 2
                + [
                    pltpu.VMEM((4, 2, side, side), BF),
                    pltpu.SemaphoreType.DMA((4,)),
                ],
                vmem=30,
                in_specs=[whole] * 4 + [far],
            )(queries[v], one, one_t, scale, stack)
        )

    out = None
    for v in range(pairs):
        around_field = halo(*fields[v][1:])
        carry = [] if out is None else [out]
        out = call(
            finish_kernel,
            shaped(vectors.shape),
            flops=40 * tall * around * deep,
            moved=12 * cells * deep,
            scratch=[
                pltpu.VMEM((tall, around, deep), F32),
                pltpu.VMEM((2, tall, around, LANES), F32),
                pltpu.VMEM((tile_x, tile_y, deep), F32),
            ],
            grid=(1,),
            vmem=18,
            in_specs=[whole, block(v)] + [whole] * 5
            + [pl.BlockSpec(memory_space=pl.ANY)] * len(carry),
            out_specs=block(v),
            input_output_aliases={7: 0} if carry else {},
        )(fields[v][0], vectors, spread, *around_field, *carry)
    return out


def solution(mesh):
    in_specs = (
        P(None, "gx", "gy", None),
        P("gx", "gy"),
        P(),
        P(),
        P(),
        P(),
        P(),
        P(),
        P(),
        P(("gx", "gy")),
        P(("gx", "gy")),
        P(("gx", "gy"), None),
        P(),
    )
    out_specs = P(None, "gx", "gy", None)
    return jax.shard_map(body, mesh=mesh, in_specs=in_specs, out_specs=out_specs, check_vma=False)
```

profile of v0, /device:TPU:9, one launch (start us, length us, event | category | flops | bytes accessed | tf_op | source)
XLA Modules:
  0.0 163.3 jit_solution(1142390221832046415)
XLA Ops:
  1.4 1.2 copy-done.6
  2.6 1.2 shard_map.131
  4.9 6.4 %all-to-all-start = ((f32[32,16,640]{2,1,0:T(8,128)}), f32[32,16,640]{2,1,0:T(8,128)}, u32[]{:S(2)}, u32[]{:S(2)}) async-start(f32[32,16,640]{2,1,0:T(8,128)} %bitcast.8), calls=%async_computation | async-start | bytes 2621440 | tf_op jit(solution)/shard_map/all_to_all | solution.py:427
  11.6 3.1 %collective-permute-start.4 = (f32[4,32,548]{2,1,0:T(8,128)S(1)}, f32[4,32,548]{2,1,0:T(8,128)S(1)}, u32[]{:S(2)}, u32[]{:S(2)}) collective-permute-start(f32[4,32,548]{2,1,0:T(8,128)S(1)} %get-tuple-element.36), channel_id=1, source_target_pairs={{0,4},{4,8},{8,12},{12,16},{16,20},{20,24},{24,28},{1,5},{5,9},{9,... | collective-permute-start | bytes 841736 | tf_op jit(solution)/shard_map/ppermute | solution.py:371
  14.7 3.1 %collective-permute-start.5 = (f32[4,32,548]{2,1,0:T(8,128)S(1)}, f32[4,32,548]{2,1,0:T(8,128)S(1)}, u32[]{:S(2)}, u32[]{:S(2)}) collective-permute-start(f32[4,32,548]{2,1,0:T(8,128)S(1)} %get-tuple-element.37), channel_id=1, source_target_pairs={{4,0},{8,4},{12,8},{16,12},{20,16},{24,20},{28,24},{5,1},{9,5},{13... | collective-permute-start | bytes 841736 | tf_op jit(solution)/shard_map/ppermute | solution.py:371
  17.8 2.2 %collective-permute-start = (f32[4,32,549]{2,1,0:T(8,128)S(1)}, f32[4,32,549]{2,1,0:T(8,128)S(1)}, u32[]{:S(2)}, u32[]{:S(2)}) collective-permute-start(f32[4,32,549]{2,1,0:T(8,128)S(1)} %get-tuple-element.30), channel_id=1, source_target_pairs={{0,4},{4,8},{8,12},{12,16},{16,20},{20,24},{24,28},{1,5},{5,9},{9,... | collective-permute-start | bytes 843272 | tf_op jit(solution)/shard_map/ppermute | solution.py:371
  20.0 4.0 %collective-permute-start.1 = (f32[4,32,549]{2,1,0:T(8,128)S(1)}, f32[4,32,549]{2,1,0:T(8,128)S(1)}, u32[]{:S(2)}, u32[]{:S(2)}) collective-permute-start(f32[4,32,549]{2,1,0:T(8,128)S(1)} %get-tuple-element.31), channel_id=1, source_target_pairs={{4,0},{8,4},{12,8},{16,12},{20,16},{24,20},{28,24},{5,1},{9,5},{13... | collective-permute-start | bytes 843272 | tf_op jit(solution)/shard_map/ppermute | solution.py:371
  24.0 18.7 %collective-permute-done.4.refs_0_ = f32[4,32,548]{2,1,0:T(8,128)S(1)} collective-permute-done((f32[4,32,548]{2,1,0:T(8,128)S(1)}, f32[4,32,548]{2,1,0:T(8,128)S(1)}, u32[]{:S(2)}, u32[]{:S(2)}) %collective-permute-start.4) | collective-permute-done | bytes 280608 | tf_op jit(solution)/shard_map/ppermute | solution.py:371
  42.8 4.7 %collective-permute-start.6 = (f32[24,4,548]{2,1,0:T(4,128)S(1)}, f32[24,4,548]{2,1,0:T(4,128)S(1)}, u32[]{:S(2)}, u32[]{:S(2)}) collective-permute-start(f32[24,4,548]{2,1,0:T(4,128)S(1)} %pad_maximum_fusion.2), channel_id=1, source_target_pairs={{0,1},{1,2},{2,3},{4,5},{5,6},{6,7},{8,9},{9,10},{10,11},{12,13},{... | collective-permute-start | bytes 631304 | tf_op jit(solution)/shard_map/ppermute | solution.py:371
  47.6 1.9 %collective-permute-start.7 = (f32[24,4,548]{2,1,0:T(4,128)S(1)}, f32[24,4,548]{2,1,0:T(4,128)S(1)}, u32[]{:S(2)}, u32[]{:S(2)}) collective-permute-start(f32[24,4,548]{2,1,0:T(4,128)S(1)} %pad_maximum_fusion.3), channel_id=1, source_target_pairs={{1,0},{2,1},{3,2},{5,4},{6,5},{7,6},{9,8},{10,9},{11,10},{13,12},{... | collective-permute-start | bytes 631304 | tf_op jit(solution)/shard_map/ppermute | solution.py:371
  49.9 5.7 %collective-permute-done.1.refs_1_ = f32[4,32,549]{2,1,0:T(8,128)S(1)} collective-permute-done((f32[4,32,549]{2,1,0:T(8,128)S(1)}, f32[4,32,549]{2,1,0:T(8,128)S(1)}, u32[]{:S(2)}, u32[]{:S(2)}) %collective-permute-start.1) | collective-permute-done | bytes 281120 | tf_op jit(solution)/shard_map/ppermute | solution.py:371
  55.7 2.5 %collective-permute-start.3 = (f32[24,4,549]{2,1,0:T(4,128)S(1)}, f32[24,4,549]{2,1,0:T(4,128)S(1)}, u32[]{:S(2)}, u32[]{:S(2)}) collective-permute-start(f32[24,4,549]{2,1,0:T(4,128)S(1)} %pad_maximum_fusion.1), channel_id=1, source_target_pairs={{1,0},{2,1},{3,2},{5,4},{6,5},{7,6},{9,8},{10,9},{11,10},{13,12},{... | collective-permute-start | bytes 632456 | tf_op jit(solution)/shard_map/ppermute | solution.py:371
  58.3 3.2 %collective-permute-start.2 = (f32[24,4,549]{2,1,0:T(4,128)S(1)}, f32[24,4,549]{2,1,0:T(4,128)S(1)}, u32[]{:S(2)}, u32[]{:S(2)}) collective-permute-start(f32[24,4,549]{2,1,0:T(4,128)S(1)} %pad_maximum_fusion), channel_id=1, source_target_pairs={{0,1},{1,2},{2,3},{4,5},{5,6},{6,7},{8,9},{9,10},{10,11},{12,13},{... | collective-permute-start | bytes 632456 | tf_op jit(solution)/shard_map/ppermute | solution.py:371
  61.5 8.5 %shard_map.128 = (bf16[2,768,768]{2,1,0:T(8,128)(2,1)}, bf16[4,2,768,768]{3,2,1,0:T(8,128)(2,1)}) custom-call(f32[548,548]{1,0:T(8,128)} %refs_0_.1, f32[548,768]{1,0:T(8,128)} %refs_1_.1, f32[768,768]{1,0:T(8,128)} %refs_2_.1, f32[616,768]{1,0:T(8,128)} %bitcast.12, f32[616,616]{1,0:T(8,128)} %refs_4_.1), custom_call_target="tpu_custom_call" | custom-call | flops 2717908992 | bytes 23592960 | tf_op jit(solution)/shard_map/pallas_call | solution.py:435
  70.2 5.7 %shard_map.129 = (f32[512,768]{1,0:T(8,128)S(1)}, f32[24,40,128]{2,1,0:T(8,128)S(1)}) custom-call(f32[2,16,32,548]{3,2,1,0:T(8,128)S(1)} %copy-done, f32[16,32,128]{2,1,0:T(8,128)S(1)} %broadcast_in_dim.20.coeff_ref, f32[4,32,549]{2,1,0:T(8,128)S(1)} %collective-permute-done.refs_0_, f32[4,32,549]{2,1,0:T(8,128)S(1)} %collective-permute-done.1.refs_1_, ...), custom_call_target="tpu_custom_call" | custom-call | flops 1509949440 | bytes 4915200 | tf_op jit(solution)/shard_map/pallas_call | solution.py:462
  75.9 1.2 copy-done.4
  77.1 5.5 %shard_map.130.q_ref = f32[512,768]{1,0:T(8,128)S(1)} custom-call(f32[2,16,32,548]{3,2,1,0:T(8,128)S(1)} %copy-done, f32[24,40,128]{2,1,0:T(8,128)S(1)} %get-tuple-element.35.coeff_ref.cb_ref, f32[4,32,548]{2,1,0:T(8,128)S(1)} %collective-permute-done.4.refs_0_, f32[4,32,548]{2,1,0:T(8,128)S(1)} %collective-permute-done.5.refs_1_, ...), custom_call_target="tpu_custom_call" | custom-call | flops 1509949440 | bytes 4915200 | tf_op jit(solution)/shard_map/pallas_call | solution.py:462
  83.7 7.3 %shard_map.132 = (f32[3,512,768]{2,1,0:T(8,128)S(1)}, bf16[512,512]{1,0:T(8,128)(2,1)S(1)}, bf16[512,512]{1,0:T(8,128)(2,1)S(1)}) custom-call(f32[512,640]{1,0:T(8,128)} %bitcast.6.x_ref, bf16[2,768,768]{2,1,0:T(8,128)(2,1)} %get-tuple-element.40.first_ref, f32[1,768]{1,0:T(1,128)S(1)} %broadcast_in_dim.23.b1_ref, ...), custom_call_target="tpu_custom_call" | custom-call | flops 3623878656 | bytes 3145728 | tf_op jit(solution)/shard_map/pallas_call | solution.py:484
  91.0 16.0 %shard_map.134 = (f32[16,32,548]{2,1,0:T(8,128)S(1)}, f32[4,32,548]{2,1,0:T(8,128)S(1)}, f32[4,32,548]{2,1,0:T(8,128)S(1)}, f32[16,4,548]{2,1,0:T(4,128)S(1)}, f32[16,4,548]{2,1,0:T(4,128)S(1)}) custom-call(f32[512,768]{1,0:T(8,128)S(1)} %copy-done.5, bf16[512,512]{1,0:T(8,128)(2,1)S(1)} %get-tuple-element.41.one_ref, ...), custom_call_target="tpu_custom_call" | custom-call | flops 10871635968 | bytes 11796480 | tf_op jit(solution)/shard_map/pallas_call | solution.py:501
  107.0 3.0 %collective-permute-start.12 = (f32[4,32,548]{2,1,0:T(8,128)S(1)}, f32[4,32,548]{2,1,0:T(8,128)S(1)}, u32[]{:S(2)}, u32[]{:S(2)}) collective-permute-start(f32[4,32,548]{2,1,0:T(8,128)S(1)} %get-tuple-element.51), channel_id=1, source_target_pairs={{0,4},{4,8},{8,12},{12,16},{16,20},{20,24},{24,28},{1,5},{5,9},{9,... | collective-permute-start | bytes 841736 | tf_op jit(solution)/shard_map/ppermute | solution.py:371
  110.0 3.2 %collective-permute-start.13 = (f32[4,32,548]{2,1,0:T(8,128)S(1)}, f32[4,32,548]{2,1,0:T(8,128)S(1)}, u32[]{:S(2)}, u32[]{:S(2)}) collective-permute-start(f32[4,32,548]{2,1,0:T(8,128)S(1)} %get-tuple-element.52), channel_id=1, source_target_pairs={{4,0},{8,4},{12,8},{16,12},{20,16},{24,20},{28,24},{5,1},{9,5},{13... | collective-permute-start | bytes 841736 | tf_op jit(solution)/shard_map/ppermute | solution.py:371
  113.2 15.8 %shard_map.133 = (f32[16,32,548]{2,1,0:T(8,128)S(1)}, f32[4,32,548]{2,1,0:T(8,128)S(1)}, f32[4,32,548]{2,1,0:T(8,128)S(1)}, f32[16,4,548]{2,1,0:T(4,128)S(1)}, f32[16,4,548]{2,1,0:T(4,128)S(1)}) custom-call(f32[512,768]{1,0:T(8,128)S(1)} %copy-done.2, bf16[512,512]{1,0:T(8,128)(2,1)S(1)} %get-tuple-element.41.one_ref, ...), custom_call_target="tpu_custom_call" | custom-call | flops 10871635968 | bytes 11796480 | tf_op jit(solution)/shard_map/pallas_call | solution.py:501
  129.0 2.1 %collective-permute-start.8 = (f32[4,32,548]{2,1,0:T(8,128)S(1)}, f32[4,32,548]{2,1,0:T(8,128)S(1)}, u32[]{:S(2)}, u32[]{:S(2)}) collective-permute-start(f32[4,32,548]{2,1,0:T(8,128)S(1)} %get-tuple-element.45), channel_id=1, source_target_pairs={{0,4},{4,8},{8,12},{12,16},{16,20},{20,24},{24,28},{1,5},{5,9},{9,... | collective-permute-start | bytes 841736 | tf_op jit(solution)/shard_map/ppermute | solution.py:371
  131.0 4.1 %collective-permute-start.9 = (f32[4,32,548]{2,1,0:T(8,128)S(1)}, f32[4,32,548]{2,1,0:T(8,128)S(1)}, u32[]{:S(2)}, u32[]{:S(2)}) collective-permute-start(f32[4,32,548]{2,1,0:T(8,128)S(1)} %get-tuple-element.46), channel_id=1, source_target_pairs={{4,0},{8,4},{12,8},{16,12},{20,16},{24,20},{28,24},{5,1},{9,5},{13... | collective-permute-start | bytes 841736 | tf_op jit(solution)/shard_map/ppermute | solution.py:371
  135.3 2.3 %collective-permute-start.15 = (f32[24,4,548]{2,1,0:T(4,128)S(1)}, f32[24,4,548]{2,1,0:T(4,128)S(1)}, u32[]{:S(2)}, u32[]{:S(2)}) collective-permute-start(f32[24,4,548]{2,1,0:T(4,128)S(1)} %pad_maximum_fusion.7), channel_id=1, source_target_pairs={{1,0},{2,1},{3,2},{5,4},{6,5},{7,6},{9,8},{10,9},{11,10},{13,12},{... | collective-permute-start | bytes 631304 | tf_op jit(solution)/shard_map/ppermute | solution.py:371
  137.6 3.3 %collective-permute-start.14 = (f32[24,4,548]{2,1,0:T(4,128)S(1)}, f32[24,4,548]{2,1,0:T(4,128)S(1)}, u32[]{:S(2)}, u32[]{:S(2)}) collective-permute-start(f32[24,4,548]{2,1,0:T(4,128)S(1)} %pad_maximum_fusion.6), channel_id=1, source_target_pairs={{0,1},{1,2},{2,3},{4,5},{5,6},{6,7},{8,9},{9,10},{10,11},{12,13},{... | collective-permute-start | bytes 631304 | tf_op jit(solution)/shard_map/ppermute | solution.py:371
  141.0 4.2 %collective-permute-done.8.refs_0_ = f32[4,32,548]{2,1,0:T(8,128)S(1)} collective-permute-done((f32[4,32,548]{2,1,0:T(8,128)S(1)}, f32[4,32,548]{2,1,0:T(8,128)S(1)}, u32[]{:S(2)}, u32[]{:S(2)}) %collective-permute-start.8) | collective-permute-done | bytes 280608 | tf_op jit(solution)/shard_map/ppermute | solution.py:371
  145.2 3.3 %collective-permute-done.9.refs_1_ = f32[4,32,548]{2,1,0:T(8,128)S(1)} collective-permute-done((f32[4,32,548]{2,1,0:T(8,128)S(1)}, f32[4,32,548]{2,1,0:T(8,128)S(1)}, u32[]{:S(2)}, u32[]{:S(2)}) %collective-permute-start.9) | collective-permute-done | bytes 280608 | tf_op jit(solution)/shard_map/ppermute | solution.py:371
  148.6 2.3 %collective-permute-start.11 = (f32[24,4,548]{2,1,0:T(4,128)S(1)}, f32[24,4,548]{2,1,0:T(4,128)S(1)}, u32[]{:S(2)}, u32[]{:S(2)}) collective-permute-start(f32[24,4,548]{2,1,0:T(4,128)S(1)} %pad_maximum_fusion.5), channel_id=1, source_target_pairs={{1,0},{2,1},{3,2},{5,4},{6,5},{7,6},{9,8},{10,9},{11,10},{13,12},{... | collective-permute-start | bytes 631304 | tf_op jit(solution)/shard_map/ppermute | solution.py:371
  151.0 3.2 %collective-permute-start.10 = (f32[24,4,548]{2,1,0:T(4,128)S(1)}, f32[24,4,548]{2,1,0:T(4,128)S(1)}, u32[]{:S(2)}, u32[]{:S(2)}) collective-permute-start(f32[24,4,548]{2,1,0:T(4,128)S(1)} %pad_maximum_fusion.4), channel_id=1, source_target_pairs={{0,1},{1,2},{2,3},{4,5},{5,6},{6,7},{8,9},{9,10},{10,11},{12,13},{... | collective-permute-start | bytes 631304 | tf_op jit(solution)/shard_map/ppermute | solution.py:371
  154.3 4.5 %shard_map.135.refs_4_ = f32[2,16,32,548]{3,2,1,0:T(8,128)} custom-call(f32[16,32,548]{2,1,0:T(8,128)S(1)} %get-tuple-element.50.field_ref, f32[2,16,32,548]{3,2,1,0:T(8,128)S(1)} %copy-done, f32[24,40,128]{2,1,0:T(8,128)S(1)} %get-tuple-element.35.coeff_ref.cb_ref, f32[4,32,548]{2,1,0:T(8,128)S(1)} %collective-permute-done.12.refs_0_, ...), custom_call_target="tpu_custom_call" | custom-call | flops 24576000 | bytes 3932160 | tf_op jit(solution)/shard_map/pallas_call | solution.py:524
  158.8 4.5 %shard_map.136 = f32[2,16,32,548]{3,2,1,0:T(8,128)} custom-call(f32[16,32,548]{2,1,0:T(8,128)S(1)} %get-tuple-element.44.field_ref, f32[2,16,32,548]{3,2,1,0:T(8,128)S(1)} %copy-done, f32[24,40,128]{2,1,0:T(8,128)S(1)} %get-tuple-element.35.coeff_ref.cb_ref, f32[4,32,548]{2,1,0:T(8,128)S(1)} %collective-permute-done.8.refs_0_, ...), custom_call_target="tpu_custom_call", output_to_operand_aliasing={{}: (7, {})} | custom-call | flops 24576000 | bytes 3932160 | tf_op jit(solution)/shard_map/pallas_call | solution.py:524
  (54 shorter events, 4.3 us)
Async XLA Ops:
  1.4 1.3 copy-start.6
  2.6 8.6 %copy-start.8 = (f32[16,32]{1,0:T(8,128)S(1)}, f32[16,32]{1,0:T(8,128)}, u32[]{:S(2)}) copy-start(f32[16,32]{1,0:T(8,128)} %param.14) | copy-start | bytes 6148
  3.8 1.1 copy-start.3
  4.9 6.5 %copy-start = (f32[2,16,32,548]{3,2,1,0:T(8,128)S(1)}, f32[2,16,32,548]{3,2,1,0:T(8,128)}, u32[]{:S(2)}) copy-start(f32[2,16,32,548]{3,2,1,0:T(8,128)} %base_ref.3) | copy-start | bytes 6733828
  4.9 78.9 %all-to-all-start = ((f32[32,16,640]{2,1,0:T(8,128)}), f32[32,16,640]{2,1,0:T(8,128)}, u32[]{:S(2)}, u32[]{:S(2)}) async-start(f32[32,16,640]{2,1,0:T(8,128)} %bitcast.8), calls=%async_computation | async-start | bytes 2621440 | tf_op jit(solution)/shard_map/all_to_all | solution.py:427
  11.6 31.1 %collective-permute-start.4 = (f32[4,32,548]{2,1,0:T(8,128)S(1)}, f32[4,32,548]{2,1,0:T(8,128)S(1)}, u32[]{:S(2)}, u32[]{:S(2)}) collective-permute-start(f32[4,32,548]{2,1,0:T(8,128)S(1)} %get-tuple-element.36), channel_id=1, source_target_pairs={{0,4},{4,8},{8,12},{12,16},{16,20},{20,24},{24,28},{1,5},{5,9},{9,... | collective-permute-start | bytes 841736 | tf_op jit(solution)/shard_map/ppermute | solution.py:371
  14.7 28.0 %collective-permute-start.5 = (f32[4,32,548]{2,1,0:T(8,128)S(1)}, f32[4,32,548]{2,1,0:T(8,128)S(1)}, u32[]{:S(2)}, u32[]{:S(2)}) collective-permute-start(f32[4,32,548]{2,1,0:T(8,128)S(1)} %get-tuple-element.37), channel_id=1, source_target_pairs={{4,0},{8,4},{12,8},{16,12},{20,16},{24,20},{28,24},{5,1},{9,5},{13... | collective-permute-start | bytes 841736 | tf_op jit(solution)/shard_map/ppermute | solution.py:371
  17.8 32.1 %collective-permute-start = (f32[4,32,549]{2,1,0:T(8,128)S(1)}, f32[4,32,549]{2,1,0:T(8,128)S(1)}, u32[]{:S(2)}, u32[]{:S(2)}) collective-permute-start(f32[4,32,549]{2,1,0:T(8,128)S(1)} %get-tuple-element.30), channel_id=1, source_target_pairs={{0,4},{4,8},{8,12},{12,16},{16,20},{20,24},{24,28},{1,5},{5,9},{9,... | collective-permute-start | bytes 843272 | tf_op jit(solution)/shard_map/ppermute | solution.py:371
  20.0 35.7 %collective-permute-start.1 = (f32[4,32,549]{2,1,0:T(8,128)S(1)}, f32[4,32,549]{2,1,0:T(8,128)S(1)}, u32[]{:S(2)}, u32[]{:S(2)}) collective-permute-start(f32[4,32,549]{2,1,0:T(8,128)S(1)} %get-tuple-element.31), channel_id=1, source_target_pairs={{4,0},{8,4},{12,8},{16,12},{20,16},{24,20},{28,24},{5,1},{9,5},{13... | collective-permute-start | bytes 843272 | tf_op jit(solution)/shard_map/ppermute | solution.py:371
  42.8 34.3 %collective-permute-start.6 = (f32[24,4,548]{2,1,0:T(4,128)S(1)}, f32[24,4,548]{2,1,0:T(4,128)S(1)}, u32[]{:S(2)}, u32[]{:S(2)}) collective-permute-start(f32[24,4,548]{2,1,0:T(4,128)S(1)} %pad_maximum_fusion.2), channel_id=1, source_target_pairs={{0,1},{1,2},{2,3},{4,5},{5,6},{6,7},{8,9},{9,10},{10,11},{12,13},{... | collective-permute-start | bytes 631304 | tf_op jit(solution)/shard_map/ppermute | solution.py:371
  47.6 29.5 %collective-permute-start.7 = (f32[24,4,548]{2,1,0:T(4,128)S(1)}, f32[24,4,548]{2,1,0:T(4,128)S(1)}, u32[]{:S(2)}, u32[]{:S(2)}) collective-permute-start(f32[24,4,548]{2,1,0:T(4,128)S(1)} %pad_maximum_fusion.3), channel_id=1, source_target_pairs={{1,0},{2,1},{3,2},{5,4},{6,5},{7,6},{9,8},{10,9},{11,10},{13,12},{... | collective-permute-start | bytes 631304 | tf_op jit(solution)/shard_map/ppermute | solution.py:371
  55.7 14.4 %collective-permute-start.3 = (f32[24,4,549]{2,1,0:T(4,128)S(1)}, f32[24,4,549]{2,1,0:T(4,128)S(1)}, u32[]{:S(2)}, u32[]{:S(2)}) collective-permute-start(f32[24,4,549]{2,1,0:T(4,128)S(1)} %pad_maximum_fusion.1), channel_id=1, source_target_pairs={{1,0},{2,1},{3,2},{5,4},{6,5},{7,6},{9,8},{10,9},{11,10},{13,12},{... | collective-permute-start | bytes 632456 | tf_op jit(solution)/shard_map/ppermute | solution.py:371
  58.3 11.8 %collective-permute-start.2 = (f32[24,4,549]{2,1,0:T(4,128)S(1)}, f32[24,4,549]{2,1,0:T(4,128)S(1)}, u32[]{:S(2)}, u32[]{:S(2)}) collective-permute-start(f32[24,4,549]{2,1,0:T(4,128)S(1)} %pad_maximum_fusion), channel_id=1, source_target_pairs={{0,1},{1,2},{2,3},{4,5},{5,6},{6,7},{8,9},{9,10},{10,11},{12,13},{... | collective-permute-start | bytes 632456 | tf_op jit(solution)/shard_map/ppermute | solution.py:371
  61.5 8.6 %copy-start.9 = (f32[768]{0:T(1024)S(1)}, f32[768]{0:T(1024)}, u32[]{:S(2)}) copy-start(f32[768]{0:T(1024)} %param.17) | copy-start | bytes 9220
  61.5 8.6 %copy-start.10 = (f32[768]{0:T(1024)S(1)}, f32[768]{0:T(1024)}, u32[]{:S(2)}) copy-start(f32[768]{0:T(1024)} %param.19) | copy-start | bytes 9220
  75.9 1.2 copy-start.4
  77.1 6.6 %copy-start.7 = (s32[32,616]{1,0:T(8,128)S(1)}, s32[32,616]{1,0:T(8,128)}, u32[]{:S(2)}) copy-start(s32[32,616]{1,0:T(8,128)} %mask_ref.1) | copy-start | bytes 236548
  82.6 1.1 copy-start.1
  83.7 7.3 %copy-start.5 = (f32[512,768]{1,0:T(8,128)S(1)}, f32[512,768]{1,0:T(8,128)}, u32[]{:S(2)}) copy-start(f32[512,768]{1,0:T(8,128)} %copy-done.4) | copy-start | bytes 4718596
  91.0 22.2 %copy-start.2 = (f32[512,768]{1,0:T(8,128)S(1)}, f32[512,768]{1,0:T(8,128)}, u32[]{:S(2)}) copy-start(f32[512,768]{1,0:T(8,128)} %copy-done.1) | copy-start | bytes 4718596
  107.0 28.2 %collective-permute-start.12 = (f32[4,32,548]{2,1,0:T(8,128)S(1)}, f32[4,32,548]{2,1,0:T(8,128)S(1)}, u32[]{:S(2)}, u32[]{:S(2)}) collective-permute-start(f32[4,32,548]{2,1,0:T(8,128)S(1)} %get-tuple-element.51), channel_id=1, source_target_pairs={{0,4},{4,8},{8,12},{12,16},{16,20},{20,24},{24,28},{1,5},{5,9},{9,... | collective-permute-start | bytes 841736 | tf_op jit(solution)/shard_map/ppermute | solution.py:371
  110.0 25.2 %collective-permute-start.13 = (f32[4,32,548]{2,1,0:T(8,128)S(1)}, f32[4,32,548]{2,1,0:T(8,128)S(1)}, u32[]{:S(2)}, u32[]{:S(2)}) collective-permute-start(f32[4,32,548]{2,1,0:T(8,128)S(1)} %get-tuple-element.52), channel_id=1, source_target_pairs={{4,0},{8,4},{12,8},{16,12},{20,16},{24,20},{28,24},{5,1},{9,5},{13... | collective-permute-start | bytes 841736 | tf_op jit(solution)/shard_map/ppermute | solution.py:371
  129.0 16.2 %collective-permute-start.8 = (f32[4,32,548]{2,1,0:T(8,128)S(1)}, f32[4,32,548]{2,1,0:T(8,128)S(1)}, u32[]{:S(2)}, u32[]{:S(2)}) collective-permute-start(f32[4,32,548]{2,1,0:T(8,128)S(1)} %get-tuple-element.45), channel_id=1, source_target_pairs={{0,4},{4,8},{8,12},{12,16},{16,20},{20,24},{24,28},{1,5},{5,9},{9,... | collective-permute-start | bytes 841736 | tf_op jit(solution)/shard_map/ppermute | solution.py:371
  131.0 17.5 %collective-permute-start.9 = (f32[4,32,548]{2,1,0:T(8,128)S(1)}, f32[4,32,548]{2,1,0:T(8,128)S(1)}, u32[]{:S(2)}, u32[]{:S(2)}) collective-permute-start(f32[4,32,548]{2,1,0:T(8,128)S(1)} %get-tuple-element.46), channel_id=1, source_target_pairs={{4,0},{8,4},{12,8},{16,12},{20,16},{24,20},{28,24},{5,1},{9,5},{13... | collective-permute-start | bytes 841736 | tf_op jit(solution)/shard_map/ppermute | solution.py:371
  135.3 18.9 %collective-permute-start.15 = (f32[24,4,548]{2,1,0:T(4,128)S(1)}, f32[24,4,548]{2,1,0:T(4,128)S(1)}, u32[]{:S(2)}, u32[]{:S(2)}) collective-permute-start(f32[24,4,548]{2,1,0:T(4,128)S(1)} %pad_maximum_fusion.7), channel_id=1, source_target_pairs={{1,0},{2,1},{3,2},{5,4},{6,5},{7,6},{9,8},{10,9},{11,10},{13,12},{... | collective-permute-start | bytes 631304 | tf_op jit(solution)/shard_map/ppermute | solution.py:371
  137.6 16.6 %collective-permute-start.14 = (f32[24,4,548]{2,1,0:T(4,128)S(1)}, f32[24,4,548]{2,1,0:T(4,128)S(1)}, u32[]{:S(2)}, u32[]{:S(2)}) collective-permute-start(f32[24,4,548]{2,1,0:T(4,128)S(1)} %pad_maximum_fusion.6), channel_id=1, source_target_pairs={{0,1},{1,2},{2,3},{4,5},{5,6},{6,7},{8,9},{9,10},{10,11},{12,13},{... | collective-permute-start | bytes 631304 | tf_op jit(solution)/shard_map/ppermute | solution.py:371
  148.6 10.2 %collective-permute-start.11 = (f32[24,4,548]{2,1,0:T(4,128)S(1)}, f32[24,4,548]{2,1,0:T(4,128)S(1)}, u32[]{:S(2)}, u32[]{:S(2)}) collective-permute-start(f32[24,4,548]{2,1,0:T(4,128)S(1)} %pad_maximum_fusion.5), channel_id=1, source_target_pairs={{1,0},{2,1},{3,2},{5,4},{6,5},{7,6},{9,8},{10,9},{11,10},{13,12},{... | collective-permute-start | bytes 631304 | tf_op jit(solution)/shard_map/ppermute | solution.py:371
  151.0 7.8 %collective-permute-start.10 = (f32[24,4,548]{2,1,0:T(4,128)S(1)}, f32[24,4,548]{2,1,0:T(4,128)S(1)}, u32[]{:S(2)}, u32[]{:S(2)}) collective-permute-start(f32[24,4,548]{2,1,0:T(4,128)S(1)} %pad_maximum_fusion.4), channel_id=1, source_target_pairs={{0,1},{1,2},{2,3},{4,5},{5,6},{6,7},{8,9},{9,10},{10,11},{12,13},{... | collective-permute-start | bytes 631304 | tf_op jit(solution)/shard_map/ppermute | solution.py:371
where the time goes:
time: 164 us; the launch traced here: 163 us
  Pallas kernels  69.1 us (42%)
  starting transfers between devices  54.5 us (33%)
  waiting for transfers between devices  32.4 us (20%)
  local copies, waits for them, and re-layouts  4.93 us (3%)
    ppermute x16, starting transfers between devices, shift(): lax.ppermute(value, axis, [(i, i + by) for i in range(count) if 0 <= i +...  48.2 us
    ppermute x16, waiting for transfers between devices, shift(): lax.ppermute(value, axis, [(i, i + by) for i in range(count) if 0 <= i +...  32.4 us
    pallas_call x2, Pallas kernels, body(): call(net_kernel, [shaped((tile_x, tile_y, levels))] + [shaped((SWEEPS, ti...  31.7 us
    pallas_call x2, Pallas kernels, body(): call(functools.partial(diffuse_kernel, v > 0), [shaped((cells, side))] +...  11.2 us
    pallas_call x2, Pallas kernels, body(): call(finish_kernel, shaped(vectors.shape), flops=40 * tall * around * dee...  9 us
    pallas_call x1, Pallas kernels, body(): call(prep_kernel, [pltpu.HBM((2, full_l, side), BF), pltpu.HBM((4, 2, sid...  8.55 us
    pallas_call x1, Pallas kernels, body(): call(functools.partial(hidden_kernel, mark, bucket), [shaped((3, slots, s...  7.27 us
    all_to_all x1, starting transfers between devices, body(): lax.all_to_all(packed.reshape(devices, bucket, deep), ('gx', 'gy'), split...  6.37 us
  transfers between devices with their start and end apart: 17, of which 5 were waited for; matrix products, arithmetic and copies ran while one was open for 0% of the time, Pallas kernels for 25%

commit v1 on v0

--- a/solution.py
+++ b/solution.py
@@ -120,34 +120,87 @@
         copy.wait()
 
 
-def cut_kernel(vectors_ref, coeff_ref, *outs):
-    pairs, rows, wide, levels = vectors_ref.shape
+def coeff_column(coeff_ref, row):
+    wide = coeff_ref.shape[1]
+    spread = jnp.broadcast_to(coeff_ref[row : row + 1, :], (wide, wide))
+    diagonal = iota((wide, wide), 0) == iota((wide, wide), 1)
+    return jnp.sum(jnp.where(diagonal, spread, 0.0), axis=1, keepdims=True)
+
+
+def cut_kernel(v, side_ref, vectors_ref, coeff_ref, xa, xb, yhead, ytail, *refs):
+    bufs, sems = refs[:4], refs[4]
+    rows, wide, levels = vectors_ref.shape[1:]
     w = SWEEPS
     parts = (
-        (slice(0, w), slice(None)), (slice(rows - w, rows), slice(None)),
-        (slice(None), slice(0, w)), (slice(None), slice(wide - w, wide)),
+        vectors_ref.at[v, pl.ds(0, w)],
+        vectors_ref.at[v, pl.ds(rows - w, w)],
+        vectors_ref.at[v, :, pl.ds(0, 8)],
+        vectors_ref.at[v, :, pl.ds(wide - 8, 8)],
     )
-    for v in range(pairs):
-        for k, part in enumerate(parts):
-            out = outs[4 * v + k]
-            out[:, :, :levels] = vectors_ref[(v,) + part]
-            if v == 0:
-                out[:, :, levels:] = coeff_ref[part][:, :, :1]
-
-
-def fill(ext, tile, xlo, xhi, ylo, yhi):
-    rows, wide, levels = tile.shape
+    copies = [pltpu.make_async_copy(parts[k], bufs[k], sems.at[k]) for k in range(4)]
+    for copy in copies:
+        copy.start()
+    even = side_ref[0] == 0
+    if v == 0:
+        columns = [coeff_column(coeff_ref, row) for row in range(rows)]
+        for row in range(w):
+            head, tail = columns[row], columns[rows - w + row]
+            xa[row, :, levels:] = jnp.where(even, tail, head)
+            xb[row, :, levels:] = jnp.where(even, head, tail)
+        for row in range(rows):
+            yhead[row, :, levels:] = columns[row][:w]
+            ytail[row, :, levels:] = columns[row][wide - w :]
+    for copy in copies:
+        copy.wait()
+    head, tail = bufs[0][...], bufs[1][...]
+    xa[:, :, :levels] = jnp.where(even, tail, head)
+    xb[:, :, :levels] = jnp.where(even, head, tail)
+    yhead[:, :, :levels] = bufs[2][:, :w]
+    ytail[:, :, :levels] = bufs[3][:, 8 - w :]
+
+
+def join_kernel(side_ref, ra, rb, yhead, ytail, ya, yb):
     w = SWEEPS
+    rows = yhead.shape[0]
+    wide = ra.shape[1]
+    even_x, even_y = side_ref[0] == 0, side_ref[1] == 0
+
+    for here, first, second in (
+        (pl.ds(0, w), rb, ra),
+        (pl.ds(w + rows, w), ra, rb),
+    ):
+        head = jnp.where(even_x, first[:, :w], second[:, :w])
+        tail = jnp.where(even_x, first[:, wide - w :], second[:, wide - w :])
+        ya[here] = jnp.where(even_y, tail, head)
+        yb[here] = jnp.where(even_y, head, tail)
+    here = pl.ds(w, rows)
+    ya[here] = jnp.where(even_y, ytail[...], yhead[...])
+    yb[here] = jnp.where(even_y, yhead[...], ytail[...])
+
+
+def fill(ext, side_ref, tile, ra, rb, qa, qb, part):
+    rows, wide = tile.shape[:2]
+    w = SWEEPS
+    even_y = side_ref[1] == 0
+    upper = jnp.where(side_ref[0] == 0, w + rows, 0)
+    tile_part, strip_part = part
+    ext[w : w + rows, :wide, tile_part] = tile
+    ext[pl.ds(upper, w), :wide, tile_part] = strip_part(ra)
+    ext[pl.ds(w + rows - upper, w), :wide, tile_part] = strip_part(rb)
+    qa, qb = strip_part(qa), strip_part(qb)
+    ext[:, wide : wide + w, tile_part] = jnp.where(even_y, qa, qb)
+    ext[:, wide + w :, tile_part] = jnp.where(even_y, qb, qa)
+
+
+def fill_levels(ext, side_ref, tile, *strips):
+    levels = tile.shape[2]
     last = up(levels, LANES) - LANES
     ext[:, :, last:] = jnp.zeros((ext.shape[0], ext.shape[1], ext.shape[2] - last), F32)
-    ext[w : w + rows, :wide, :levels] = tile
-    ext[:w, :wide, :levels] = xlo[:, :, :levels]
-    ext[w + rows :, :wide, :levels] = xhi[:, :, :levels]
-    ext[:, wide : wide + w, :levels] = yhi[:, :, :levels]
-    ext[:, wide + w :, :levels] = ylo[:, :, :levels]
-
-
-def diffuse_kernel(given, tile_ref, coeff_ref, *refs):
+    part = (pl.ds(0, levels), lambda ref: ref[:, :, :levels])
+    fill(ext, side_ref, tile, *strips, part)
+
+
+def diffuse_kernel(given, side_ref, tile_ref, coeff_ref, *refs):
     strips, stack_ref, refs = refs[:4], refs[4], refs[5:]
     ext, work, high_ref, low_ref, both, sem = refs[-6:]
     out_ref = refs[0]
@@ -157,7 +210,7 @@
     rows, wide, levels = tile_ref.shape[1:]
     tall = rows + 2 * w
     around = wide + 2 * w
-    fill(ext, tile_ref[0], *strips)
+    fill_levels(ext, side_ref, tile_ref[0], *strips)
     if given:
         cb_ref = coeff_ref
     else:
@@ -167,12 +220,10 @@
             column = ref[:, :, levels : levels + 1]
             return jnp.broadcast_to(column, column.shape[:2] + (LANES,))
 
-        xlo, xhi, ylo, yhi = strips
-        cb_ref[w : w + rows, :wide, :] = coeff_ref[...]
-        cb_ref[:w, :wide, :] = spread(xlo)
-        cb_ref[w + rows :, :wide, :] = spread(xhi)
-        cb_ref[:, wide : wide + w, :] = spread(yhi)
-        cb_ref[:, wide + w :, :] = spread(ylo)
+        own = jnp.stack(
+            [jnp.broadcast_to(coeff_column(coeff_ref, k), (wide, LANES)) for k in range(rows)]
+        )
+        fill(cb_ref, side_ref, own, *strips, (pl.ds(0, LANES), spread))
 
     def chunk(j, _):
         lanes = pl.ds(pl.multiple_of(j * LANES, LANES), LANES)
@@ -255,8 +306,8 @@
 
 
 def net_kernel(
-    q_ref, one_ref, one_t_ref, scale_ref, stack_ref,
-    out_ref, xhead, xtail, yhead, ytail, x1, top, low, acc_top, acc_low, stack, sems,
+    side_ref, q_ref, one_ref, one_t_ref, scale_ref, stack_ref,
+    out_ref, xa, xb, yhead, ytail, x1, top, low, acc_top, acc_low, stack, sems,
 ):
     fetch = [
         pltpu.make_async_copy(stack_ref.at[k], stack.at[k], sems.at[k]) for k in range(4)
@@ -321,20 +372,20 @@
         got = got.reshape(tall, wide, got.shape[1])[:, :, :levels]
         here = pl.ds(k * tall, tall)
         out_ref[here] = got
-        if k == 0:
-            xhead[...] = got[:SWEEPS]
-        if (k + 1) * tall == rows:
-            xtail[...] = got[tall - SWEEPS :]
         yhead[here] = got[:, :SWEEPS]
         ytail[here] = got[:, wide - SWEEPS :]
-
-
-def finish_kernel(field_ref, base_ref, cb_ref, *refs):
+    even = side_ref[0] == 0
+    head, tail = out_ref[:SWEEPS], out_ref[rows - SWEEPS :]
+    xa[...] = jnp.where(even, tail, head)
+    xb[...] = jnp.where(even, head, tail)
+
+
+def finish_kernel(side_ref, field_ref, base_ref, cb_ref, *refs):
     out_ref, ext, work, total = refs[-4:]
     w = SWEEPS
     rows, wide, levels = field_ref.shape
     tall = rows + 2 * w
-    fill(ext, field_ref[...], *refs[:4])
+    fill_levels(ext, side_ref, field_ref[...], *refs[:4])
     around = wide + 2 * w
 
     def chunk(j, _):
@@ -366,21 +417,27 @@
     out_ref[0] = base_ref[0] + total[:, :, :levels]
 
 
-def shift(value, axis, by):
-    count = lax.axis_size(axis)
-    return lax.ppermute(
-        value, axis, [(i, i + by) for i in range(count) if 0 <= i + by < count]
-    )
-
-
-def halo(xhead, xtail, yhead, ytail):
-    xlo = shift(xtail, "gx", 1)
-    xhi = shift(xhead, "gx", -1)
-    last = jnp.concatenate([xlo[:, -SWEEPS:], ytail, xhi[:, -SWEEPS:]], axis=0)
-    head = jnp.concatenate([xlo[:, :SWEEPS], yhead, xhi[:, :SWEEPS]], axis=0)
-    ylo = shift(last, "gy", 1)
-    yhi = shift(head, "gy", -1)
-    return xlo, xhi, ylo, yhi
+def swap(value, axis, start):
+    pairs = [(i, i + 1) for i in range(start, lax.axis_size(axis) - 1, 2)]
+    return lax.ppermute(value, axis, pairs + [(j, i) for i, j in pairs])
+
+
+def halo(sides, xa, xb, yhead, ytail):
+    ra = swap(xa, "gx", 0)
+    rb = swap(xb, "gx", 1)
+    whole = pl.BlockSpec(memory_space=pltpu.VMEM)
+    tall = yhead.shape[0] + 2 * SWEEPS
+    ya, yb = call(
+        join_kernel,
+        [shaped((tall,) + yhead.shape[1:])] * 2,
+        flops=0,
+        moved=16 * yhead.size,
+        vmem=8,
+        in_specs=[pl.BlockSpec(memory_space=pltpu.SMEM)] + [whole] * 4,
+    )(sides, ra, rb, yhead, ytail)
+    qa = swap(ya, "gy", 0)
+    qb = swap(yb, "gy", 1)
+    return ra, rb, qa, qb
 
 
 def body(
@@ -402,13 +459,26 @@
     full_c = up(error_inverse.shape[0], WIDE)
     mark = up(levels, 16)
 
-    coeff = jnp.broadcast_to(diffusivity[:, :, None], (tile_x, tile_y, LANES))
-    shapes = []
+    sides = jnp.stack([lax.axis_index("gx") % 2, lax.axis_index("gy") % 2]).astype(jnp.int32)
+    whole = pl.BlockSpec(memory_space=pltpu.VMEM)
+    far = pl.BlockSpec(memory_space=pltpu.HBM)
+    scalars = pl.BlockSpec(memory_space=pltpu.SMEM)
+    base = pltpu.with_memory_space_constraint(vectors, pltpu.HBM)
+    strips = []
     for v in range(pairs):
         deep_v = levels + (v == 0)
-        shapes += [shaped((SWEEPS, tile_y, deep_v))] * 2 + [shaped((tile_x, SWEEPS, deep_v))] * 2
-    cuts = call(cut_kernel, shapes, flops=0, moved=8 * vectors.size, vmem=16)(vectors, coeff)
-    strips = [halo(*cuts[4 * v : 4 * v + 4]) for v in range(pairs)]
+        cuts = call(
+            functools.partial(cut_kernel, v),
+            [shaped((SWEEPS, tile_y, deep_v))] * 2 + [shaped((tile_x, SWEEPS, deep_v))] * 2,
+            flops=0,
+            moved=4 * vectors.size,
+            vmem=12,
+            scratch=[pltpu.VMEM((SWEEPS, tile_y, levels), F32)] * 2
+            + [pltpu.VMEM((tile_x, 8, levels), F32)] * 2
+            + [pltpu.SemaphoreType.DMA((4,))],
+            in_specs=[scalars, far, whole],
+        )(sides, base, diffusivity)
+        strips.append(halo(sides, *cuts))
 
     position = jnp.arange(slots, dtype=jnp.int32)
     grid_row = observed_column // grid_wide
@@ -430,7 +500,6 @@
     ).reshape(slots, deep)
 
     side = max(full_l, full_u, full_c)
-    far = pl.BlockSpec(memory_space=pltpu.HBM)
     weights = (vertical_factor, weight_first, weight_second, weight_out.T, error_inverse)
     first, stack = call(
         prep_kernel,
@@ -449,8 +518,6 @@
     )(*[pltpu.with_memory_space_constraint(weight, pltpu.HBM) for weight in weights])
     first, stack = (pltpu.with_memory_space_constraint(x, pltpu.HBM) for x in (first, stack))
 
-    whole = pl.BlockSpec(memory_space=pltpu.VMEM)
-
     def wide_bias(bias):
         return jnp.pad(bias, (0, side - bias.shape[0]))[None, :]
 
@@ -474,9 +541,9 @@
             ],
             grid=(1,),
             vmem=18,
-            in_specs=[block(v)] + [whole] * 5 + [far],
+            in_specs=[scalars, block(v)] + [whole] * 5 + [far],
             out_specs=[whole] * (2 - (v > 0)),
-        )(vectors, spread if v else coeff, *strips[v], stack)
+        )(sides, vectors, spread if v else diffusivity, *strips[v], stack)
         queries.append(got[0])
         if v == 0:
             spread = got[1]
@@ -513,13 +580,13 @@
                     pltpu.SemaphoreType.DMA((4,)),
                 ],
                 vmem=30,
-                in_specs=[whole] * 4 + [far],
-            )(queries[v], one, one_t, scale, stack)
+                in_specs=[scalars] + [whole] * 4 + [far],
+            )(sides, queries[v], one, one_t, scale, stack)
         )
 
     out = None
     for v in range(pairs):
-        around_field = halo(*fields[v][1:])
+        around_field = halo(sides, *fields[v][1:])
         carry = [] if out is None else [out]
         out = call(
             finish_kernel,
@@ -533,11 +600,11 @@
             ],
             grid=(1,),
             vmem=18,
-            in_specs=[whole, block(v)] + [whole] * 5
+            in_specs=[scalars, whole, block(v)] + [whole] * 5
             + [pl.BlockSpec(memory_space=pl.ANY)] * len(carry),
             out_specs=block(v),
-            input_output_aliases={7: 0} if carry else {},
-        )(fields[v][0], vectors, spread, *around_field, *carry)
+            input_output_aliases={8: 0} if carry else {},
+        )(sides, fields[v][0], vectors, spread, *around_field, *carry)
     return out
 
 

time: 164 us -> 162 us (0.988)
  starting transfers between devices: 54.5 us -> 34 us
  Pallas kernels: 69.1 us -> 80.2 us
  waiting for transfers between devices: 32.4 us -> 40 us
    ppermute x16, starting transfers between devices: 48.2 us -> 27.7 us  [swap(): return lax.ppermute(value, axis, pairs + [(j, i) for i, j in pairs])]
    ppermute x16, waiting for transfers between devices: 32.4 us -> 40 us  [swap(): return lax.ppermute(value, axis, pairs + [(j, i) for i, j in pairs])]
    pallas_call x1 -> x6, Pallas kernels: 0.18 us -> 6.38 us  [the longest x2 3.86 us: body(): call(functools.partial(cut_kernel, v), [shaped((SWEEPS, tile_y, deep_v))]...]
    unnamed x22 -> x20, local copies, waits for them, and re-layouts: 4.67 us -> 3.61 us
  transfers between devices with their start and end apart: 17 -> 17, of which waited for: 5 -> 3; matrix products, arithmetic and copies ran while one was open for 0% -> 0% of each run, Pallas kernels for 25% -> 31%
where the time goes in v1:
time: 162 us; the launch traced here: 160 us
  Pallas kernels  80.2 us (50%)
  waiting for transfers between devices  40 us (25%)
  starting transfers between devices  34 us (21%)
  local copies, waits for them, and re-layouts  3.62 us (2%)
    ppermute x16, waiting for transfers between devices, swap(): return lax.ppermute(value, axis, pairs + [(j, i) for i, j in pairs])  40 us
    pallas_call x2, Pallas kernels, body(): call(net_kernel, [shaped((tile_x, tile_y, levels))] + [shaped((SWEEPS, ti...  33 us
    ppermute x16, starting transfers between devices, swap(): return lax.ppermute(value, axis, pairs + [(j, i) for i, j in pairs])  27.7 us
    pallas_call x2, Pallas kernels, body(): call(functools.partial(diffuse_kernel, v > 0), [shaped((cells, side))] +...  12.4 us
    pallas_call x2, Pallas kernels, body(): call(finish_kernel, shaped(vectors.shape), flops=40 * tall * around * dee...  10.1 us
    pallas_call x1, Pallas kernels, body(): call(prep_kernel, [pltpu.HBM((2, full_l, side), BF), pltpu.HBM((4, 2, sid...  8.72 us
    pallas_call x1, Pallas kernels, body(): call(functools.partial(hidden_kernel, mark, bucket), [shaped((3, slots, s...  7.27 us
    all_to_all x1, starting transfers between devices, body(): lax.all_to_all(packed.reshape(devices, bucket, deep), ('gx', 'gy'), split...  6.37 us
  transfers between devices with their start and end apart: 17, of which 3 were waited for; matrix products, arithmetic and copies ran while one was open for 0% of the time, Pallas kernels for 31%

profile of v1, /device:TPU:9, one launch (start us, length us, event | category | flops | bytes accessed | tf_op | source)
XLA Modules:
  0.0 159.7 jit_solution(3107731233762820978)
XLA Ops:
  0.7 0.7 fusion.6
  1.4 1.2 copy-done.6
  2.6 2.3 %shard_map.134 = f32[512,640]{1,0:T(8,128)} custom-call(s32[1,512]{1,0:T(1,128)S(1)} %bitcast.11, f32[1,512]{1,0:T(1,128)S(1)} %bitcast.10, f32[548,512]{1,0:T(8,128)S(1)} %bitcast.12), custom_call_target="tpu_custom_call" | custom-call | flops 1006632960 | bytes 2621440 | tf_op jit(solution)/shard_map/pallas_call | solution.py:489
  4.9 6.4 %all-to-all-start = ((f32[32,16,640]{2,1,0:T(8,128)}), f32[32,16,640]{2,1,0:T(8,128)}, u32[]{:S(2)}, u32[]{:S(2)}) async-start(f32[32,16,640]{2,1,0:T(8,128)} %bitcast.7), calls=%async_computation | async-start | bytes 2621440 | tf_op jit(solution)/shard_map/all_to_all | solution.py:497
  11.4 1.9 %shard_map.127 = (f32[4,32,549]{2,1,0:T(8,128)S(1)}, f32[4,32,549]{2,1,0:T(8,128)S(1)}, f32[16,4,549]{2,1,0:T(4,128)S(1)}, f32[16,4,549]{2,1,0:T(4,128)S(1)}) custom-call(s32[2]{0:T(128)S(1)} %pad_add_fusion.side_ref, f32[2,16,32,548]{3,2,1,0:T(8,128)} %base_ref.3, f32[16,32]{1,0:T(8,128)S(1)} %copy-done.3), custom_call_target="tpu_custom_call" | custom-call | bytes 2244608 | tf_op jit(solution)/shard_map/pallas_call | solution.py:470
  13.3 1.2 collective-permute-start
  14.5 2.0 %collective-permute-start.1 = (f32[4,32,549]{2,1,0:T(8,128)S(1)}, f32[4,32,549]{2,1,0:T(8,128)S(1)}, u32[]{:S(2)}, u32[]{:S(2)}) collective-permute-start(f32[4,32,549]{2,1,0:T(8,128)S(1)} %get-tuple-element.39), channel_id=1, source_target_pairs={{4,8},{12,16},{20,24},{8,4},{16,12},{24,20},{5,9},{13,17},{21,25},... | collective-permute-start | bytes 843272 | tf_op jit(solution)/shard_map/ppermute | solution.py:422
  16.6 1.9 %shard_map.131 = (f32[4,32,548]{2,1,0:T(8,128)S(1)}, f32[4,32,548]{2,1,0:T(8,128)S(1)}, f32[16,4,548]{2,1,0:T(4,128)S(1)}, f32[16,4,548]{2,1,0:T(4,128)S(1)}) custom-call(s32[2]{0:T(128)S(1)} %pad_add_fusion.side_ref, f32[2,16,32,548]{3,2,1,0:T(8,128)} %base_ref.3, f32[16,32]{1,0:T(8,128)S(1)} %copy-done.3), custom_call_target="tpu_custom_call" | custom-call | bytes 2244608 | tf_op jit(solution)/shard_map/pallas_call | solution.py:470
  18.5 2.3 %collective-permute-start.4 = (f32[4,32,548]{2,1,0:T(8,128)S(1)}, f32[4,32,548]{2,1,0:T(8,128)S(1)}, u32[]{:S(2)}, u32[]{:S(2)}) collective-permute-start(f32[4,32,548]{2,1,0:T(8,128)S(1)} %get-tuple-element.46), channel_id=1, source_target_pairs={{0,4},{8,12},{16,20},{24,28},{4,0},{12,8},{20,16},{28,24},{1,5},{9... | collective-permute-start | bytes 841736 | tf_op jit(solution)/shard_map/ppermute | solution.py:422
  20.8 1.9 %collective-permute-start.5 = (f32[4,32,548]{2,1,0:T(8,128)S(1)}, f32[4,32,548]{2,1,0:T(8,128)S(1)}, u32[]{:S(2)}, u32[]{:S(2)}) collective-permute-start(f32[4,32,548]{2,1,0:T(8,128)S(1)} %get-tuple-element.47), channel_id=1, source_target_pairs={{4,8},{12,16},{20,24},{8,4},{16,12},{24,20},{5,9},{13,17},{21,25},... | collective-permute-start | bytes 841736 | tf_op jit(solution)/shard_map/ppermute | solution.py:422
  22.7 32.5 %collective-permute-done.4.ra.refs_0_ = f32[4,32,548]{2,1,0:T(8,128)S(1)} collective-permute-done((f32[4,32,548]{2,1,0:T(8,128)S(1)}, f32[4,32,548]{2,1,0:T(8,128)S(1)}, u32[]{:S(2)}, u32[]{:S(2)}) %collective-permute-start.4) | collective-permute-done | bytes 280608 | tf_op jit(solution)/shard_map/ppermute | solution.py:422
  55.9 1.0 collective-permute-start.6
  57.0 3.0 %collective-permute-start.7 = (f32[24,4,548]{2,1,0:T(4,128)S(1)}, f32[24,4,548]{2,1,0:T(4,128)S(1)}, u32[]{:S(2)}, u32[]{:S(2)}) collective-permute-start(f32[24,4,548]{2,1,0:T(4,128)S(1)} %get-tuple-element.51), channel_id=1, source_target_pairs={{1,2},{2,1},{5,6},{6,5},{9,10},{10,9},{13,14},{14,13},{17,18},{18,... | collective-permute-start | bytes 631304 | tf_op jit(solution)/shard_map/ppermute | solution.py:422
  60.7 2.6 %collective-permute-start.3 = (f32[24,4,549]{2,1,0:T(4,128)S(1)}, f32[24,4,549]{2,1,0:T(4,128)S(1)}, u32[]{:S(2)}, u32[]{:S(2)}) collective-permute-start(f32[24,4,549]{2,1,0:T(4,128)S(1)} %get-tuple-element.43), channel_id=1, source_target_pairs={{1,2},{2,1},{5,6},{6,5},{9,10},{10,9},{13,14},{14,13},{17,18},{18,... | collective-permute-start | bytes 632456 | tf_op jit(solution)/shard_map/ppermute | solution.py:422
  63.3 8.7 %shard_map.129 = (bf16[2,768,768]{2,1,0:T(8,128)(2,1)}, bf16[4,2,768,768]{3,2,1,0:T(8,128)(2,1)}) custom-call(f32[548,548]{1,0:T(8,128)} %refs_0_.1, f32[548,768]{1,0:T(8,128)} %refs_1_.1, f32[768,768]{1,0:T(8,128)} %refs_2_.1, f32[616,768]{1,0:T(8,128)} %bitcast.13, f32[616,616]{1,0:T(8,128)} %refs_4_.1), custom_call_target="tpu_custom_call" | custom-call | flops 2717908992 | bytes 23592960 | tf_op jit(solution)/shard_map/pallas_call | solution.py:504
  72.1 6.4 %shard_map.130 = (f32[512,768]{1,0:T(8,128)S(1)}, f32[24,40,128]{2,1,0:T(8,128)S(1)}) custom-call(s32[2]{0:T(128)S(1)} %pad_add_fusion.side_ref, f32[2,16,32,548]{3,2,1,0:T(8,128)S(1)} %copy-done, f32[16,32]{1,0:T(8,128)S(1)} %copy-done.3, f32[4,32,549]{2,1,0:T(8,128)S(1)} %collective-permute-done.ra.refs_0_, ...), custom_call_target="tpu_custom_call" | custom-call | flops 1509949440 | bytes 4915200 | tf_op jit(solution)/shard_map/pallas_call | solution.py:529
  78.5 1.2 copy-done.4
  79.7 6.0 %shard_map.133.q_ref = f32[512,768]{1,0:T(8,128)S(1)} custom-call(s32[2]{0:T(128)S(1)} %pad_add_fusion.side_ref, f32[2,16,32,548]{3,2,1,0:T(8,128)S(1)} %copy-done, f32[24,40,128]{2,1,0:T(8,128)S(1)} %get-tuple-element.45.coeff_ref.cb_ref, f32[4,32,548]{2,1,0:T(8,128)S(1)} %collective-permute-done.4.ra.refs_0_, ...), custom_call_target="tpu_custom_call" | custom-call | flops 1509949440 | bytes 4915200 | tf_op jit(solution)/shard_map/pallas_call | solution.py:529
  85.8 1.1 copy-done.1
  86.9 7.3 %shard_map.135 = (f32[3,512,768]{2,1,0:T(8,128)S(1)}, bf16[512,512]{1,0:T(8,128)(2,1)S(1)}, bf16[512,512]{1,0:T(8,128)(2,1)S(1)}) custom-call(f32[512,640]{1,0:T(8,128)} %bitcast.8.x_ref, bf16[2,768,768]{2,1,0:T(8,128)(2,1)} %get-tuple-element.52.first_ref, f32[1,768]{1,0:T(1,128)S(1)} %broadcast_in_dim.16.b1_ref, ...), custom_call_target="tpu_custom_call" | custom-call | flops 3623878656 | bytes 3145728 | tf_op jit(solution)/shard_map/pallas_call | solution.py:551
  94.2 16.5 %shard_map.138 = (f32[16,32,548]{2,1,0:T(8,128)S(1)}, f32[4,32,548]{2,1,0:T(8,128)S(1)}, f32[4,32,548]{2,1,0:T(8,128)S(1)}, f32[16,4,548]{2,1,0:T(4,128)S(1)}, f32[16,4,548]{2,1,0:T(4,128)S(1)}) custom-call(s32[2]{0:T(128)S(1)} %pad_add_fusion.side_ref, f32[512,768]{1,0:T(8,128)S(1)} %copy-done.5, bf16[512,512]{1,0:T(8,128)(2,1)S(1)} %get-tuple-element.53.one_ref, ...), custom_call_target="tpu_custom_call" | custom-call | flops 10871635968 | bytes 11796480 | tf_op jit(solution)/shard_map/pallas_call | solution.py:568
  110.7 1.3 collective-permute-start.12
  112.0 1.9 %collective-permute-start.13 = (f32[4,32,548]{2,1,0:T(8,128)S(1)}, f32[4,32,548]{2,1,0:T(8,128)S(1)}, u32[]{:S(2)}, u32[]{:S(2)}) collective-permute-start(f32[4,32,548]{2,1,0:T(8,128)S(1)} %get-tuple-element.66), channel_id=1, source_target_pairs={{4,8},{12,16},{20,24},{8,4},{16,12},{24,20},{5,9},{13,17},{21,25},... | collective-permute-start | bytes 841736 | tf_op jit(solution)/shard_map/ppermute | solution.py:422
  113.9 16.5 %shard_map.136 = (f32[16,32,548]{2,1,0:T(8,128)S(1)}, f32[4,32,548]{2,1,0:T(8,128)S(1)}, f32[4,32,548]{2,1,0:T(8,128)S(1)}, f32[16,4,548]{2,1,0:T(4,128)S(1)}, f32[16,4,548]{2,1,0:T(4,128)S(1)}) custom-call(s32[2]{0:T(128)S(1)} %pad_add_fusion.side_ref, f32[512,768]{1,0:T(8,128)S(1)} %copy-done.2, bf16[512,512]{1,0:T(8,128)(2,1)S(1)} %get-tuple-element.53.one_ref, ...), custom_call_target="tpu_custom_call" | custom-call | flops 10871635968 | bytes 11796480 | tf_op jit(solution)/shard_map/pallas_call | solution.py:568
  130.4 1.6 collective-permute-start.8
  132.0 2.8 %collective-permute-start.9 = (f32[4,32,548]{2,1,0:T(8,128)S(1)}, f32[4,32,548]{2,1,0:T(8,128)S(1)}, u32[]{:S(2)}, u32[]{:S(2)}) collective-permute-start(f32[4,32,548]{2,1,0:T(8,128)S(1)} %get-tuple-element.58), channel_id=1, source_target_pairs={{4,8},{12,16},{20,24},{8,4},{16,12},{24,20},{5,9},{13,17},{21,25},... | collective-permute-start | bytes 841736 | tf_op jit(solution)/shard_map/ppermute | solution.py:422
  134.8 0.6 shard_map.139
  135.5 3.9 %collective-permute-start.15 = (f32[24,4,548]{2,1,0:T(4,128)S(1)}, f32[24,4,548]{2,1,0:T(4,128)S(1)}, u32[]{:S(2)}, u32[]{:S(2)}) collective-permute-start(f32[24,4,548]{2,1,0:T(4,128)S(1)} %get-tuple-element.70), channel_id=1, source_target_pairs={{1,2},{2,1},{5,6},{6,5},{9,10},{10,9},{13,14},{14,13},{17,18},{18,... | collective-permute-start | bytes 631304 | tf_op jit(solution)/shard_map/ppermute | solution.py:422
  139.4 6.9 %collective-permute-done.8.ra.refs_0_ = f32[4,32,548]{2,1,0:T(8,128)S(1)} collective-permute-done((f32[4,32,548]{2,1,0:T(8,128)S(1)}, f32[4,32,548]{2,1,0:T(8,128)S(1)}, u32[]{:S(2)}, u32[]{:S(2)}) %collective-permute-start.8) | collective-permute-done | bytes 280608 | tf_op jit(solution)/shard_map/ppermute | solution.py:422
  147.1 1.9 %collective-permute-start.11 = (f32[24,4,548]{2,1,0:T(4,128)S(1)}, f32[24,4,548]{2,1,0:T(4,128)S(1)}, u32[]{:S(2)}, u32[]{:S(2)}) collective-permute-start(f32[24,4,548]{2,1,0:T(4,128)S(1)} %get-tuple-element.62), channel_id=1, source_target_pairs={{1,2},{2,1},{5,6},{6,5},{9,10},{10,9},{13,14},{14,13},{17,18},{18,... | collective-permute-start | bytes 631304 | tf_op jit(solution)/shard_map/ppermute | solution.py:422
  149.1 5.1 %shard_map.140.refs_4_ = f32[2,16,32,548]{3,2,1,0:T(8,128)} custom-call(s32[2]{0:T(128)S(1)} %pad_add_fusion.side_ref, f32[16,32,548]{2,1,0:T(8,128)S(1)} %get-tuple-element.64.field_ref, f32[2,16,32,548]{3,2,1,0:T(8,128)S(1)} %copy-done, f32[24,40,128]{2,1,0:T(8,128)S(1)} %get-tuple-element.45.coeff_ref.cb_ref, ...), custom_call_target="tpu_custom_call" | custom-call | flops 24576000 | bytes 3932160 | tf_op jit(solution)/shard_map/pallas_call | solution.py:591
  154.6 5.0 %shard_map.141 = f32[2,16,32,548]{3,2,1,0:T(8,128)} custom-call(s32[2]{0:T(128)S(1)} %pad_add_fusion.side_ref, f32[16,32,548]{2,1,0:T(8,128)S(1)} %get-tuple-element.56.field_ref, f32[2,16,32,548]{3,2,1,0:T(8,128)S(1)} %copy-done, f32[24,40,128]{2,1,0:T(8,128)S(1)} %get-tuple-element.45.coeff_ref.cb_ref, ...), custom_call_target="tpu_custom_call", output_to_operand_aliasing={{}: (8, {})} | custom-call | flops 24576000 | bytes 3932160 | tf_op jit(solution)/shard_map/pallas_call | solution.py:591
  (41 shorter events, 2.8 us)
Async XLA Ops:
  1.4 1.3 copy-start.6
  4.9 6.5 %copy-start.3 = (f32[16,32]{1,0:T(8,128)S(1)}, f32[16,32]{1,0:T(8,128)}, u32[]{:S(2)}) copy-start(f32[16,32]{1,0:T(8,128)} %coeff_ref.5) | copy-start | bytes 6148
  4.9 82.0 %all-to-all-start = ((f32[32,16,640]{2,1,0:T(8,128)}), f32[32,16,640]{2,1,0:T(8,128)}, u32[]{:S(2)}, u32[]{:S(2)}) async-start(f32[32,16,640]{2,1,0:T(8,128)} %bitcast.7), calls=%async_computation | async-start | bytes 2621440 | tf_op jit(solution)/shard_map/all_to_all | solution.py:497
  13.3 46.7 %collective-permute-start = (f32[4,32,549]{2,1,0:T(8,128)S(1)}, f32[4,32,549]{2,1,0:T(8,128)S(1)}, u32[]{:S(2)}, u32[]{:S(2)}) collective-permute-start(f32[4,32,549]{2,1,0:T(8,128)S(1)} %get-tuple-element.38), channel_id=1, source_target_pairs={{0,4},{8,12},{16,20},{24,28},{4,0},{12,8},{20,16},{28,24},{1,5},{9... | collective-permute-start | bytes 843272 | tf_op jit(solution)/shard_map/ppermute | solution.py:422
  14.5 45.4 %collective-permute-start.1 = (f32[4,32,549]{2,1,0:T(8,128)S(1)}, f32[4,32,549]{2,1,0:T(8,128)S(1)}, u32[]{:S(2)}, u32[]{:S(2)}) collective-permute-start(f32[4,32,549]{2,1,0:T(8,128)S(1)} %get-tuple-element.39), channel_id=1, source_target_pairs={{4,8},{12,16},{20,24},{8,4},{16,12},{24,20},{5,9},{13,17},{21,25},... | collective-permute-start | bytes 843272 | tf_op jit(solution)/shard_map/ppermute | solution.py:422
  18.5 36.8 %collective-permute-start.4 = (f32[4,32,548]{2,1,0:T(8,128)S(1)}, f32[4,32,548]{2,1,0:T(8,128)S(1)}, u32[]{:S(2)}, u32[]{:S(2)}) collective-permute-start(f32[4,32,548]{2,1,0:T(8,128)S(1)} %get-tuple-element.46), channel_id=1, source_target_pairs={{0,4},{8,12},{16,20},{24,28},{4,0},{12,8},{20,16},{28,24},{1,5},{9... | collective-permute-start | bytes 841736 | tf_op jit(solution)/shard_map/ppermute | solution.py:422
  20.8 34.5 %collective-permute-start.5 = (f32[4,32,548]{2,1,0:T(8,128)S(1)}, f32[4,32,548]{2,1,0:T(8,128)S(1)}, u32[]{:S(2)}, u32[]{:S(2)}) collective-permute-start(f32[4,32,548]{2,1,0:T(8,128)S(1)} %get-tuple-element.47), channel_id=1, source_target_pairs={{4,8},{12,16},{20,24},{8,4},{16,12},{24,20},{5,9},{13,17},{21,25},... | collective-permute-start | bytes 841736 | tf_op jit(solution)/shard_map/ppermute | solution.py:422
  55.9 23.8 %collective-permute-start.6 = (f32[24,4,548]{2,1,0:T(4,128)S(1)}, f32[24,4,548]{2,1,0:T(4,128)S(1)}, u32[]{:S(2)}, u32[]{:S(2)}) collective-permute-start(f32[24,4,548]{2,1,0:T(4,128)S(1)} %get-tuple-element.50), channel_id=1, source_target_pairs={{0,1},{2,3},{1,0},{3,2},{4,5},{6,7},{5,4},{7,6},{8,9},{10,11},{9,8... | collective-permute-start | bytes 631304 | tf_op jit(solution)/shard_map/ppermute | solution.py:422
  57.0 22.8 %collective-permute-start.7 = (f32[24,4,548]{2,1,0:T(4,128)S(1)}, f32[24,4,548]{2,1,0:T(4,128)S(1)}, u32[]{:S(2)}, u32[]{:S(2)}) collective-permute-start(f32[24,4,548]{2,1,0:T(4,128)S(1)} %get-tuple-element.51), channel_id=1, source_target_pairs={{1,2},{2,1},{5,6},{6,5},{9,10},{10,9},{13,14},{14,13},{17,18},{18,... | collective-permute-start | bytes 631304 | tf_op jit(solution)/shard_map/ppermute | solution.py:422
  60.6 11.4 %collective-permute-start.2 = (f32[24,4,549]{2,1,0:T(4,128)S(1)}, f32[24,4,549]{2,1,0:T(4,128)S(1)}, u32[]{:S(2)}, u32[]{:S(2)}) collective-permute-start(f32[24,4,549]{2,1,0:T(4,128)S(1)} %get-tuple-element.42), channel_id=1, source_target_pairs={{0,1},{2,3},{1,0},{3,2},{4,5},{6,7},{5,4},{7,6},{8,9},{10,11},{9,8... | collective-permute-start | bytes 632456 | tf_op jit(solution)/shard_map/ppermute | solution.py:422
  60.7 11.4 %collective-permute-start.3 = (f32[24,4,549]{2,1,0:T(4,128)S(1)}, f32[24,4,549]{2,1,0:T(4,128)S(1)}, u32[]{:S(2)}, u32[]{:S(2)}) collective-permute-start(f32[24,4,549]{2,1,0:T(4,128)S(1)} %get-tuple-element.43), channel_id=1, source_target_pairs={{1,2},{2,1},{5,6},{6,5},{9,10},{10,9},{13,14},{14,13},{17,18},{18,... | collective-permute-start | bytes 632456 | tf_op jit(solution)/shard_map/ppermute | solution.py:422
  63.3 8.8 %copy-start.8 = (f32[768]{0:T(1024)S(1)}, f32[768]{0:T(1024)}, u32[]{:S(2)}) copy-start(f32[768]{0:T(1024)} %param.17) | copy-start | bytes 9220
  63.3 8.8 %copy-start.9 = (f32[768]{0:T(1024)S(1)}, f32[768]{0:T(1024)}, u32[]{:S(2)}) copy-start(f32[768]{0:T(1024)} %param.19) | copy-start | bytes 9220
  63.3 8.8 %copy-start = (f32[2,16,32,548]{3,2,1,0:T(8,128)S(1)}, f32[2,16,32,548]{3,2,1,0:T(8,128)}, u32[]{:S(2)}) copy-start(f32[2,16,32,548]{3,2,1,0:T(8,128)} %base_ref.3) | copy-start | bytes 6733828
  78.5 1.2 copy-start.4
  79.7 7.2 %copy-start.7 = (s32[32,616]{1,0:T(8,128)S(1)}, s32[32,616]{1,0:T(8,128)}, u32[]{:S(2)}) copy-start(s32[32,616]{1,0:T(8,128)} %mask_ref.1) | copy-start | bytes 236548
  85.8 1.1 copy-start.1
  86.9 7.3 %copy-start.5 = (f32[512,768]{1,0:T(8,128)S(1)}, f32[512,768]{1,0:T(8,128)}, u32[]{:S(2)}) copy-start(f32[512,768]{1,0:T(8,128)} %copy-done.4) | copy-start | bytes 4718596
  94.2 19.7 %copy-start.2 = (f32[512,768]{1,0:T(8,128)S(1)}, f32[512,768]{1,0:T(8,128)}, u32[]{:S(2)}) copy-start(f32[512,768]{1,0:T(8,128)} %copy-done.1) | copy-start | bytes 4718596
  110.7 24.0 %collective-permute-start.12 = (f32[4,32,548]{2,1,0:T(8,128)S(1)}, f32[4,32,548]{2,1,0:T(8,128)S(1)}, u32[]{:S(2)}, u32[]{:S(2)}) collective-permute-start(f32[4,32,548]{2,1,0:T(8,128)S(1)} %get-tuple-element.65), channel_id=1, source_target_pairs={{0,4},{8,12},{16,20},{24,28},{4,0},{12,8},{20,16},{28,24},{1,5},{9... | collective-permute-start | bytes 841736 | tf_op jit(solution)/shard_map/ppermute | solution.py:422
  112.0 22.8 %collective-permute-start.13 = (f32[4,32,548]{2,1,0:T(8,128)S(1)}, f32[4,32,548]{2,1,0:T(8,128)S(1)}, u32[]{:S(2)}, u32[]{:S(2)}) collective-permute-start(f32[4,32,548]{2,1,0:T(8,128)S(1)} %get-tuple-element.66), channel_id=1, source_target_pairs={{4,8},{12,16},{20,24},{8,4},{16,12},{24,20},{5,9},{13,17},{21,25},... | collective-permute-start | bytes 841736 | tf_op jit(solution)/shard_map/ppermute | solution.py:422
  130.4 15.9 %collective-permute-start.8 = (f32[4,32,548]{2,1,0:T(8,128)S(1)}, f32[4,32,548]{2,1,0:T(8,128)S(1)}, u32[]{:S(2)}, u32[]{:S(2)}) collective-permute-start(f32[4,32,548]{2,1,0:T(8,128)S(1)} %get-tuple-element.57), channel_id=1, source_target_pairs={{0,4},{8,12},{16,20},{24,28},{4,0},{12,8},{20,16},{28,24},{1,5},{9... | collective-permute-start | bytes 841736 | tf_op jit(solution)/shard_map/ppermute | solution.py:422
  132.0 14.4 %collective-permute-start.9 = (f32[4,32,548]{2,1,0:T(8,128)S(1)}, f32[4,32,548]{2,1,0:T(8,128)S(1)}, u32[]{:S(2)}, u32[]{:S(2)}) collective-permute-start(f32[4,32,548]{2,1,0:T(8,128)S(1)} %get-tuple-element.58), channel_id=1, source_target_pairs={{4,8},{12,16},{20,24},{8,4},{16,12},{24,20},{5,9},{13,17},{21,25},... | collective-permute-start | bytes 841736 | tf_op jit(solution)/shard_map/ppermute | solution.py:422
  135.4 13.6 %collective-permute-start.14 = (f32[24,4,548]{2,1,0:T(4,128)S(1)}, f32[24,4,548]{2,1,0:T(4,128)S(1)}, u32[]{:S(2)}, u32[]{:S(2)}) collective-permute-start(f32[24,4,548]{2,1,0:T(4,128)S(1)} %get-tuple-element.69), channel_id=1, source_target_pairs={{0,1},{2,3},{1,0},{3,2},{4,5},{6,7},{5,4},{7,6},{8,9},{10,11},{9,8... | collective-permute-start | bytes 631304 | tf_op jit(solution)/shard_map/ppermute | solution.py:422
  135.5 13.5 %collective-permute-start.15 = (f32[24,4,548]{2,1,0:T(4,128)S(1)}, f32[24,4,548]{2,1,0:T(4,128)S(1)}, u32[]{:S(2)}, u32[]{:S(2)}) collective-permute-start(f32[24,4,548]{2,1,0:T(4,128)S(1)} %get-tuple-element.70), channel_id=1, source_target_pairs={{1,2},{2,1},{5,6},{6,5},{9,10},{10,9},{13,14},{14,13},{17,18},{18,... | collective-permute-start | bytes 631304 | tf_op jit(solution)/shard_map/ppermute | solution.py:422
  147.0 7.1 %collective-permute-start.10 = (f32[24,4,548]{2,1,0:T(4,128)S(1)}, f32[24,4,548]{2,1,0:T(4,128)S(1)}, u32[]{:S(2)}, u32[]{:S(2)}) collective-permute-start(f32[24,4,548]{2,1,0:T(4,128)S(1)} %get-tuple-element.61), channel_id=1, source_target_pairs={{0,1},{2,3},{1,0},{3,2},{4,5},{6,7},{5,4},{7,6},{8,9},{10,11},{9,8... | collective-permute-start | bytes 631304 | tf_op jit(solution)/shard_map/ppermute | solution.py:422
  147.1 7.5 %collective-permute-start.11 = (f32[24,4,548]{2,1,0:T(4,128)S(1)}, f32[24,4,548]{2,1,0:T(4,128)S(1)}, u32[]{:S(2)}, u32[]{:S(2)}) collective-permute-start(f32[24,4,548]{2,1,0:T(4,128)S(1)} %get-tuple-element.62), channel_id=1, source_target_pairs={{1,2},{2,1},{5,6},{6,5},{9,10},{10,9},{13,14},{14,13},{17,18},{18,... | collective-permute-start | bytes 631304 | tf_op jit(solution)/shard_map/ppermute | solution.py:422

commit v2 on v1

--- a/solution.py
+++ b/solution.py
@@ -107,14 +107,18 @@
     fetch[1].wait()
     put(raw[1][...], first)
     send(first, first_out)
-    deep = turned.shape[2]
-    for part in halves(turned.shape[1]):
-        got = mm3(turned[0, part, :], turned[1, part, :], first[0, :deep], first[1, :deep])
-        stack[3, 0, part, :], stack[3, 1, part, :] = split(got)
-    send(stack.at[3], stack_out.at[3])
+    for copy in fetch[2:]:
+        copy.wait()
+    rows = up(raw[0].shape[1], LANES)
+    stack[3, :, rows:, :] = jnp.zeros((2,) + (stack.shape[2] - rows, stack.shape[3]), BF)
+    parts = halves(rows)
     for k in range(3):
-        fetch[k + 2].wait()
+        if k < len(parts):
+            part = parts[k]
+            got = mm3(turned[0, part, :], turned[1, part, :], first[0], first[1])
+            stack[3, 0, part, :], stack[3, 1, part, :] = split(got)
         put(raw[k + 2][...], stack.at[k])
+    for k in range(4):
         send(stack.at[k], stack_out.at[k])
     for copy in sends:
         copy.wait()
@@ -223,7 +227,8 @@
         own = jnp.stack(
             [jnp.broadcast_to(coeff_column(coeff_ref, k), (wide, LANES)) for k in range(rows)]
         )
-        fill(cb_ref, side_ref, own, *strips, (pl.ds(0, LANES), spread))
+        fill(cb_ref.at[0], side_ref, own, *strips, (pl.ds(0, LANES), spread))
+        cb_ref[1] = 1.0 - 4.0 * cb_ref[0]
 
     def chunk(j, _):
         lanes = pl.ds(pl.multiple_of(j * LANES, LANES), LANES)
@@ -234,7 +239,7 @@
                 else:
                     above, mid, below = (work[(sweep + 1) % 2, k] for k in (i - 1, i, i + 1))
                 beside = above + below + pltpu.roll(mid, 1, 0) + pltpu.roll(mid, around - 1, 0)
-                new = mid + cb_ref[i] * (beside - 4.0 * mid)
+                new = cb_ref[1, i] * mid + cb_ref[0, i] * beside
                 if sweep == SWEEPS - 1:
                     high, low = split(new[:wide])
                     here = pl.ds((i - w) * wide, wide)
@@ -255,8 +260,10 @@
 
 def hidden_kernel(
     mark, bucket, x_ref, first_ref, b1_ref, stack_ref, b2_ref, mask_ref,
-    scale_ref, one_ref, one_t_ref, high_ref, low_ref, first, second, sems,
+    scale_ref, one_ref, one_t_ref, high_ref, low_ref, x_buf, first, second, sems,
 ):
+    fetch_x = pltpu.make_async_copy(x_ref, x_buf, sems.at[2])
+    fetch_x.start()
     fetch_first = pltpu.make_async_copy(first_ref, first, sems.at[0])
     fetch_second = pltpu.make_async_copy(stack_ref.at[0], second, sems.at[1])
     fetch_first.start()
@@ -265,6 +272,8 @@
     slots, deep = x_ref.shape
     cells = one_ref.shape[1]
     devices, channels = mask_ref.shape
+    fetch_x.wait()
+    x_ref = x_buf
     index = x_ref[:, mark : mark + 1]
     cell = index.astype(jnp.int32) - 1
     live = index > 0.5
@@ -394,7 +403,7 @@
 
             def read(k):
                 value = ext[k, :, lanes] if sweep == 0 else work[(sweep + 1) % 2, k]
-                return value, cb_ref[k] * value
+                return value, cb_ref[0, k] * value
 
             above = read(sweep)
             mid = read(sweep + 1)
@@ -405,7 +414,7 @@
                     above[1] + below[1]
                     + pltpu.roll(scaled, 1, 0) + pltpu.roll(scaled, around - 1, 0)
                 )
-                new = mid[0] + (beside - 4.0 * scaled)
+                new = cb_ref[1, i] * mid[0] + beside
                 if sweep == SWEEPS - 1:
                     total[i - w, :, lanes] = new[:wide]
                 else:
@@ -528,7 +537,7 @@
     for v in range(pairs):
         got = call(
             functools.partial(diffuse_kernel, v > 0),
-            [shaped((cells, side))] + [shaped((tall, around, LANES))] * (v == 0),
+            [shaped((cells, side))] + [shaped((2, tall, around, LANES))] * (v == 0),
             flops=6 * cells * deep * full_u,
             moved=8 * tall * around * deep,
             scratch=[
@@ -555,12 +564,13 @@
         moved=8 * slots * full_u,
         scratch=[pltpu.VMEM((slots, side), BF)] * 2
         + [
+            pltpu.VMEM((slots, deep), F32),
             pltpu.VMEM((2, full_l, side), BF), pltpu.VMEM((2, side, side), BF),
-            pltpu.SemaphoreType.DMA((2,)),
+            pltpu.SemaphoreType.DMA((3,)),
         ],
         vmem=24,
-        in_specs=[whole, far, whole, far, whole, whole],
-    )(carried, first, wide_bias(bias_first), stack, wide_bias(bias_second), channel_mask)
+        in_specs=[far, far, whole, far, whole, whole],
+    )(pltpu.with_memory_space_constraint(carried, pltpu.HBM), first, wide_bias(bias_first), stack, wide_bias(bias_second), channel_mask)
 
     fields = []
     for v in range(pairs):

time: 162 us -> 166 us (1.025)
  Pallas kernels: 80.2 us -> 82.9 us
    pallas_call x1, Pallas kernels: 8.72 us -> 12.2 us  [body(): call(prep_kernel, [pltpu.HBM((2, full_l, side), BF), pltpu.HBM((4, 2, sid...]
    unnamed x20 -> x24, local copies, waits for them, and re-layouts: 3.61 us -> 4.58 us
  transfers between devices with their start and end apart: 17 -> 17, of which waited for: 3 -> 3; matrix products, arithmetic and copies ran while one was open for 0% -> 0% of each run, Pallas kernels for 31% -> 32%
where the time goes in v2:
time: 166 us; the launch traced here: 163 us
  Pallas kernels  82.9 us (50%)
  waiting for transfers between devices  39.9 us (24%)
  starting transfers between devices  34.2 us (21%)
  local copies, waits for them, and re-layouts  4.59 us (3%)
    ppermute x16, waiting for transfers between devices, swap(): return lax.ppermute(value, axis, pairs + [(j, i) for i, j in pairs])  39.9 us
    pallas_call x2, Pallas kernels, body(): call(net_kernel, [shaped((tile_x, tile_y, levels))] + [shaped((SWEEPS, ti...  33.2 us
    ppermute x16, starting transfers between devices, swap(): return lax.ppermute(value, axis, pairs + [(j, i) for i, j in pairs])  27.8 us
    pallas_call x1, Pallas kernels, body(): call(prep_kernel, [pltpu.HBM((2, full_l, side), BF), pltpu.HBM((4, 2, sid...  12.2 us
    pallas_call x2, Pallas kernels, body(): call(functools.partial(diffuse_kernel, v > 0), [shaped((cells, side))] +...  12.1 us
    pallas_call x2, Pallas kernels, body(): call(finish_kernel, shaped(vectors.shape), flops=40 * tall * around * dee...  10 us
    pallas_call x1, Pallas kernels, body(): call(functools.partial(hidden_kernel, mark, bucket), [shaped((3, slots, s...  6.65 us
    all_to_all x1, starting transfers between devices, body(): lax.all_to_all(packed.reshape(devices, bucket, deep), ('gx', 'gy'), split...  6.37 us
  transfers between devices with their start and end apart: 17, of which 3 were waited for; matrix products, arithmetic and copies ran while one was open for 0% of the time, Pallas kernels for 32%

profile of v2, /device:TPU:9, one launch (start us, length us, event | category | flops | bytes accessed | tf_op | source)
XLA Modules:
  0.0 163.4 jit_solution(8896661243482959595)
XLA Ops:
  0.7 0.7 fusion.6
  1.4 1.2 copy-done.8
  2.6 2.2 %shard_map.134 = f32[512,640]{1,0:T(8,128)} custom-call(s32[1,512]{1,0:T(1,128)S(1)} %bitcast.11, f32[1,512]{1,0:T(1,128)S(1)} %bitcast.10, f32[548,512]{1,0:T(8,128)S(1)} %bitcast.12), custom_call_target="tpu_custom_call" | custom-call | flops 1006632960 | bytes 2621440 | tf_op jit(solution)/shard_map/pallas_call | solution.py:498
  4.9 6.4 %all-to-all-start = ((f32[32,16,640]{2,1,0:T(8,128)}), f32[32,16,640]{2,1,0:T(8,128)}, u32[]{:S(2)}, u32[]{:S(2)}) async-start(f32[32,16,640]{2,1,0:T(8,128)} %bitcast.7), calls=%async_computation | async-start | bytes 2621440 | tf_op jit(solution)/shard_map/all_to_all | solution.py:506
  11.3 1.9 %shard_map.127 = (f32[4,32,549]{2,1,0:T(8,128)S(1)}, f32[4,32,549]{2,1,0:T(8,128)S(1)}, f32[16,4,549]{2,1,0:T(4,128)S(1)}, f32[16,4,549]{2,1,0:T(4,128)S(1)}) custom-call(s32[2]{0:T(128)S(1)} %pad_add_fusion.side_ref, f32[2,16,32,548]{3,2,1,0:T(8,128)} %base_ref.3, f32[16,32]{1,0:T(8,128)S(1)} %copy-done.5), custom_call_target="tpu_custom_call" | custom-call | bytes 2244608 | tf_op jit(solution)/shard_map/pallas_call | solution.py:479
  13.3 1.2 collective-permute-start
  14.5 2.0 %collective-permute-start.1 = (f32[4,32,549]{2,1,0:T(8,128)S(1)}, f32[4,32,549]{2,1,0:T(8,128)S(1)}, u32[]{:S(2)}, u32[]{:S(2)}) collective-permute-start(f32[4,32,549]{2,1,0:T(8,128)S(1)} %get-tuple-element.39), channel_id=1, source_target_pairs={{4,8},{12,16},{20,24},{8,4},{16,12},{24,20},{5,9},{13,17},{21,25},... | collective-permute-start | bytes 843272 | tf_op jit(solution)/shard_map/ppermute | solution.py:431
  16.5 1.9 %shard_map.131 = (f32[4,32,548]{2,1,0:T(8,128)S(1)}, f32[4,32,548]{2,1,0:T(8,128)S(1)}, f32[16,4,548]{2,1,0:T(4,128)S(1)}, f32[16,4,548]{2,1,0:T(4,128)S(1)}) custom-call(s32[2]{0:T(128)S(1)} %pad_add_fusion.side_ref, f32[2,16,32,548]{3,2,1,0:T(8,128)} %base_ref.3, f32[16,32]{1,0:T(8,128)S(1)} %copy-done.5), custom_call_target="tpu_custom_call" | custom-call | bytes 2244608 | tf_op jit(solution)/shard_map/pallas_call | solution.py:479
  18.5 2.3 %collective-permute-start.4 = (f32[4,32,548]{2,1,0:T(8,128)S(1)}, f32[4,32,548]{2,1,0:T(8,128)S(1)}, u32[]{:S(2)}, u32[]{:S(2)}) collective-permute-start(f32[4,32,548]{2,1,0:T(8,128)S(1)} %get-tuple-element.46), channel_id=1, source_target_pairs={{0,4},{8,12},{16,20},{24,28},{4,0},{12,8},{20,16},{28,24},{1,5},{9... | collective-permute-start | bytes 841736 | tf_op jit(solution)/shard_map/ppermute | solution.py:431
  20.8 1.9 %collective-permute-start.5 = (f32[4,32,548]{2,1,0:T(8,128)S(1)}, f32[4,32,548]{2,1,0:T(8,128)S(1)}, u32[]{:S(2)}, u32[]{:S(2)}) collective-permute-start(f32[4,32,548]{2,1,0:T(8,128)S(1)} %get-tuple-element.47), channel_id=1, source_target_pairs={{4,8},{12,16},{20,24},{8,4},{16,12},{24,20},{5,9},{13,17},{21,25},... | collective-permute-start | bytes 841736 | tf_op jit(solution)/shard_map/ppermute | solution.py:431
  22.7 32.5 %collective-permute-done.4.ra.refs_0_ = f32[4,32,548]{2,1,0:T(8,128)S(1)} collective-permute-done((f32[4,32,548]{2,1,0:T(8,128)S(1)}, f32[4,32,548]{2,1,0:T(8,128)S(1)}, u32[]{:S(2)}, u32[]{:S(2)}) %collective-permute-start.4) | collective-permute-done | bytes 280608 | tf_op jit(solution)/shard_map/ppermute | solution.py:431
  55.9 1.0 collective-permute-start.6
  57.0 3.0 %collective-permute-start.7 = (f32[24,4,548]{2,1,0:T(4,128)S(1)}, f32[24,4,548]{2,1,0:T(4,128)S(1)}, u32[]{:S(2)}, u32[]{:S(2)}) collective-permute-start(f32[24,4,548]{2,1,0:T(4,128)S(1)} %get-tuple-element.51), channel_id=1, source_target_pairs={{1,2},{2,1},{5,6},{6,5},{9,10},{10,9},{13,14},{14,13},{17,18},{18,... | collective-permute-start | bytes 631304 | tf_op jit(solution)/shard_map/ppermute | solution.py:431
  60.7 2.6 %collective-permute-start.3 = (f32[24,4,549]{2,1,0:T(4,128)S(1)}, f32[24,4,549]{2,1,0:T(4,128)S(1)}, u32[]{:S(2)}, u32[]{:S(2)}) collective-permute-start(f32[24,4,549]{2,1,0:T(4,128)S(1)} %get-tuple-element.43), channel_id=1, source_target_pairs={{1,2},{2,1},{5,6},{6,5},{9,10},{10,9},{13,14},{14,13},{17,18},{18,... | collective-permute-start | bytes 632456 | tf_op jit(solution)/shard_map/ppermute | solution.py:431
  63.3 12.2 %shard_map.129 = (bf16[2,768,768]{2,1,0:T(8,128)(2,1)}, bf16[4,2,768,768]{3,2,1,0:T(8,128)(2,1)}) custom-call(f32[548,548]{1,0:T(8,128)} %refs_0_.1, f32[548,768]{1,0:T(8,128)} %refs_1_.1, f32[768,768]{1,0:T(8,128)} %refs_2_.1, f32[616,768]{1,0:T(8,128)} %bitcast.13, f32[616,616]{1,0:T(8,128)} %refs_4_.1), custom_call_target="tpu_custom_call" | custom-call | flops 2717908992 | bytes 23592960 | tf_op jit(solution)/shard_map/pallas_call | solution.py:513
  75.6 6.3 %shard_map.130 = (f32[512,768]{1,0:T(8,128)S(1)}, f32[2,24,40,128]{3,2,1,0:T(8,128)S(1)}) custom-call(s32[2]{0:T(128)S(1)} %pad_add_fusion.side_ref, f32[2,16,32,548]{3,2,1,0:T(8,128)S(1)} %copy-done, f32[16,32]{1,0:T(8,128)S(1)} %copy-done.5, f32[4,32,549]{2,1,0:T(8,128)S(1)} %collective-permute-done.ra.refs_0_, ...), custom_call_target="tpu_custom_call" | custom-call | flops 1509949440 | bytes 4915200 | tf_op jit(solution)/shard_map/pallas_call | solution.py:538
  81.9 1.1 copy-done.6
  83.1 5.8 %shard_map.133.q_ref = f32[512,768]{1,0:T(8,128)S(1)} custom-call(s32[2]{0:T(128)S(1)} %pad_add_fusion.side_ref, f32[2,16,32,548]{3,2,1,0:T(8,128)S(1)} %copy-done, f32[2,24,40,128]{3,2,1,0:T(8,128)S(1)} %get-tuple-element.45.coeff_ref.cb_ref, f32[4,32,548]{2,1,0:T(8,128)S(1)} %collective-permute-done.4.ra.refs_0_, ...), custom_call_target="tpu_custom_call" | custom-call | flops 1509949440 | bytes 4915200 | tf_op jit(solution)/shard_map/pallas_call | solution.py:538
  88.9 1.0 copy-done.1
  89.9 1.2 copy-done.3
  91.1 6.6 %shard_map.135 = (f32[3,512,768]{2,1,0:T(8,128)S(1)}, bf16[512,512]{1,0:T(8,128)(2,1)S(1)}, bf16[512,512]{1,0:T(8,128)(2,1)S(1)}) custom-call(f32[512,640]{1,0:T(8,128)} %bitcast.8.x_ref, bf16[2,768,768]{2,1,0:T(8,128)(2,1)} %get-tuple-element.52.first_ref, f32[1,768]{1,0:T(1,128)S(1)} %broadcast_in_dim.16.b1_ref, ...), custom_call_target="tpu_custom_call" | custom-call | flops 3623878656 | bytes 3145728 | tf_op jit(solution)/shard_map/pallas_call | solution.py:560
  97.8 16.7 %shard_map.138 = (f32[16,32,548]{2,1,0:T(8,128)S(1)}, f32[4,32,548]{2,1,0:T(8,128)S(1)}, f32[4,32,548]{2,1,0:T(8,128)S(1)}, f32[16,4,548]{2,1,0:T(4,128)S(1)}, f32[16,4,548]{2,1,0:T(4,128)S(1)}) custom-call(s32[2]{0:T(128)S(1)} %pad_add_fusion.side_ref, f32[512,768]{1,0:T(8,128)S(1)} %copy-done.7, bf16[512,512]{1,0:T(8,128)(2,1)S(1)} %get-tuple-element.53.one_ref, ...), custom_call_target="tpu_custom_call" | custom-call | flops 10871635968 | bytes 11796480 | tf_op jit(solution)/shard_map/pallas_call | solution.py:578
  114.5 1.3 collective-permute-start.12
  115.7 1.9 %collective-permute-start.13 = (f32[4,32,548]{2,1,0:T(8,128)S(1)}, f32[4,32,548]{2,1,0:T(8,128)S(1)}, u32[]{:S(2)}, u32[]{:S(2)}) collective-permute-start(f32[4,32,548]{2,1,0:T(8,128)S(1)} %get-tuple-element.66), channel_id=1, source_target_pairs={{4,8},{12,16},{20,24},{8,4},{16,12},{24,20},{5,9},{13,17},{21,25},... | collective-permute-start | bytes 841736 | tf_op jit(solution)/shard_map/ppermute | solution.py:431
  117.7 16.5 %shard_map.136 = (f32[16,32,548]{2,1,0:T(8,128)S(1)}, f32[4,32,548]{2,1,0:T(8,128)S(1)}, f32[4,32,548]{2,1,0:T(8,128)S(1)}, f32[16,4,548]{2,1,0:T(4,128)S(1)}, f32[16,4,548]{2,1,0:T(4,128)S(1)}) custom-call(s32[2]{0:T(128)S(1)} %pad_add_fusion.side_ref, f32[512,768]{1,0:T(8,128)S(1)} %copy-done.4, bf16[512,512]{1,0:T(8,128)(2,1)S(1)} %get-tuple-element.53.one_ref, ...), custom_call_target="tpu_custom_call" | custom-call | flops 10871635968 | bytes 11796480 | tf_op jit(solution)/shard_map/pallas_call | solution.py:578
  134.2 1.5 collective-permute-start.8
  135.7 2.9 %collective-permute-start.9 = (f32[4,32,548]{2,1,0:T(8,128)S(1)}, f32[4,32,548]{2,1,0:T(8,128)S(1)}, u32[]{:S(2)}, u32[]{:S(2)}) collective-permute-start(f32[4,32,548]{2,1,0:T(8,128)S(1)} %get-tuple-element.58), channel_id=1, source_target_pairs={{4,8},{12,16},{20,24},{8,4},{16,12},{24,20},{5,9},{13,17},{21,25},... | collective-permute-start | bytes 841736 | tf_op jit(solution)/shard_map/ppermute | solution.py:431
  139.4 3.9 %collective-permute-start.15 = (f32[24,4,548]{2,1,0:T(4,128)S(1)}, f32[24,4,548]{2,1,0:T(4,128)S(1)}, u32[]{:S(2)}, u32[]{:S(2)}) collective-permute-start(f32[24,4,548]{2,1,0:T(4,128)S(1)} %get-tuple-element.70), channel_id=1, source_target_pairs={{1,2},{2,1},{5,6},{6,5},{9,10},{10,9},{13,14},{14,13},{17,18},{18,... | collective-permute-start | bytes 631304 | tf_op jit(solution)/shard_map/ppermute | solution.py:431
  143.3 6.8 %collective-permute-done.8.ra.refs_0_ = f32[4,32,548]{2,1,0:T(8,128)S(1)} collective-permute-done((f32[4,32,548]{2,1,0:T(8,128)S(1)}, f32[4,32,548]{2,1,0:T(8,128)S(1)}, u32[]{:S(2)}, u32[]{:S(2)}) %collective-permute-start.8) | collective-permute-done | bytes 280608 | tf_op jit(solution)/shard_map/ppermute | solution.py:431
  150.9 1.9 %collective-permute-start.11 = (f32[24,4,548]{2,1,0:T(4,128)S(1)}, f32[24,4,548]{2,1,0:T(4,128)S(1)}, u32[]{:S(2)}, u32[]{:S(2)}) collective-permute-start(f32[24,4,548]{2,1,0:T(4,128)S(1)} %get-tuple-element.62), channel_id=1, source_target_pairs={{1,2},{2,1},{5,6},{6,5},{9,10},{10,9},{13,14},{14,13},{17,18},{18,... | collective-permute-start | bytes 631304 | tf_op jit(solution)/shard_map/ppermute | solution.py:431
  152.9 5.0 %shard_map.140.refs_4_ = f32[2,16,32,548]{3,2,1,0:T(8,128)} custom-call(s32[2]{0:T(128)S(1)} %pad_add_fusion.side_ref, f32[16,32,548]{2,1,0:T(8,128)S(1)} %get-tuple-element.64.field_ref, f32[2,16,32,548]{3,2,1,0:T(8,128)S(1)} %copy-done, f32[2,24,40,128]{3,2,1,0:T(8,128)S(1)} %copy-done.2, f32[4,32,548]{2,1,0:T(8,128)S(1)} %collective-permute-done.12.ra.refs_0_, ...), custom_call_target="tpu_custom_call" | custom-call | flops 24576000 | bytes 3932160 | tf_op jit(solution)/shard_map/pallas_call | solution.py:601
  158.4 5.0 %shard_map.141 = f32[2,16,32,548]{3,2,1,0:T(8,128)} custom-call(s32[2]{0:T(128)S(1)} %pad_add_fusion.side_ref, f32[16,32,548]{2,1,0:T(8,128)S(1)} %get-tuple-element.56.field_ref, f32[2,16,32,548]{3,2,1,0:T(8,128)S(1)} %copy-done, f32[2,24,40,128]{3,2,1,0:T(8,128)S(1)} %copy-done.2, ...), custom_call_target="tpu_custom_call", output_to_operand_aliasing={{}: (8, {})} | custom-call | flops 24576000 | bytes 3932160 | tf_op jit(solution)/shard_map/pallas_call | solution.py:601
  (45 shorter events, 3.5 us)
Async XLA Ops:
  1.4 1.3 copy-start.8
  4.9 6.5 %copy-start.5 = (f32[16,32]{1,0:T(8,128)S(1)}, f32[16,32]{1,0:T(8,128)}, u32[]{:S(2)}) copy-start(f32[16,32]{1,0:T(8,128)} %coeff_ref.5) | copy-start | bytes 6148
  4.9 86.2 %all-to-all-start = ((f32[32,16,640]{2,1,0:T(8,128)}), f32[32,16,640]{2,1,0:T(8,128)}, u32[]{:S(2)}, u32[]{:S(2)}) async-start(f32[32,16,640]{2,1,0:T(8,128)} %bitcast.7), calls=%async_computation | async-start | bytes 2621440 | tf_op jit(solution)/shard_map/all_to_all | solution.py:506
  13.3 46.7 %collective-permute-start = (f32[4,32,549]{2,1,0:T(8,128)S(1)}, f32[4,32,549]{2,1,0:T(8,128)S(1)}, u32[]{:S(2)}, u32[]{:S(2)}) collective-permute-start(f32[4,32,549]{2,1,0:T(8,128)S(1)} %get-tuple-element.38), channel_id=1, source_target_pairs={{0,4},{8,12},{16,20},{24,28},{4,0},{12,8},{20,16},{28,24},{1,5},{9... | collective-permute-start | bytes 843272 | tf_op jit(solution)/shard_map/ppermute | solution.py:431
  14.5 45.4 %collective-permute-start.1 = (f32[4,32,549]{2,1,0:T(8,128)S(1)}, f32[4,32,549]{2,1,0:T(8,128)S(1)}, u32[]{:S(2)}, u32[]{:S(2)}) collective-permute-start(f32[4,32,549]{2,1,0:T(8,128)S(1)} %get-tuple-element.39), channel_id=1, source_target_pairs={{4,8},{12,16},{20,24},{8,4},{16,12},{24,20},{5,9},{13,17},{21,25},... | collective-permute-start | bytes 843272 | tf_op jit(solution)/shard_map/ppermute | solution.py:431
  18.5 36.8 %collective-permute-start.4 = (f32[4,32,548]{2,1,0:T(8,128)S(1)}, f32[4,32,548]{2,1,0:T(8,128)S(1)}, u32[]{:S(2)}, u32[]{:S(2)}) collective-permute-start(f32[4,32,548]{2,1,0:T(8,128)S(1)} %get-tuple-element.46), channel_id=1, source_target_pairs={{0,4},{8,12},{16,20},{24,28},{4,0},{12,8},{20,16},{28,24},{1,5},{9... | collective-permute-start | bytes 841736 | tf_op jit(solution)/shard_map/ppermute | solution.py:431
  20.8 34.5 %collective-permute-start.5 = (f32[4,32,548]{2,1,0:T(8,128)S(1)}, f32[4,32,548]{2,1,0:T(8,128)S(1)}, u32[]{:S(2)}, u32[]{:S(2)}) collective-permute-start(f32[4,32,548]{2,1,0:T(8,128)S(1)} %get-tuple-element.47), channel_id=1, source_target_pairs={{4,8},{12,16},{20,24},{8,4},{16,12},{24,20},{5,9},{13,17},{21,25},... | collective-permute-start | bytes 841736 | tf_op jit(solution)/shard_map/ppermute | solution.py:431
  55.9 27.2 %collective-permute-start.6 = (f32[24,4,548]{2,1,0:T(4,128)S(1)}, f32[24,4,548]{2,1,0:T(4,128)S(1)}, u32[]{:S(2)}, u32[]{:S(2)}) collective-permute-start(f32[24,4,548]{2,1,0:T(4,128)S(1)} %get-tuple-element.50), channel_id=1, source_target_pairs={{0,1},{2,3},{1,0},{3,2},{4,5},{6,7},{5,4},{7,6},{8,9},{10,11},{9,8... | collective-permute-start | bytes 631304 | tf_op jit(solution)/shard_map/ppermute | solution.py:431
  57.0 26.1 %collective-permute-start.7 = (f32[24,4,548]{2,1,0:T(4,128)S(1)}, f32[24,4,548]{2,1,0:T(4,128)S(1)}, u32[]{:S(2)}, u32[]{:S(2)}) collective-permute-start(f32[24,4,548]{2,1,0:T(4,128)S(1)} %get-tuple-element.51), channel_id=1, source_target_pairs={{1,2},{2,1},{5,6},{6,5},{9,10},{10,9},{13,14},{14,13},{17,18},{18,... | collective-permute-start | bytes 631304 | tf_op jit(solution)/shard_map/ppermute | solution.py:431
  60.6 15.0 %collective-permute-start.2 = (f32[24,4,549]{2,1,0:T(4,128)S(1)}, f32[24,4,549]{2,1,0:T(4,128)S(1)}, u32[]{:S(2)}, u32[]{:S(2)}) collective-permute-start(f32[24,4,549]{2,1,0:T(4,128)S(1)} %get-tuple-element.42), channel_id=1, source_target_pairs={{0,1},{2,3},{1,0},{3,2},{4,5},{6,7},{5,4},{7,6},{8,9},{10,11},{9,8... | collective-permute-start | bytes 632456 | tf_op jit(solution)/shard_map/ppermute | solution.py:431
  60.7 14.9 %collective-permute-start.3 = (f32[24,4,549]{2,1,0:T(4,128)S(1)}, f32[24,4,549]{2,1,0:T(4,128)S(1)}, u32[]{:S(2)}, u32[]{:S(2)}) collective-permute-start(f32[24,4,549]{2,1,0:T(4,128)S(1)} %get-tuple-element.43), channel_id=1, source_target_pairs={{1,2},{2,1},{5,6},{6,5},{9,10},{10,9},{13,14},{14,13},{17,18},{18,... | collective-permute-start | bytes 632456 | tf_op jit(solution)/shard_map/ppermute | solution.py:431
  63.3 12.3 %copy-start.10 = (f32[768]{0:T(1024)S(1)}, f32[768]{0:T(1024)}, u32[]{:S(2)}) copy-start(f32[768]{0:T(1024)} %param.17) | copy-start | bytes 9220
  63.3 12.3 %copy-start.11 = (f32[768]{0:T(1024)S(1)}, f32[768]{0:T(1024)}, u32[]{:S(2)}) copy-start(f32[768]{0:T(1024)} %param.19) | copy-start | bytes 9220
  63.3 12.3 %copy-start = (f32[2,16,32,548]{3,2,1,0:T(8,128)S(1)}, f32[2,16,32,548]{3,2,1,0:T(8,128)}, u32[]{:S(2)}) copy-start(f32[2,16,32,548]{3,2,1,0:T(8,128)} %base_ref.3) | copy-start | bytes 6733828
  81.9 1.1 copy-start.6
  83.1 8.0 %copy-start.9 = (s32[32,616]{1,0:T(8,128)S(1)}, s32[32,616]{1,0:T(8,128)}, u32[]{:S(2)}) copy-start(s32[32,616]{1,0:T(8,128)} %mask_ref.1) | copy-start | bytes 236548
  88.9 1.0 copy-start.1
  89.9 1.2 copy-start.3
  91.1 6.7 %copy-start.7 = (f32[512,768]{1,0:T(8,128)S(1)}, f32[512,768]{1,0:T(8,128)}, u32[]{:S(2)}) copy-start(f32[512,768]{1,0:T(8,128)} %copy-done.6) | copy-start | bytes 4718596
  97.8 19.9 %copy-start.4 = (f32[512,768]{1,0:T(8,128)S(1)}, f32[512,768]{1,0:T(8,128)}, u32[]{:S(2)}) copy-start(f32[512,768]{1,0:T(8,128)} %copy-done.3) | copy-start | bytes 4718596
  114.5 24.2 %collective-permute-start.12 = (f32[4,32,548]{2,1,0:T(8,128)S(1)}, f32[4,32,548]{2,1,0:T(8,128)S(1)}, u32[]{:S(2)}, u32[]{:S(2)}) collective-permute-start(f32[4,32,548]{2,1,0:T(8,128)S(1)} %get-tuple-element.65), channel_id=1, source_target_pairs={{0,4},{8,12},{16,20},{24,28},{4,0},{12,8},{20,16},{28,24},{1,5},{9... | collective-permute-start | bytes 841736 | tf_op jit(solution)/shard_map/ppermute | solution.py:431
  115.7 22.9 %collective-permute-start.13 = (f32[4,32,548]{2,1,0:T(8,128)S(1)}, f32[4,32,548]{2,1,0:T(8,128)S(1)}, u32[]{:S(2)}, u32[]{:S(2)}) collective-permute-start(f32[4,32,548]{2,1,0:T(8,128)S(1)} %get-tuple-element.66), channel_id=1, source_target_pairs={{4,8},{12,16},{20,24},{8,4},{16,12},{24,20},{5,9},{13,17},{21,25},... | collective-permute-start | bytes 841736 | tf_op jit(solution)/shard_map/ppermute | solution.py:431
  134.2 18.7 %copy-start.2 = (f32[2,24,40,128]{3,2,1,0:T(8,128)S(1)}, f32[2,24,40,128]{3,2,1,0:T(8,128)}, u32[]{:S(2)}) copy-start(f32[2,24,40,128]{3,2,1,0:T(8,128)} %copy-done.1) | copy-start | bytes 2949124
  134.2 15.9 %collective-permute-start.8 = (f32[4,32,548]{2,1,0:T(8,128)S(1)}, f32[4,32,548]{2,1,0:T(8,128)S(1)}, u32[]{:S(2)}, u32[]{:S(2)}) collective-permute-start(f32[4,32,548]{2,1,0:T(8,128)S(1)} %get-tuple-element.57), channel_id=1, source_target_pairs={{0,4},{8,12},{16,20},{24,28},{4,0},{12,8},{20,16},{28,24},{1,5},{9... | collective-permute-start | bytes 841736 | tf_op jit(solution)/shard_map/ppermute | solution.py:431
  135.7 14.4 %collective-permute-start.9 = (f32[4,32,548]{2,1,0:T(8,128)S(1)}, f32[4,32,548]{2,1,0:T(8,128)S(1)}, u32[]{:S(2)}, u32[]{:S(2)}) collective-permute-start(f32[4,32,548]{2,1,0:T(8,128)S(1)} %get-tuple-element.58), channel_id=1, source_target_pairs={{4,8},{12,16},{20,24},{8,4},{16,12},{24,20},{5,9},{13,17},{21,25},... | collective-permute-start | bytes 841736 | tf_op jit(solution)/shard_map/ppermute | solution.py:431
  139.3 13.5 %collective-permute-start.14 = (f32[24,4,548]{2,1,0:T(4,128)S(1)}, f32[24,4,548]{2,1,0:T(4,128)S(1)}, u32[]{:S(2)}, u32[]{:S(2)}) collective-permute-start(f32[24,4,548]{2,1,0:T(4,128)S(1)} %get-tuple-element.69), channel_id=1, source_target_pairs={{0,1},{2,3},{1,0},{3,2},{4,5},{6,7},{5,4},{7,6},{8,9},{10,11},{9,8... | collective-permute-start | bytes 631304 | tf_op jit(solution)/shard_map/ppermute | solution.py:431
  139.4 13.4 %collective-permute-start.15 = (f32[24,4,548]{2,1,0:T(4,128)S(1)}, f32[24,4,548]{2,1,0:T(4,128)S(1)}, u32[]{:S(2)}, u32[]{:S(2)}) collective-permute-start(f32[24,4,548]{2,1,0:T(4,128)S(1)} %get-tuple-element.70), channel_id=1, source_target_pairs={{1,2},{2,1},{5,6},{6,5},{9,10},{10,9},{13,14},{14,13},{17,18},{18,... | collective-permute-start | bytes 631304 | tf_op jit(solution)/shard_map/ppermute | solution.py:431
  150.8 7.1 %collective-permute-start.10 = (f32[24,4,548]{2,1,0:T(4,128)S(1)}, f32[24,4,548]{2,1,0:T(4,128)S(1)}, u32[]{:S(2)}, u32[]{:S(2)}) collective-permute-start(f32[24,4,548]{2,1,0:T(4,128)S(1)} %get-tuple-element.61), channel_id=1, source_target_pairs={{0,1},{2,3},{1,0},{3,2},{4,5},{6,7},{5,4},{7,6},{8,9},{10,11},{9,8... | collective-permute-start | bytes 631304 | tf_op jit(solution)/shard_map/ppermute | solution.py:431
  150.9 7.5 %collective-permute-start.11 = (f32[24,4,548]{2,1,0:T(4,128)S(1)}, f32[24,4,548]{2,1,0:T(4,128)S(1)}, u32[]{:S(2)}, u32[]{:S(2)}) collective-permute-start(f32[24,4,548]{2,1,0:T(4,128)S(1)} %get-tuple-element.62), channel_id=1, source_target_pairs={{1,2},{2,1},{5,6},{6,5},{9,10},{10,9},{13,14},{14,13},{17,18},{18,... | collective-permute-start | bytes 631304 | tf_op jit(solution)/shard_map/ppermute | solution.py:431

commit v3 on v2

--- a/solution.py
+++ b/solution.py
@@ -30,9 +30,9 @@
 
 
 def mm3(left_high, left_low, right_high, right_low, dims=NN):
-    return mm(left_high, right_high, dims) + (
-        mm(left_high, right_low, dims) + mm(left_low, right_high, dims)
-    )
+    left = jnp.concatenate([left_high, left_low, left_high], axis=dims[0][0])
+    right = jnp.concatenate([right_high, right_high, right_low], axis=dims[1][0])
+    return mm(left, right, dims)
 
 
 def halves(size):
@@ -107,18 +107,15 @@
     fetch[1].wait()
     put(raw[1][...], first)
     send(first, first_out)
-    for copy in fetch[2:]:
-        copy.wait()
     rows = up(raw[0].shape[1], LANES)
     stack[3, :, rows:, :] = jnp.zeros((2,) + (stack.shape[2] - rows, stack.shape[3]), BF)
-    parts = halves(rows)
+    for part in halves(rows):
+        got = mm3(turned[0, part, :], turned[1, part, :], first[0], first[1])
+        stack[3, 0, part, :], stack[3, 1, part, :] = split(got)
+    send(stack.at[3], stack_out.at[3])
     for k in range(3):
-        if k < len(parts):
-            part = parts[k]
-            got = mm3(turned[0, part, :], turned[1, part, :], first[0], first[1])
-            stack[3, 0, part, :], stack[3, 1, part, :] = split(got)
+        fetch[k + 2].wait()
         put(raw[k + 2][...], stack.at[k])
-    for k in range(4):
         send(stack.at[k], stack_out.at[k])
     for copy in sends:
         copy.wait()
@@ -521,7 +518,7 @@
             pltpu.VMEM((2, side, full_l), BF),
             pltpu.SemaphoreType.DMA((5,)), pltpu.SemaphoreType.DMA((5,)),
         ],
-        vmem=34,
+        vmem=27,
         in_specs=[far] * 5,
         out_specs=[far] * 2,
     )(*[pltpu.with_memory_space_constraint(weight, pltpu.HBM) for weight in weights])
@@ -549,7 +546,7 @@
                 pltpu.SemaphoreType.DMA,
             ],
             grid=(1,),
-            vmem=18,
+            vmem=14,
             in_specs=[scalars, block(v)] + [whole] * 5 + [far],
             out_specs=[whole] * (2 - (v > 0)),
         )(sides, vectors, spread if v else diffusivity, *strips[v], stack)
@@ -568,7 +565,7 @@
             pltpu.VMEM((2, full_l, side), BF), pltpu.VMEM((2, side, side), BF),
             pltpu.SemaphoreType.DMA((3,)),
         ],
-        vmem=24,
+        vmem=18,
         in_specs=[far, far, whole, far, whole, whole],
     )(pltpu.with_memory_space_constraint(carried, pltpu.HBM), first, wide_bias(bias_first), stack, wide_bias(bias_second), channel_mask)
 
@@ -589,7 +586,7 @@
                     pltpu.VMEM((4, 2, side, side), BF),
                     pltpu.SemaphoreType.DMA((4,)),
                 ],
-                vmem=30,
+                vmem=22,
                 in_specs=[scalars] + [whole] * 4 + [far],
             )(sides, queries[v], one, one_t, scale, stack)
         )
@@ -609,7 +606,7 @@
                 pltpu.VMEM((tile_x, tile_y, deep), F32),
             ],
             grid=(1,),
-            vmem=18,
+            vmem=14,
             in_specs=[scalars, whole, block(v)] + [whole] * 5
             + [pl.BlockSpec(memory_space=pl.ANY)] * len(carry),
             out_specs=block(v),

time: 166 us -> 161 us (0.970)
  Pallas kernels: 82.9 us -> 78.6 us
    pallas_call x1, Pallas kernels: 12.2 us -> 8.29 us  [body(): call(prep_kernel, [pltpu.HBM((2, full_l, side), BF), pltpu.HBM((4, 2, sid...]
  transfers between devices with their start and end apart: 17 -> 17, of which waited for: 3 -> 3; matrix products, arithmetic and copies ran while one was open for 0% -> 0% of each run, Pallas kernels for 32% -> 30%
where the time goes in v3:
time: 161 us; the launch traced here: 159 us
  Pallas kernels  78.6 us (49%)
  waiting for transfers between devices  39.9 us (25%)
  starting transfers between devices  34.2 us (21%)
  local copies, waits for them, and re-layouts  4.59 us (3%)
    ppermute x16, waiting for transfers between devices, swap(): return lax.ppermute(value, axis, pairs + [(j, i) for i, j in pairs])  39.9 us
    pallas_call x2, Pallas kernels, body(): call(net_kernel, [shaped((tile_x, tile_y, levels))] + [shaped((SWEEPS, ti...  33.6 us
    ppermute x16, starting transfers between devices, swap(): return lax.ppermute(value, axis, pairs + [(j, i) for i, j in pairs])  27.8 us
    pallas_call x2, Pallas kernels, body(): call(functools.partial(diffuse_kernel, v > 0), [shaped((cells, side))] +...  11.8 us
    pallas_call x2, Pallas kernels, body(): call(finish_kernel, shaped(vectors.shape), flops=40 * tall * around * dee...  10 us
    pallas_call x1, Pallas kernels, body(): call(prep_kernel, [pltpu.HBM((2, full_l, side), BF), pltpu.HBM((4, 2, sid...  8.29 us
    all_to_all x1, starting transfers between devices, body(): lax.all_to_all(packed.reshape(devices, bucket, deep), ('gx', 'gy'), split...  6.37 us
    pallas_call x1, Pallas kernels, body(): call(functools.partial(hidden_kernel, mark, bucket), [shaped((3, slots, s...  6.3 us
  transfers between devices with their start and end apart: 17, of which 3 were waited for; matrix products, arithmetic and copies ran while one was open for 0% of the time, Pallas kernels for 30%

profile of v3, /device:TPU:9, one launch (start us, length us, event | category | flops | bytes accessed | tf_op | source)
XLA Modules:
  0.0 159.1 jit_solution(12590001039510848397)
XLA Ops:
  0.7 0.7 fusion.6
  1.4 1.2 copy-done.8
  2.6 2.2 %shard_map.134 = f32[512,640]{1,0:T(8,128)} custom-call(s32[1,512]{1,0:T(1,128)S(1)} %bitcast.11, f32[1,512]{1,0:T(1,128)S(1)} %bitcast.10, f32[548,512]{1,0:T(8,128)S(1)} %bitcast.12), custom_call_target="tpu_custom_call" | custom-call | flops 1006632960 | bytes 2621440 | tf_op jit(solution)/shard_map/pallas_call | solution.py:495
  4.9 6.4 %all-to-all-start = ((f32[32,16,640]{2,1,0:T(8,128)}), f32[32,16,640]{2,1,0:T(8,128)}, u32[]{:S(2)}, u32[]{:S(2)}) async-start(f32[32,16,640]{2,1,0:T(8,128)} %bitcast.7), calls=%async_computation | async-start | bytes 2621440 | tf_op jit(solution)/shard_map/all_to_all | solution.py:503
  11.3 1.9 %shard_map.127 = (f32[4,32,549]{2,1,0:T(8,128)S(1)}, f32[4,32,549]{2,1,0:T(8,128)S(1)}, f32[16,4,549]{2,1,0:T(4,128)S(1)}, f32[16,4,549]{2,1,0:T(4,128)S(1)}) custom-call(s32[2]{0:T(128)S(1)} %pad_add_fusion.side_ref, f32[2,16,32,548]{3,2,1,0:T(8,128)} %base_ref.3, f32[16,32]{1,0:T(8,128)S(1)} %copy-done.5), custom_call_target="tpu_custom_call" | custom-call | bytes 2244608 | tf_op jit(solution)/shard_map/pallas_call | solution.py:476
  13.3 1.2 collective-permute-start
  14.5 2.0 %collective-permute-start.1 = (f32[4,32,549]{2,1,0:T(8,128)S(1)}, f32[4,32,549]{2,1,0:T(8,128)S(1)}, u32[]{:S(2)}, u32[]{:S(2)}) collective-permute-start(f32[4,32,549]{2,1,0:T(8,128)S(1)} %get-tuple-element.39), channel_id=1, source_target_pairs={{4,8},{12,16},{20,24},{8,4},{16,12},{24,20},{5,9},{13,17},{21,25},... | collective-permute-start | bytes 843272 | tf_op jit(solution)/shard_map/ppermute | solution.py:428
  16.5 1.9 %shard_map.131 = (f32[4,32,548]{2,1,0:T(8,128)S(1)}, f32[4,32,548]{2,1,0:T(8,128)S(1)}, f32[16,4,548]{2,1,0:T(4,128)S(1)}, f32[16,4,548]{2,1,0:T(4,128)S(1)}) custom-call(s32[2]{0:T(128)S(1)} %pad_add_fusion.side_ref, f32[2,16,32,548]{3,2,1,0:T(8,128)} %base_ref.3, f32[16,32]{1,0:T(8,128)S(1)} %copy-done.5), custom_call_target="tpu_custom_call" | custom-call | bytes 2244608 | tf_op jit(solution)/shard_map/pallas_call | solution.py:476
  18.5 2.3 %collective-permute-start.4 = (f32[4,32,548]{2,1,0:T(8,128)S(1)}, f32[4,32,548]{2,1,0:T(8,128)S(1)}, u32[]{:S(2)}, u32[]{:S(2)}) collective-permute-start(f32[4,32,548]{2,1,0:T(8,128)S(1)} %get-tuple-element.46), channel_id=1, source_target_pairs={{0,4},{8,12},{16,20},{24,28},{4,0},{12,8},{20,16},{28,24},{1,5},{9... | collective-permute-start | bytes 841736 | tf_op jit(solution)/shard_map/ppermute | solution.py:428
  20.8 1.9 %collective-permute-start.5 = (f32[4,32,548]{2,1,0:T(8,128)S(1)}, f32[4,32,548]{2,1,0:T(8,128)S(1)}, u32[]{:S(2)}, u32[]{:S(2)}) collective-permute-start(f32[4,32,548]{2,1,0:T(8,128)S(1)} %get-tuple-element.47), channel_id=1, source_target_pairs={{4,8},{12,16},{20,24},{8,4},{16,12},{24,20},{5,9},{13,17},{21,25},... | collective-permute-start | bytes 841736 | tf_op jit(solution)/shard_map/ppermute | solution.py:428
  22.7 32.5 %collective-permute-done.4.ra.refs_0_ = f32[4,32,548]{2,1,0:T(8,128)S(1)} collective-permute-done((f32[4,32,548]{2,1,0:T(8,128)S(1)}, f32[4,32,548]{2,1,0:T(8,128)S(1)}, u32[]{:S(2)}, u32[]{:S(2)}) %collective-permute-start.4) | collective-permute-done | bytes 280608 | tf_op jit(solution)/shard_map/ppermute | solution.py:428
  55.9 1.0 collective-permute-start.6
  57.0 3.0 %collective-permute-start.7 = (f32[24,4,548]{2,1,0:T(4,128)S(1)}, f32[24,4,548]{2,1,0:T(4,128)S(1)}, u32[]{:S(2)}, u32[]{:S(2)}) collective-permute-start(f32[24,4,548]{2,1,0:T(4,128)S(1)} %get-tuple-element.51), channel_id=1, source_target_pairs={{1,2},{2,1},{5,6},{6,5},{9,10},{10,9},{13,14},{14,13},{17,18},{18,... | collective-permute-start | bytes 631304 | tf_op jit(solution)/shard_map/ppermute | solution.py:428
  60.7 2.6 %collective-permute-start.3 = (f32[24,4,549]{2,1,0:T(4,128)S(1)}, f32[24,4,549]{2,1,0:T(4,128)S(1)}, u32[]{:S(2)}, u32[]{:S(2)}) collective-permute-start(f32[24,4,549]{2,1,0:T(4,128)S(1)} %get-tuple-element.43), channel_id=1, source_target_pairs={{1,2},{2,1},{5,6},{6,5},{9,10},{10,9},{13,14},{14,13},{17,18},{18,... | collective-permute-start | bytes 632456 | tf_op jit(solution)/shard_map/ppermute | solution.py:428
  63.3 8.3 %shard_map.129 = (bf16[2,768,768]{2,1,0:T(8,128)(2,1)}, bf16[4,2,768,768]{3,2,1,0:T(8,128)(2,1)}) custom-call(f32[548,548]{1,0:T(8,128)} %refs_0_.1, f32[548,768]{1,0:T(8,128)} %refs_1_.1, f32[768,768]{1,0:T(8,128)} %refs_2_.1, f32[616,768]{1,0:T(8,128)} %bitcast.13, f32[616,616]{1,0:T(8,128)} %refs_4_.1), custom_call_target="tpu_custom_call" | custom-call | flops 2717908992 | bytes 23592960 | tf_op jit(solution)/shard_map/pallas_call | solution.py:510
  71.7 6.1 %shard_map.130 = (f32[512,768]{1,0:T(8,128)S(1)}, f32[2,24,40,128]{3,2,1,0:T(8,128)S(1)}) custom-call(s32[2]{0:T(128)S(1)} %pad_add_fusion.side_ref, f32[2,16,32,548]{3,2,1,0:T(8,128)S(1)} %copy-done, f32[16,32]{1,0:T(8,128)S(1)} %copy-done.5, f32[4,32,549]{2,1,0:T(8,128)S(1)} %collective-permute-done.ra.refs_0_, ...), custom_call_target="tpu_custom_call" | custom-call | flops 1509949440 | bytes 4915200 | tf_op jit(solution)/shard_map/pallas_call | solution.py:535
  77.8 1.1 copy-done.6
  78.9 5.6 %shard_map.133.q_ref = f32[512,768]{1,0:T(8,128)S(1)} custom-call(s32[2]{0:T(128)S(1)} %pad_add_fusion.side_ref, f32[2,16,32,548]{3,2,1,0:T(8,128)S(1)} %copy-done, f32[2,24,40,128]{3,2,1,0:T(8,128)S(1)} %get-tuple-element.45.coeff_ref.cb_ref, f32[4,32,548]{2,1,0:T(8,128)S(1)} %collective-permute-done.4.ra.refs_0_, ...), custom_call_target="tpu_custom_call" | custom-call | flops 1509949440 | bytes 4915200 | tf_op jit(solution)/shard_map/pallas_call | solution.py:535
  84.6 1.0 copy-done.1
  85.6 1.2 copy-done.3
  86.8 6.3 %shard_map.135 = (f32[3,512,768]{2,1,0:T(8,128)S(1)}, bf16[512,512]{1,0:T(8,128)(2,1)S(1)}, bf16[512,512]{1,0:T(8,128)(2,1)S(1)}) custom-call(f32[512,640]{1,0:T(8,128)} %bitcast.8.x_ref, bf16[2,768,768]{2,1,0:T(8,128)(2,1)} %get-tuple-element.52.first_ref, f32[1,768]{1,0:T(1,128)S(1)} %broadcast_in_dim.16.b1_ref, ...), custom_call_target="tpu_custom_call" | custom-call | flops 3623878656 | bytes 3145728 | tf_op jit(solution)/shard_map/pallas_call | solution.py:557
  93.1 16.9 %shard_map.138 = (f32[16,32,548]{2,1,0:T(8,128)S(1)}, f32[4,32,548]{2,1,0:T(8,128)S(1)}, f32[4,32,548]{2,1,0:T(8,128)S(1)}, f32[16,4,548]{2,1,0:T(4,128)S(1)}, f32[16,4,548]{2,1,0:T(4,128)S(1)}) custom-call(s32[2]{0:T(128)S(1)} %pad_add_fusion.side_ref, f32[512,768]{1,0:T(8,128)S(1)} %copy-done.7, bf16[512,512]{1,0:T(8,128)(2,1)S(1)} %get-tuple-element.53.one_ref, ...), custom_call_target="tpu_custom_call" | custom-call | flops 10871635968 | bytes 11796480 | tf_op jit(solution)/shard_map/pallas_call | solution.py:575
  110.0 1.2 collective-permute-start.12
  111.3 1.9 %collective-permute-start.13 = (f32[4,32,548]{2,1,0:T(8,128)S(1)}, f32[4,32,548]{2,1,0:T(8,128)S(1)}, u32[]{:S(2)}, u32[]{:S(2)}) collective-permute-start(f32[4,32,548]{2,1,0:T(8,128)S(1)} %get-tuple-element.66), channel_id=1, source_target_pairs={{4,8},{12,16},{20,24},{8,4},{16,12},{24,20},{5,9},{13,17},{21,25},... | collective-permute-start | bytes 841736 | tf_op jit(solution)/shard_map/ppermute | solution.py:428
  113.2 16.7 %shard_map.136 = (f32[16,32,548]{2,1,0:T(8,128)S(1)}, f32[4,32,548]{2,1,0:T(8,128)S(1)}, f32[4,32,548]{2,1,0:T(8,128)S(1)}, f32[16,4,548]{2,1,0:T(4,128)S(1)}, f32[16,4,548]{2,1,0:T(4,128)S(1)}) custom-call(s32[2]{0:T(128)S(1)} %pad_add_fusion.side_ref, f32[512,768]{1,0:T(8,128)S(1)} %copy-done.4, bf16[512,512]{1,0:T(8,128)(2,1)S(1)} %get-tuple-element.53.one_ref, ...), custom_call_target="tpu_custom_call" | custom-call | flops 10871635968 | bytes 11796480 | tf_op jit(solution)/shard_map/pallas_call | solution.py:575
  129.9 1.5 collective-permute-start.8
  131.4 2.9 %collective-permute-start.9 = (f32[4,32,548]{2,1,0:T(8,128)S(1)}, f32[4,32,548]{2,1,0:T(8,128)S(1)}, u32[]{:S(2)}, u32[]{:S(2)}) collective-permute-start(f32[4,32,548]{2,1,0:T(8,128)S(1)} %get-tuple-element.58), channel_id=1, source_target_pairs={{4,8},{12,16},{20,24},{8,4},{16,12},{24,20},{5,9},{13,17},{21,25},... | collective-permute-start | bytes 841736 | tf_op jit(solution)/shard_map/ppermute | solution.py:428
  135.1 3.9 %collective-permute-start.15 = (f32[24,4,548]{2,1,0:T(4,128)S(1)}, f32[24,4,548]{2,1,0:T(4,128)S(1)}, u32[]{:S(2)}, u32[]{:S(2)}) collective-permute-start(f32[24,4,548]{2,1,0:T(4,128)S(1)} %get-tuple-element.70), channel_id=1, source_target_pairs={{1,2},{2,1},{5,6},{6,5},{9,10},{10,9},{13,14},{14,13},{17,18},{18,... | collective-permute-start | bytes 631304 | tf_op jit(solution)/shard_map/ppermute | solution.py:428
  139.0 6.8 %collective-permute-done.8.ra.refs_0_ = f32[4,32,548]{2,1,0:T(8,128)S(1)} collective-permute-done((f32[4,32,548]{2,1,0:T(8,128)S(1)}, f32[4,32,548]{2,1,0:T(8,128)S(1)}, u32[]{:S(2)}, u32[]{:S(2)}) %collective-permute-start.8) | collective-permute-done | bytes 280608 | tf_op jit(solution)/shard_map/ppermute | solution.py:428
  146.6 1.9 %collective-permute-start.11 = (f32[24,4,548]{2,1,0:T(4,128)S(1)}, f32[24,4,548]{2,1,0:T(4,128)S(1)}, u32[]{:S(2)}, u32[]{:S(2)}) collective-permute-start(f32[24,4,548]{2,1,0:T(4,128)S(1)} %get-tuple-element.62), channel_id=1, source_target_pairs={{1,2},{2,1},{5,6},{6,5},{9,10},{10,9},{13,14},{14,13},{17,18},{18,... | collective-permute-start | bytes 631304 | tf_op jit(solution)/shard_map/ppermute | solution.py:428
  148.5 5.0 %shard_map.140.refs_4_ = f32[2,16,32,548]{3,2,1,0:T(8,128)} custom-call(s32[2]{0:T(128)S(1)} %pad_add_fusion.side_ref, f32[16,32,548]{2,1,0:T(8,128)S(1)} %get-tuple-element.64.field_ref, f32[2,16,32,548]{3,2,1,0:T(8,128)S(1)} %copy-done, f32[2,24,40,128]{3,2,1,0:T(8,128)S(1)} %copy-done.2, f32[4,32,548]{2,1,0:T(8,128)S(1)} %collective-permute-done.12.ra.refs_0_, ...), custom_call_target="tpu_custom_call" | custom-call | flops 24576000 | bytes 3932160 | tf_op jit(solution)/shard_map/pallas_call | solution.py:598
  154.1 5.0 %shard_map.141 = f32[2,16,32,548]{3,2,1,0:T(8,128)} custom-call(s32[2]{0:T(128)S(1)} %pad_add_fusion.side_ref, f32[16,32,548]{2,1,0:T(8,128)S(1)} %get-tuple-element.56.field_ref, f32[2,16,32,548]{3,2,1,0:T(8,128)S(1)} %copy-done, f32[2,24,40,128]{3,2,1,0:T(8,128)S(1)} %copy-done.2, ...), custom_call_target="tpu_custom_call", output_to_operand_aliasing={{}: (8, {})} | custom-call | flops 24576000 | bytes 3932160 | tf_op jit(solution)/shard_map/pallas_call | solution.py:598
  (45 shorter events, 3.5 us)
Async XLA Ops:
  1.4 1.3 copy-start.8
  4.9 6.5 %copy-start.5 = (f32[16,32]{1,0:T(8,128)S(1)}, f32[16,32]{1,0:T(8,128)}, u32[]{:S(2)}) copy-start(f32[16,32]{1,0:T(8,128)} %coeff_ref.5) | copy-start | bytes 6148
  4.9 81.9 %all-to-all-start = ((f32[32,16,640]{2,1,0:T(8,128)}), f32[32,16,640]{2,1,0:T(8,128)}, u32[]{:S(2)}, u32[]{:S(2)}) async-start(f32[32,16,640]{2,1,0:T(8,128)} %bitcast.7), calls=%async_computation | async-start | bytes 2621440 | tf_op jit(solution)/shard_map/all_to_all | solution.py:503
  13.3 46.7 %collective-permute-start = (f32[4,32,549]{2,1,0:T(8,128)S(1)}, f32[4,32,549]{2,1,0:T(8,128)S(1)}, u32[]{:S(2)}, u32[]{:S(2)}) collective-permute-start(f32[4,32,549]{2,1,0:T(8,128)S(1)} %get-tuple-element.38), channel_id=1, source_target_pairs={{0,4},{8,12},{16,20},{24,28},{4,0},{12,8},{20,16},{28,24},{1,5},{9... | collective-permute-start | bytes 843272 | tf_op jit(solution)/shard_map/ppermute | solution.py:428
  14.5 45.4 %collective-permute-start.1 = (f32[4,32,549]{2,1,0:T(8,128)S(1)}, f32[4,32,549]{2,1,0:T(8,128)S(1)}, u32[]{:S(2)}, u32[]{:S(2)}) collective-permute-start(f32[4,32,549]{2,1,0:T(8,128)S(1)} %get-tuple-element.39), channel_id=1, source_target_pairs={{4,8},{12,16},{20,24},{8,4},{16,12},{24,20},{5,9},{13,17},{21,25},... | collective-permute-start | bytes 843272 | tf_op jit(solution)/shard_map/ppermute | solution.py:428
  18.5 36.8 %collective-permute-start.4 = (f32[4,32,548]{2,1,0:T(8,128)S(1)}, f32[4,32,548]{2,1,0:T(8,128)S(1)}, u32[]{:S(2)}, u32[]{:S(2)}) collective-permute-start(f32[4,32,548]{2,1,0:T(8,128)S(1)} %get-tuple-element.46), channel_id=1, source_target_pairs={{0,4},{8,12},{16,20},{24,28},{4,0},{12,8},{20,16},{28,24},{1,5},{9... | collective-permute-start | bytes 841736 | tf_op jit(solution)/shard_map/ppermute | solution.py:428
  20.8 34.5 %collective-permute-start.5 = (f32[4,32,548]{2,1,0:T(8,128)S(1)}, f32[4,32,548]{2,1,0:T(8,128)S(1)}, u32[]{:S(2)}, u32[]{:S(2)}) collective-permute-start(f32[4,32,548]{2,1,0:T(8,128)S(1)} %get-tuple-element.47), channel_id=1, source_target_pairs={{4,8},{12,16},{20,24},{8,4},{16,12},{24,20},{5,9},{13,17},{21,25},... | collective-permute-start | bytes 841736 | tf_op jit(solution)/shard_map/ppermute | solution.py:428
  55.9 23.0 %collective-permute-start.6 = (f32[24,4,548]{2,1,0:T(4,128)S(1)}, f32[24,4,548]{2,1,0:T(4,128)S(1)}, u32[]{:S(2)}, u32[]{:S(2)}) collective-permute-start(f32[24,4,548]{2,1,0:T(4,128)S(1)} %get-tuple-element.50), channel_id=1, source_target_pairs={{0,1},{2,3},{1,0},{3,2},{4,5},{6,7},{5,4},{7,6},{8,9},{10,11},{9,8... | collective-permute-start | bytes 631304 | tf_op jit(solution)/shard_map/ppermute | solution.py:428
  57.0 22.0 %collective-permute-start.7 = (f32[24,4,548]{2,1,0:T(4,128)S(1)}, f32[24,4,548]{2,1,0:T(4,128)S(1)}, u32[]{:S(2)}, u32[]{:S(2)}) collective-permute-start(f32[24,4,548]{2,1,0:T(4,128)S(1)} %get-tuple-element.51), channel_id=1, source_target_pairs={{1,2},{2,1},{5,6},{6,5},{9,10},{10,9},{13,14},{14,13},{17,18},{18,... | collective-permute-start | bytes 631304 | tf_op jit(solution)/shard_map/ppermute | solution.py:428
  60.6 11.0 %collective-permute-start.2 = (f32[24,4,549]{2,1,0:T(4,128)S(1)}, f32[24,4,549]{2,1,0:T(4,128)S(1)}, u32[]{:S(2)}, u32[]{:S(2)}) collective-permute-start(f32[24,4,549]{2,1,0:T(4,128)S(1)} %get-tuple-element.42), channel_id=1, source_target_pairs={{0,1},{2,3},{1,0},{3,2},{4,5},{6,7},{5,4},{7,6},{8,9},{10,11},{9,8... | collective-permute-start | bytes 632456 | tf_op jit(solution)/shard_map/ppermute | solution.py:428
  60.7 11.0 %collective-permute-start.3 = (f32[24,4,549]{2,1,0:T(4,128)S(1)}, f32[24,4,549]{2,1,0:T(4,128)S(1)}, u32[]{:S(2)}, u32[]{:S(2)}) collective-permute-start(f32[24,4,549]{2,1,0:T(4,128)S(1)} %get-tuple-element.43), channel_id=1, source_target_pairs={{1,2},{2,1},{5,6},{6,5},{9,10},{10,9},{13,14},{14,13},{17,18},{18,... | collective-permute-start | bytes 632456 | tf_op jit(solution)/shard_map/ppermute | solution.py:428
  63.3 8.3 %copy-start.10 = (f32[768]{0:T(1024)S(1)}, f32[768]{0:T(1024)}, u32[]{:S(2)}) copy-start(f32[768]{0:T(1024)} %param.17) | copy-start | bytes 9220
  63.3 8.3 %copy-start.11 = (f32[768]{0:T(1024)S(1)}, f32[768]{0:T(1024)}, u32[]{:S(2)}) copy-start(f32[768]{0:T(1024)} %param.19) | copy-start | bytes 9220
  63.3 8.4 %copy-start = (f32[2,16,32,548]{3,2,1,0:T(8,128)S(1)}, f32[2,16,32,548]{3,2,1,0:T(8,128)}, u32[]{:S(2)}) copy-start(f32[2,16,32,548]{3,2,1,0:T(8,128)} %base_ref.3) | copy-start | bytes 6733828
  77.8 1.1 copy-start.6
  78.9 7.8 %copy-start.9 = (s32[32,616]{1,0:T(8,128)S(1)}, s32[32,616]{1,0:T(8,128)}, u32[]{:S(2)}) copy-start(s32[32,616]{1,0:T(8,128)} %mask_ref.1) | copy-start | bytes 236548
  84.6 1.0 copy-start.1
  85.6 1.2 copy-start.3
  86.8 6.3 %copy-start.7 = (f32[512,768]{1,0:T(8,128)S(1)}, f32[512,768]{1,0:T(8,128)}, u32[]{:S(2)}) copy-start(f32[512,768]{1,0:T(8,128)} %copy-done.6) | copy-start | bytes 4718596
  93.1 20.1 %copy-start.4 = (f32[512,768]{1,0:T(8,128)S(1)}, f32[512,768]{1,0:T(8,128)}, u32[]{:S(2)}) copy-start(f32[512,768]{1,0:T(8,128)} %copy-done.3) | copy-start | bytes 4718596
  110.0 24.4 %collective-permute-start.12 = (f32[4,32,548]{2,1,0:T(8,128)S(1)}, f32[4,32,548]{2,1,0:T(8,128)S(1)}, u32[]{:S(2)}, u32[]{:S(2)}) collective-permute-start(f32[4,32,548]{2,1,0:T(8,128)S(1)} %get-tuple-element.65), channel_id=1, source_target_pairs={{0,4},{8,12},{16,20},{24,28},{4,0},{12,8},{20,16},{28,24},{1,5},{9... | collective-permute-start | bytes 841736 | tf_op jit(solution)/shard_map/ppermute | solution.py:428
  111.3 23.1 %collective-permute-start.13 = (f32[4,32,548]{2,1,0:T(8,128)S(1)}, f32[4,32,548]{2,1,0:T(8,128)S(1)}, u32[]{:S(2)}, u32[]{:S(2)}) collective-permute-start(f32[4,32,548]{2,1,0:T(8,128)S(1)} %get-tuple-element.66), channel_id=1, source_target_pairs={{4,8},{12,16},{20,24},{8,4},{16,12},{24,20},{5,9},{13,17},{21,25},... | collective-permute-start | bytes 841736 | tf_op jit(solution)/shard_map/ppermute | solution.py:428
  129.9 18.7 %copy-start.2 = (f32[2,24,40,128]{3,2,1,0:T(8,128)S(1)}, f32[2,24,40,128]{3,2,1,0:T(8,128)}, u32[]{:S(2)}) copy-start(f32[2,24,40,128]{3,2,1,0:T(8,128)} %copy-done.1) | copy-start | bytes 2949124
  129.9 15.9 %collective-permute-start.8 = (f32[4,32,548]{2,1,0:T(8,128)S(1)}, f32[4,32,548]{2,1,0:T(8,128)S(1)}, u32[]{:S(2)}, u32[]{:S(2)}) collective-permute-start(f32[4,32,548]{2,1,0:T(8,128)S(1)} %get-tuple-element.57), channel_id=1, source_target_pairs={{0,4},{8,12},{16,20},{24,28},{4,0},{12,8},{20,16},{28,24},{1,5},{9... | collective-permute-start | bytes 841736 | tf_op jit(solution)/shard_map/ppermute | solution.py:428
  131.4 14.4 %collective-permute-start.9 = (f32[4,32,548]{2,1,0:T(8,128)S(1)}, f32[4,32,548]{2,1,0:T(8,128)S(1)}, u32[]{:S(2)}, u32[]{:S(2)}) collective-permute-start(f32[4,32,548]{2,1,0:T(8,128)S(1)} %get-tuple-element.58), channel_id=1, source_target_pairs={{4,8},{12,16},{20,24},{8,4},{16,12},{24,20},{5,9},{13,17},{21,25},... | collective-permute-start | bytes 841736 | tf_op jit(solution)/shard_map/ppermute | solution.py:428
  135.0 13.5 %collective-permute-start.14 = (f32[24,4,548]{2,1,0:T(4,128)S(1)}, f32[24,4,548]{2,1,0:T(4,128)S(1)}, u32[]{:S(2)}, u32[]{:S(2)}) collective-permute-start(f32[24,4,548]{2,1,0:T(4,128)S(1)} %get-tuple-element.69), channel_id=1, source_target_pairs={{0,1},{2,3},{1,0},{3,2},{4,5},{6,7},{5,4},{7,6},{8,9},{10,11},{9,8... | collective-permute-start | bytes 631304 | tf_op jit(solution)/shard_map/ppermute | solution.py:428
  135.1 13.4 %collective-permute-start.15 = (f32[24,4,548]{2,1,0:T(4,128)S(1)}, f32[24,4,548]{2,1,0:T(4,128)S(1)}, u32[]{:S(2)}, u32[]{:S(2)}) collective-permute-start(f32[24,4,548]{2,1,0:T(4,128)S(1)} %get-tuple-element.70), channel_id=1, source_target_pairs={{1,2},{2,1},{5,6},{6,5},{9,10},{10,9},{13,14},{14,13},{17,18},{18,... | collective-permute-start | bytes 631304 | tf_op jit(solution)/shard_map/ppermute | solution.py:428
  146.4 7.1 %collective-permute-start.10 = (f32[24,4,548]{2,1,0:T(4,128)S(1)}, f32[24,4,548]{2,1,0:T(4,128)S(1)}, u32[]{:S(2)}, u32[]{:S(2)}) collective-permute-start(f32[24,4,548]{2,1,0:T(4,128)S(1)} %get-tuple-element.61), channel_id=1, source_target_pairs={{0,1},{2,3},{1,0},{3,2},{4,5},{6,7},{5,4},{7,6},{8,9},{10,11},{9,8... | collective-permute-start | bytes 631304 | tf_op jit(solution)/shard_map/ppermute | solution.py:428
  146.6 7.5 %collective-permute-start.11 = (f32[24,4,548]{2,1,0:T(4,128)S(1)}, f32[24,4,548]{2,1,0:T(4,128)S(1)}, u32[]{:S(2)}, u32[]{:S(2)}) collective-permute-start(f32[24,4,548]{2,1,0:T(4,128)S(1)} %get-tuple-element.62), channel_id=1, source_target_pairs={{1,2},{2,1},{5,6},{6,5},{9,10},{10,9},{13,14},{14,13},{17,18},{18,... | collective-permute-start | bytes 631304 | tf_op jit(solution)/shard_map/ppermute | solution.py:428

commit v4 on v3

--- a/solution.py
+++ b/solution.py
@@ -78,7 +78,19 @@
     high, low = split(tall)
     high_ref[mark : mark + 16, :] = high
     low_ref[mark : mark + 16, :] = low
-    out_ref[...] = mm(pick, high_ref[...], NT) + mm(pick, low_ref[...], NT)
+    rows = mm(pick, high_ref[...], NT) + mm(pick, low_ref[...], NT)
+    if out_ref.shape == rows.shape:
+        out_ref[...] = rows
+        return
+    whole = rows.shape[1] // LANES - 1
+    for k in range(whole):
+        piece = rows[:, k * LANES : (k + 1) * LANES].reshape(devices, bucket, LANES)
+        out_ref[:, k * bucket : (k + 1) * bucket, :] = piece
+    tail = rows[:, whole * LANES :].reshape(devices, bucket, LANES)
+    half = bucket // 2
+    left = iota((devices, half, LANES), 2) < LANES // 2
+    turned = pltpu.roll(tail[:, half:], LANES // 2, 2)
+    out_ref[:, whole * bucket :, :] = jnp.where(left, tail[:, :half], turned)
 
 
 def prep_kernel(*refs):
@@ -201,7 +213,7 @@
     fill(ext, side_ref, tile, *strips, part)
 
 
-def diffuse_kernel(given, side_ref, tile_ref, coeff_ref, *refs):
+def diffuse_kernel(v, side_ref, tile_ref, coeff_ref, *refs):
     strips, stack_ref, refs = refs[:4], refs[4], refs[5:]
     ext, work, high_ref, low_ref, both, sem = refs[-6:]
     out_ref = refs[0]
@@ -211,8 +223,8 @@
     rows, wide, levels = tile_ref.shape[1:]
     tall = rows + 2 * w
     around = wide + 2 * w
-    fill_levels(ext, side_ref, tile_ref[0], *strips)
-    if given:
+    fill_levels(ext, side_ref, tile_ref[v], *strips)
+    if v > 0:
         cb_ref = coeff_ref
     else:
         cb_ref = refs[1]
@@ -266,12 +278,23 @@
     fetch_first.start()
     fetch_second.start()
     s1_ref, s2_ref, gate_ref = (scale_ref.at[k] for k in range(3))
-    slots, deep = x_ref.shape
-    cells = one_ref.shape[1]
+    slots, cells = one_ref.shape
     devices, channels = mask_ref.shape
     fetch_x.wait()
-    x_ref = x_buf
-    index = x_ref[:, mark : mark + 1]
+    if len(x_buf.shape) == 2:
+        deep = x_buf.shape[1]
+        pieces = [x_buf[:, k : k + LANES] for k in range(0, deep, LANES)]
+    else:
+        whole = x_buf.shape[1] // bucket
+        deep = (whole + 1) * LANES
+        pieces = [
+            x_buf[:, k * bucket : (k + 1) * bucket, :].reshape(slots, LANES)
+            for k in range(whole)
+        ]
+        tail = x_buf[:, whole * bucket :, :]
+        tail = jnp.concatenate([tail, pltpu.roll(tail, LANES // 2, 2)], axis=1)
+        pieces.append(tail.reshape(slots, LANES))
+    index = pieces[-1][:, mark % LANES : mark % LANES + 1]
     cell = index.astype(jnp.int32) - 1
     live = index > 0.5
     one_ref[...] = (iota((slots, cells), 1) == cell).astype(BF)
@@ -282,9 +305,9 @@
     from_owner = ((at >= begin) & (at < begin + bucket) & live).astype(BF)
     gate_ref[...] = jnp.zeros_like(gate_ref)
     gate_ref[:, :channels] = mm(from_owner, mask_ref[...].astype(F32).astype(BF))
-    high, low = split(x_ref[...])
-    high_ref[:, :deep] = high
-    low_ref[:, :deep] = low
+    for k, piece in enumerate(pieces):
+        here = pl.ds(k * LANES, LANES)
+        high_ref[:, here], low_ref[:, here] = split(piece)
     parts = halves(slots)
     fetch_first.wait()
     for part in parts:
@@ -386,8 +409,8 @@
     xb[...] = jnp.where(even, head, tail)
 
 
-def finish_kernel(side_ref, field_ref, base_ref, cb_ref, *refs):
-    out_ref, ext, work, total = refs[-4:]
+def finish_kernel(v, side_ref, field_ref, base_ref, cb_ref, *refs):
+    out_ref, ext, work, total, result, sems = refs[-6:]
     w = SWEEPS
     rows, wide, levels = field_ref.shape
     tall = rows + 2 * w
@@ -420,7 +443,14 @@
         return 0
 
     lax.fori_loop(0, ext.shape[2] // LANES, chunk, 0)
-    out_ref[0] = base_ref[0] + total[:, :, :levels]
+    sends = []
+    for k in range(2):
+        part = pl.ds(k * (rows // 2), rows // 2)
+        result[part] = base_ref[v, part] + total[part, :, :levels]
+        sends.append(pltpu.make_async_copy(result.at[part], out_ref.at[v, part], sems.at[k]))
+        sends[-1].start()
+    for copy in sends:
+        copy.wait()
 
 
 def swap(value, axis, start):
@@ -492,18 +522,22 @@
     target = grid_row // tile_x * count_y + grid_col // tile_y
     dest = jnp.where(position < owner_count[0], target, -1)
     cell = (grid_row % tile_x * tile_y + grid_col % tile_y + 1).astype(F32)
+    tight = bucket % 16 == 0 and mark // LANES == deep // LANES - 1 and mark % LANES < LANES // 2
+    packed_shape = (slots, deep)
+    if tight:
+        packed_shape = (devices, bucket * (deep // LANES - 1) + bucket // 2, LANES)
     packed = call(
         functools.partial(pack_kernel, bucket),
-        shaped((slots, deep)),
+        shaped(packed_shape),
         flops=6 * slots * slots * deep,
         moved=8 * slots * deep,
         scratch=[pltpu.VMEM((deep, slots), BF)] * 2,
         vmem=12,
     )(dest[None, :], cell[None, :], observed_state.T)
     carried = lax.all_to_all(
-        packed.reshape(devices, bucket, deep), ("gx", "gy"), split_axis=0,
-        concat_axis=0, tiled=True,
-    ).reshape(slots, deep)
+        packed if tight else packed.reshape(devices, bucket, deep), ("gx", "gy"),
+        split_axis=0, concat_axis=0, tiled=True,
+    ).reshape(packed_shape)
 
     side = max(full_l, full_u, full_c)
     weights = (vertical_factor, weight_first, weight_second, weight_out.T, error_inverse)
@@ -527,13 +561,10 @@
     def wide_bias(bias):
         return jnp.pad(bias, (0, side - bias.shape[0]))[None, :]
 
-    def block(v):
-        return pl.BlockSpec((1, tile_x, tile_y, levels), lambda i: (v, 0, 0, 0))
-
     queries = []
     for v in range(pairs):
         got = call(
-            functools.partial(diffuse_kernel, v > 0),
+            functools.partial(diffuse_kernel, v),
             [shaped((cells, side))] + [shaped((2, tall, around, LANES))] * (v == 0),
             flops=6 * cells * deep * full_u,
             moved=8 * tall * around * deep,
@@ -545,9 +576,8 @@
                 pltpu.VMEM((2, side, side), BF),
                 pltpu.SemaphoreType.DMA,
             ],
-            grid=(1,),
-            vmem=14,
-            in_specs=[scalars, block(v)] + [whole] * 5 + [far],
+            vmem=16,
+            in_specs=[scalars, whole] + [whole] * 5 + [far],
             out_specs=[whole] * (2 - (v > 0)),
         )(sides, vectors, spread if v else diffusivity, *strips[v], stack)
         queries.append(got[0])
@@ -561,7 +591,7 @@
         moved=8 * slots * full_u,
         scratch=[pltpu.VMEM((slots, side), BF)] * 2
         + [
-            pltpu.VMEM((slots, deep), F32),
+            pltpu.VMEM(packed_shape, F32),
             pltpu.VMEM((2, full_l, side), BF), pltpu.VMEM((2, side, side), BF),
             pltpu.SemaphoreType.DMA((3,)),
         ],
@@ -596,20 +626,20 @@
         around_field = halo(sides, *fields[v][1:])
         carry = [] if out is None else [out]
         out = call(
-            finish_kernel,
-            shaped(vectors.shape),
+            functools.partial(finish_kernel, v),
+            pltpu.HBM(vectors.shape, F32),
             flops=40 * tall * around * deep,
             moved=12 * cells * deep,
             scratch=[
                 pltpu.VMEM((tall, around, deep), F32),
                 pltpu.VMEM((2, tall, around, LANES), F32),
                 pltpu.VMEM((tile_x, tile_y, deep), F32),
+                pltpu.VMEM((tile_x, tile_y, levels), F32),
+                pltpu.SemaphoreType.DMA((2,)),
             ],
-            grid=(1,),
-            vmem=14,
-            in_specs=[scalars, whole, block(v)] + [whole] * 5
-            + [pl.BlockSpec(memory_space=pl.ANY)] * len(carry),
-            out_specs=block(v),
+            vmem=16,
+            in_specs=[scalars] + [whole] * 7 + [far] * len(carry),
+            out_specs=far,
             input_output_aliases={8: 0} if carry else {},
         )(sides, fields[v][0], vectors, spread, *around_field, *carry)
     return out

time: 161 us -> 159 us (0.988)
  no operation moved by 1% of the time
where the time goes in v4:
time: 159 us; the launch traced here: 158 us
  Pallas kernels  78.4 us (49%)
  waiting for transfers between devices  39.4 us (25%)
  starting transfers between devices  33.3 us (21%)
  local copies, waits for them, and re-layouts  4.59 us (3%)
    ppermute x16, waiting for transfers between devices, swap(): return lax.ppermute(value, axis, pairs + [(j, i) for i, j in pairs])  39.4 us
    pallas_call x2, Pallas kernels, body(): call(net_kernel, [shaped((tile_x, tile_y, levels))] + [shaped((SWEEPS, ti...  33.6 us
    ppermute x16, starting transfers between devices, swap(): return lax.ppermute(value, axis, pairs + [(j, i) for i, j in pairs])  26.9 us
    pallas_call x2, Pallas kernels, body(): call(functools.partial(diffuse_kernel, v), [shaped((cells, side))] + [sha...  11.8 us
    pallas_call x2, Pallas kernels, body(): call(functools.partial(finish_kernel, v), pltpu.HBM(vectors.shape, F32),...  9.89 us
    pallas_call x1, Pallas kernels, body(): call(prep_kernel, [pltpu.HBM((2, full_l, side), BF), pltpu.HBM((4, 2, sid...  8.29 us
    all_to_all x1, starting transfers between devices, body(): lax.all_to_all(packed if tight else packed.reshape(devices, bucket, deep)...  6.38 us
    pallas_call x1, Pallas kernels, body(): call(functools.partial(hidden_kernel, mark, bucket), [shaped((3, slots, s...  6.2 us
  transfers between devices with their start and end apart: 17, of which 3 were waited for; matrix products, arithmetic and copies ran while one was open for 0% of the time, Pallas kernels for 30%

profile of v4, /device:TPU:9, one launch (start us, length us, event | category | flops | bytes accessed | tf_op | source)
XLA Modules:
  0.0 157.6 jit_solution(1200273736071585579)
XLA Ops:
  0.7 0.7 fusion.6
  1.4 1.2 copy-done.8
  2.6 2.3 %shard_map.134 = f32[32,72,128]{2,1,0:T(8,128)} custom-call(s32[1,512]{1,0:T(1,128)S(1)} %bitcast.9, f32[1,512]{1,0:T(1,128)S(1)} %bitcast.8, f32[548,512]{1,0:T(8,128)S(1)} %bitcast.10), custom_call_target="tpu_custom_call" | custom-call | flops 1006632960 | bytes 2621440 | tf_op jit(solution)/shard_map/pallas_call | solution.py:529
  4.9 6.4 %all-to-all-start = ((f32[32,72,128]{2,1,0:T(8,128)}), f32[32,72,128]{2,1,0:T(8,128)}, u32[]{:S(2)}, u32[]{:S(2)}) async-start(f32[32,72,128]{2,1,0:T(8,128)} %shard_map.134), calls=%async_computation | async-start | bytes 2359296 | tf_op jit(solution)/shard_map/all_to_all | solution.py:537
  11.4 1.9 %shard_map.127 = (f32[4,32,549]{2,1,0:T(8,128)S(1)}, f32[4,32,549]{2,1,0:T(8,128)S(1)}, f32[16,4,549]{2,1,0:T(4,128)S(1)}, f32[16,4,549]{2,1,0:T(4,128)S(1)}) custom-call(s32[2]{0:T(128)S(1)} %pad_add_fusion.side_ref, f32[2,16,32,548]{3,2,1,0:T(8,128)} %base_ref.3, f32[16,32]{1,0:T(8,128)S(1)} %copy-done.5), custom_call_target="tpu_custom_call" | custom-call | bytes 2244608 | tf_op jit(solution)/shard_map/pallas_call | solution.py:506
  13.3 1.2 collective-permute-start
  14.6 2.0 %collective-permute-start.1 = (f32[4,32,549]{2,1,0:T(8,128)S(1)}, f32[4,32,549]{2,1,0:T(8,128)S(1)}, u32[]{:S(2)}, u32[]{:S(2)}) collective-permute-start(f32[4,32,549]{2,1,0:T(8,128)S(1)} %get-tuple-element.39), channel_id=1, source_target_pairs={{4,8},{12,16},{20,24},{8,4},{16,12},{24,20},{5,9},{13,17},{21,25},... | collective-permute-start | bytes 843272 | tf_op jit(solution)/shard_map/ppermute | solution.py:458
  16.6 1.9 %shard_map.131 = (f32[4,32,548]{2,1,0:T(8,128)S(1)}, f32[4,32,548]{2,1,0:T(8,128)S(1)}, f32[16,4,548]{2,1,0:T(4,128)S(1)}, f32[16,4,548]{2,1,0:T(4,128)S(1)}) custom-call(s32[2]{0:T(128)S(1)} %pad_add_fusion.side_ref, f32[2,16,32,548]{3,2,1,0:T(8,128)} %base_ref.3, f32[16,32]{1,0:T(8,128)S(1)} %copy-done.5), custom_call_target="tpu_custom_call" | custom-call | bytes 2244608 | tf_op jit(solution)/shard_map/pallas_call | solution.py:506
  18.5 2.3 %collective-permute-start.4 = (f32[4,32,548]{2,1,0:T(8,128)S(1)}, f32[4,32,548]{2,1,0:T(8,128)S(1)}, u32[]{:S(2)}, u32[]{:S(2)}) collective-permute-start(f32[4,32,548]{2,1,0:T(8,128)S(1)} %get-tuple-element.46), channel_id=1, source_target_pairs={{0,4},{8,12},{16,20},{24,28},{4,0},{12,8},{20,16},{28,24},{1,5},{9... | collective-permute-start | bytes 841736 | tf_op jit(solution)/shard_map/ppermute | solution.py:458
  20.8 1.9 %collective-permute-start.5 = (f32[4,32,548]{2,1,0:T(8,128)S(1)}, f32[4,32,548]{2,1,0:T(8,128)S(1)}, u32[]{:S(2)}, u32[]{:S(2)}) collective-permute-start(f32[4,32,548]{2,1,0:T(8,128)S(1)} %get-tuple-element.47), channel_id=1, source_target_pairs={{4,8},{12,16},{20,24},{8,4},{16,12},{24,20},{5,9},{13,17},{21,25},... | collective-permute-start | bytes 841736 | tf_op jit(solution)/shard_map/ppermute | solution.py:458
  22.8 31.1 %collective-permute-done.4.ra.refs_0_ = f32[4,32,548]{2,1,0:T(8,128)S(1)} collective-permute-done((f32[4,32,548]{2,1,0:T(8,128)S(1)}, f32[4,32,548]{2,1,0:T(8,128)S(1)}, u32[]{:S(2)}, u32[]{:S(2)}) %collective-permute-start.4) | collective-permute-done | bytes 280608 | tf_op jit(solution)/shard_map/ppermute | solution.py:458
  54.5 1.0 collective-permute-start.6
  55.6 3.0 %collective-permute-start.7 = (f32[24,4,548]{2,1,0:T(4,128)S(1)}, f32[24,4,548]{2,1,0:T(4,128)S(1)}, u32[]{:S(2)}, u32[]{:S(2)}) collective-permute-start(f32[24,4,548]{2,1,0:T(4,128)S(1)} %get-tuple-element.51), channel_id=1, source_target_pairs={{1,2},{2,1},{5,6},{6,5},{9,10},{10,9},{13,14},{14,13},{17,18},{18,... | collective-permute-start | bytes 631304 | tf_op jit(solution)/shard_map/ppermute | solution.py:458
  59.3 2.6 %collective-permute-start.3 = (f32[24,4,549]{2,1,0:T(4,128)S(1)}, f32[24,4,549]{2,1,0:T(4,128)S(1)}, u32[]{:S(2)}, u32[]{:S(2)}) collective-permute-start(f32[24,4,549]{2,1,0:T(4,128)S(1)} %get-tuple-element.43), channel_id=1, source_target_pairs={{1,2},{2,1},{5,6},{6,5},{9,10},{10,9},{13,14},{14,13},{17,18},{18,... | collective-permute-start | bytes 632456 | tf_op jit(solution)/shard_map/ppermute | solution.py:458
  61.9 8.3 %shard_map.129 = (bf16[2,768,768]{2,1,0:T(8,128)(2,1)}, bf16[4,2,768,768]{3,2,1,0:T(8,128)(2,1)}) custom-call(f32[548,548]{1,0:T(8,128)} %refs_0_.1, f32[548,768]{1,0:T(8,128)} %refs_1_.1, f32[768,768]{1,0:T(8,128)} %refs_2_.1, f32[616,768]{1,0:T(8,128)} %bitcast.11, f32[616,616]{1,0:T(8,128)} %refs_4_.1), custom_call_target="tpu_custom_call" | custom-call | flops 2717908992 | bytes 23592960 | tf_op jit(solution)/shard_map/pallas_call | solution.py:544
  70.3 6.1 %shard_map.130 = (f32[512,768]{1,0:T(8,128)S(1)}, f32[2,24,40,128]{3,2,1,0:T(8,128)S(1)}) custom-call(s32[2]{0:T(128)S(1)} %pad_add_fusion.side_ref, f32[2,16,32,548]{3,2,1,0:T(8,128)S(1)} %copy-done, f32[16,32]{1,0:T(8,128)S(1)} %copy-done.5, f32[4,32,549]{2,1,0:T(8,128)S(1)} %collective-permute-done.ra.refs_0_, ...), custom_call_target="tpu_custom_call" | custom-call | flops 1509949440 | bytes 4915200 | tf_op jit(solution)/shard_map/pallas_call | solution.py:566
  76.4 1.1 copy-done.6
  77.6 5.6 %shard_map.133.q_ref = f32[512,768]{1,0:T(8,128)S(1)} custom-call(s32[2]{0:T(128)S(1)} %pad_add_fusion.side_ref, f32[2,16,32,548]{3,2,1,0:T(8,128)S(1)} %copy-done, f32[2,24,40,128]{3,2,1,0:T(8,128)S(1)} %get-tuple-element.45.coeff_ref.cb_ref, f32[4,32,548]{2,1,0:T(8,128)S(1)} %collective-permute-done.4.ra.refs_0_, ...), custom_call_target="tpu_custom_call" | custom-call | flops 1509949440 | bytes 4915200 | tf_op jit(solution)/shard_map/pallas_call | solution.py:566
  83.2 1.0 copy-done.1
  84.2 1.2 copy-done.3
  85.4 6.2 %shard_map.135 = (f32[3,512,768]{2,1,0:T(8,128)S(1)}, bf16[512,512]{1,0:T(8,128)(2,1)S(1)}, bf16[512,512]{1,0:T(8,128)(2,1)S(1)}) custom-call(f32[32,72,128]{2,1,0:T(8,128)} %all-to-all-done.x_ref, bf16[2,768,768]{2,1,0:T(8,128)(2,1)} %get-tuple-element.52.first_ref, f32[1,768]{1,0:T(1,128)S(1)} %broadcast_in_dim.16.b1_ref, ...), custom_call_target="tpu_custom_call" | custom-call | flops 3623878656 | bytes 3145728 | tf_op jit(solution)/shard_map/pallas_call | solution.py:587
  91.6 16.9 %shard_map.138 = (f32[16,32,548]{2,1,0:T(8,128)S(1)}, f32[4,32,548]{2,1,0:T(8,128)S(1)}, f32[4,32,548]{2,1,0:T(8,128)S(1)}, f32[16,4,548]{2,1,0:T(4,128)S(1)}, f32[16,4,548]{2,1,0:T(4,128)S(1)}) custom-call(s32[2]{0:T(128)S(1)} %pad_add_fusion.side_ref, f32[512,768]{1,0:T(8,128)S(1)} %copy-done.7, bf16[512,512]{1,0:T(8,128)(2,1)S(1)} %get-tuple-element.53.one_ref, ...), custom_call_target="tpu_custom_call" | custom-call | flops 10871635968 | bytes 11796480 | tf_op jit(solution)/shard_map/pallas_call | solution.py:605
  108.9 1.9 %collective-permute-start.13 = (f32[4,32,548]{2,1,0:T(8,128)S(1)}, f32[4,32,548]{2,1,0:T(8,128)S(1)}, u32[]{:S(2)}, u32[]{:S(2)}) collective-permute-start(f32[4,32,548]{2,1,0:T(8,128)S(1)} %get-tuple-element.66), channel_id=1, source_target_pairs={{4,8},{12,16},{20,24},{8,4},{16,12},{24,20},{5,9},{13,17},{21,25},... | collective-permute-start | bytes 841736 | tf_op jit(solution)/shard_map/ppermute | solution.py:458
  110.8 16.7 %shard_map.136 = (f32[16,32,548]{2,1,0:T(8,128)S(1)}, f32[4,32,548]{2,1,0:T(8,128)S(1)}, f32[4,32,548]{2,1,0:T(8,128)S(1)}, f32[16,4,548]{2,1,0:T(4,128)S(1)}, f32[16,4,548]{2,1,0:T(4,128)S(1)}) custom-call(s32[2]{0:T(128)S(1)} %pad_add_fusion.side_ref, f32[512,768]{1,0:T(8,128)S(1)} %copy-done.4, bf16[512,512]{1,0:T(8,128)(2,1)S(1)} %get-tuple-element.53.one_ref, ...), custom_call_target="tpu_custom_call" | custom-call | flops 10871635968 | bytes 11796480 | tf_op jit(solution)/shard_map/pallas_call | solution.py:605
  127.5 2.4 %collective-permute-start.8 = (f32[4,32,548]{2,1,0:T(8,128)S(1)}, f32[4,32,548]{2,1,0:T(8,128)S(1)}, u32[]{:S(2)}, u32[]{:S(2)}) collective-permute-start(f32[4,32,548]{2,1,0:T(8,128)S(1)} %get-tuple-element.57), channel_id=1, source_target_pairs={{0,4},{8,12},{16,20},{24,28},{4,0},{12,8},{20,16},{28,24},{1,5},{9... | collective-permute-start | bytes 841736 | tf_op jit(solution)/shard_map/ppermute | solution.py:458
  129.9 2.0 %collective-permute-start.9 = (f32[4,32,548]{2,1,0:T(8,128)S(1)}, f32[4,32,548]{2,1,0:T(8,128)S(1)}, u32[]{:S(2)}, u32[]{:S(2)}) collective-permute-start(f32[4,32,548]{2,1,0:T(8,128)S(1)} %get-tuple-element.58), channel_id=1, source_target_pairs={{4,8},{12,16},{20,24},{8,4},{16,12},{24,20},{5,9},{13,17},{21,25},... | collective-permute-start | bytes 841736 | tf_op jit(solution)/shard_map/ppermute | solution.py:458
  132.0 0.6 shard_map.139
  132.7 3.8 %collective-permute-start.15 = (f32[24,4,548]{2,1,0:T(4,128)S(1)}, f32[24,4,548]{2,1,0:T(4,128)S(1)}, u32[]{:S(2)}, u32[]{:S(2)}) collective-permute-start(f32[24,4,548]{2,1,0:T(4,128)S(1)} %get-tuple-element.70), channel_id=1, source_target_pairs={{1,2},{2,1},{5,6},{6,5},{9,10},{10,9},{13,14},{14,13},{17,18},{18,... | collective-permute-start | bytes 631304 | tf_op jit(solution)/shard_map/ppermute | solution.py:458
  136.6 7.7 %collective-permute-done.8.ra.refs_0_ = f32[4,32,548]{2,1,0:T(8,128)S(1)} collective-permute-done((f32[4,32,548]{2,1,0:T(8,128)S(1)}, f32[4,32,548]{2,1,0:T(8,128)S(1)}, u32[]{:S(2)}, u32[]{:S(2)}) %collective-permute-start.8) | collective-permute-done | bytes 280608 | tf_op jit(solution)/shard_map/ppermute | solution.py:458
  145.0 2.0 %collective-permute-start.11 = (f32[24,4,548]{2,1,0:T(4,128)S(1)}, f32[24,4,548]{2,1,0:T(4,128)S(1)}, u32[]{:S(2)}, u32[]{:S(2)}) collective-permute-start(f32[24,4,548]{2,1,0:T(4,128)S(1)} %get-tuple-element.62), channel_id=1, source_target_pairs={{1,2},{2,1},{5,6},{6,5},{9,10},{10,9},{13,14},{14,13},{17,18},{18,... | collective-permute-start | bytes 631304 | tf_op jit(solution)/shard_map/ppermute | solution.py:458
  147.0 4.9 %shard_map.140.refs_4_ = f32[2,16,32,548]{3,2,1,0:T(8,128)} custom-call(s32[2]{0:T(128)S(1)} %pad_add_fusion.side_ref, f32[16,32,548]{2,1,0:T(8,128)S(1)} %get-tuple-element.64.field_ref, f32[2,16,32,548]{3,2,1,0:T(8,128)S(1)} %copy-done, f32[2,24,40,128]{3,2,1,0:T(8,128)S(1)} %copy-done.2, f32[4,32,548]{2,1,0:T(8,128)S(1)} %collective-permute-done.12.ra.refs_0_, ...), custom_call_target="tpu_custom_call" | custom-call | flops 24576000 | bytes 3932160 | tf_op jit(solution)/shard_map/pallas_call | solution.py:628
  152.5 4.9 %shard_map.141 = f32[2,16,32,548]{3,2,1,0:T(8,128)} custom-call(s32[2]{0:T(128)S(1)} %pad_add_fusion.side_ref, f32[16,32,548]{2,1,0:T(8,128)S(1)} %get-tuple-element.56.field_ref, f32[2,16,32,548]{3,2,1,0:T(8,128)S(1)} %copy-done, f32[2,24,40,128]{3,2,1,0:T(8,128)S(1)} %copy-done.2, ...), custom_call_target="tpu_custom_call", output_to_operand_aliasing={{}: (8, {})} | custom-call | flops 24576000 | bytes 3932160 | tf_op jit(solution)/shard_map/pallas_call | solution.py:628
  (45 shorter events, 3.1 us)
Async XLA Ops:
  1.4 1.3 copy-start.8
  4.9 6.5 %copy-start.5 = (f32[16,32]{1,0:T(8,128)S(1)}, f32[16,32]{1,0:T(8,128)}, u32[]{:S(2)}) copy-start(f32[16,32]{1,0:T(8,128)} %coeff_ref.5) | copy-start | bytes 6148
  4.9 80.5 %all-to-all-start = ((f32[32,72,128]{2,1,0:T(8,128)}), f32[32,72,128]{2,1,0:T(8,128)}, u32[]{:S(2)}, u32[]{:S(2)}) async-start(f32[32,72,128]{2,1,0:T(8,128)} %shard_map.134), calls=%async_computation | async-start | bytes 2359296 | tf_op jit(solution)/shard_map/all_to_all | solution.py:537
  13.3 45.3 %collective-permute-start = (f32[4,32,549]{2,1,0:T(8,128)S(1)}, f32[4,32,549]{2,1,0:T(8,128)S(1)}, u32[]{:S(2)}, u32[]{:S(2)}) collective-permute-start(f32[4,32,549]{2,1,0:T(8,128)S(1)} %get-tuple-element.38), channel_id=1, source_target_pairs={{0,4},{8,12},{16,20},{24,28},{4,0},{12,8},{20,16},{28,24},{1,5},{9... | collective-permute-start | bytes 843272 | tf_op jit(solution)/shard_map/ppermute | solution.py:458
  14.6 44.0 %collective-permute-start.1 = (f32[4,32,549]{2,1,0:T(8,128)S(1)}, f32[4,32,549]{2,1,0:T(8,128)S(1)}, u32[]{:S(2)}, u32[]{:S(2)}) collective-permute-start(f32[4,32,549]{2,1,0:T(8,128)S(1)} %get-tuple-element.39), channel_id=1, source_target_pairs={{4,8},{12,16},{20,24},{8,4},{16,12},{24,20},{5,9},{13,17},{21,25},... | collective-permute-start | bytes 843272 | tf_op jit(solution)/shard_map/ppermute | solution.py:458
  18.5 35.4 %collective-permute-start.4 = (f32[4,32,548]{2,1,0:T(8,128)S(1)}, f32[4,32,548]{2,1,0:T(8,128)S(1)}, u32[]{:S(2)}, u32[]{:S(2)}) collective-permute-start(f32[4,32,548]{2,1,0:T(8,128)S(1)} %get-tuple-element.46), channel_id=1, source_target_pairs={{0,4},{8,12},{16,20},{24,28},{4,0},{12,8},{20,16},{28,24},{1,5},{9... | collective-permute-start | bytes 841736 | tf_op jit(solution)/shard_map/ppermute | solution.py:458
  20.8 33.1 %collective-permute-start.5 = (f32[4,32,548]{2,1,0:T(8,128)S(1)}, f32[4,32,548]{2,1,0:T(8,128)S(1)}, u32[]{:S(2)}, u32[]{:S(2)}) collective-permute-start(f32[4,32,548]{2,1,0:T(8,128)S(1)} %get-tuple-element.47), channel_id=1, source_target_pairs={{4,8},{12,16},{20,24},{8,4},{16,12},{24,20},{5,9},{13,17},{21,25},... | collective-permute-start | bytes 841736 | tf_op jit(solution)/shard_map/ppermute | solution.py:458
  54.5 23.0 %collective-permute-start.6 = (f32[24,4,548]{2,1,0:T(4,128)S(1)}, f32[24,4,548]{2,1,0:T(4,128)S(1)}, u32[]{:S(2)}, u32[]{:S(2)}) collective-permute-start(f32[24,4,548]{2,1,0:T(4,128)S(1)} %get-tuple-element.50), channel_id=1, source_target_pairs={{0,1},{2,3},{1,0},{3,2},{4,5},{6,7},{5,4},{7,6},{8,9},{10,11},{9,8... | collective-permute-start | bytes 631304 | tf_op jit(solution)/shard_map/ppermute | solution.py:458
  55.6 22.0 %collective-permute-start.7 = (f32[24,4,548]{2,1,0:T(4,128)S(1)}, f32[24,4,548]{2,1,0:T(4,128)S(1)}, u32[]{:S(2)}, u32[]{:S(2)}) collective-permute-start(f32[24,4,548]{2,1,0:T(4,128)S(1)} %get-tuple-element.51), channel_id=1, source_target_pairs={{1,2},{2,1},{5,6},{6,5},{9,10},{10,9},{13,14},{14,13},{17,18},{18,... | collective-permute-start | bytes 631304 | tf_op jit(solution)/shard_map/ppermute | solution.py:458
  59.2 11.0 %collective-permute-start.2 = (f32[24,4,549]{2,1,0:T(4,128)S(1)}, f32[24,4,549]{2,1,0:T(4,128)S(1)}, u32[]{:S(2)}, u32[]{:S(2)}) collective-permute-start(f32[24,4,549]{2,1,0:T(4,128)S(1)} %get-tuple-element.42), channel_id=1, source_target_pairs={{0,1},{2,3},{1,0},{3,2},{4,5},{6,7},{5,4},{7,6},{8,9},{10,11},{9,8... | collective-permute-start | bytes 632456 | tf_op jit(solution)/shard_map/ppermute | solution.py:458
  59.3 11.0 %collective-permute-start.3 = (f32[24,4,549]{2,1,0:T(4,128)S(1)}, f32[24,4,549]{2,1,0:T(4,128)S(1)}, u32[]{:S(2)}, u32[]{:S(2)}) collective-permute-start(f32[24,4,549]{2,1,0:T(4,128)S(1)} %get-tuple-element.43), channel_id=1, source_target_pairs={{1,2},{2,1},{5,6},{6,5},{9,10},{10,9},{13,14},{14,13},{17,18},{18,... | collective-permute-start | bytes 632456 | tf_op jit(solution)/shard_map/ppermute | solution.py:458
  61.9 8.3 %copy-start.10 = (f32[768]{0:T(1024)S(1)}, f32[768]{0:T(1024)}, u32[]{:S(2)}) copy-start(f32[768]{0:T(1024)} %param.17) | copy-start | bytes 9220
  61.9 8.3 %copy-start.11 = (f32[768]{0:T(1024)S(1)}, f32[768]{0:T(1024)}, u32[]{:S(2)}) copy-start(f32[768]{0:T(1024)} %param.19) | copy-start | bytes 9220
  61.9 8.4 %copy-start = (f32[2,16,32,548]{3,2,1,0:T(8,128)S(1)}, f32[2,16,32,548]{3,2,1,0:T(8,128)}, u32[]{:S(2)}) copy-start(f32[2,16,32,548]{3,2,1,0:T(8,128)} %base_ref.3) | copy-start | bytes 6733828
  76.4 1.1 copy-start.6
  77.5 7.8 %copy-start.9 = (s32[32,616]{1,0:T(8,128)S(1)}, s32[32,616]{1,0:T(8,128)}, u32[]{:S(2)}) copy-start(s32[32,616]{1,0:T(8,128)} %mask_ref.1) | copy-start | bytes 236548
  83.2 1.0 copy-start.1
  84.2 1.2 copy-start.3
  85.4 6.2 %copy-start.7 = (f32[512,768]{1,0:T(8,128)S(1)}, f32[512,768]{1,0:T(8,128)}, u32[]{:S(2)}) copy-start(f32[512,768]{1,0:T(8,128)} %copy-done.6) | copy-start | bytes 4718596
  91.6 19.2 %copy-start.4 = (f32[512,768]{1,0:T(8,128)S(1)}, f32[512,768]{1,0:T(8,128)}, u32[]{:S(2)}) copy-start(f32[512,768]{1,0:T(8,128)} %copy-done.3) | copy-start | bytes 4718596
  108.5 23.5 %collective-permute-start.12 = (f32[4,32,548]{2,1,0:T(8,128)S(1)}, f32[4,32,548]{2,1,0:T(8,128)S(1)}, u32[]{:S(2)}, u32[]{:S(2)}) collective-permute-start(f32[4,32,548]{2,1,0:T(8,128)S(1)} %get-tuple-element.65), channel_id=1, source_target_pairs={{0,4},{8,12},{16,20},{24,28},{4,0},{12,8},{20,16},{28,24},{1,5},{9... | collective-permute-start | bytes 841736 | tf_op jit(solution)/shard_map/ppermute | solution.py:458
  108.9 23.1 %collective-permute-start.13 = (f32[4,32,548]{2,1,0:T(8,128)S(1)}, f32[4,32,548]{2,1,0:T(8,128)S(1)}, u32[]{:S(2)}, u32[]{:S(2)}) collective-permute-start(f32[4,32,548]{2,1,0:T(8,128)S(1)} %get-tuple-element.66), channel_id=1, source_target_pairs={{4,8},{12,16},{20,24},{8,4},{16,12},{24,20},{5,9},{13,17},{21,25},... | collective-permute-start | bytes 841736 | tf_op jit(solution)/shard_map/ppermute | solution.py:458
  127.5 19.5 %copy-start.2 = (f32[2,24,40,128]{3,2,1,0:T(8,128)S(1)}, f32[2,24,40,128]{3,2,1,0:T(8,128)}, u32[]{:S(2)}) copy-start(f32[2,24,40,128]{3,2,1,0:T(8,128)} %copy-done.1) | copy-start | bytes 2949124
  127.5 16.8 %collective-permute-start.8 = (f32[4,32,548]{2,1,0:T(8,128)S(1)}, f32[4,32,548]{2,1,0:T(8,128)S(1)}, u32[]{:S(2)}, u32[]{:S(2)}) collective-permute-start(f32[4,32,548]{2,1,0:T(8,128)S(1)} %get-tuple-element.57), channel_id=1, source_target_pairs={{0,4},{8,12},{16,20},{24,28},{4,0},{12,8},{20,16},{28,24},{1,5},{9... | collective-permute-start | bytes 841736 | tf_op jit(solution)/shard_map/ppermute | solution.py:458
  129.9 14.3 %collective-permute-start.9 = (f32[4,32,548]{2,1,0:T(8,128)S(1)}, f32[4,32,548]{2,1,0:T(8,128)S(1)}, u32[]{:S(2)}, u32[]{:S(2)}) collective-permute-start(f32[4,32,548]{2,1,0:T(8,128)S(1)} %get-tuple-element.58), channel_id=1, source_target_pairs={{4,8},{12,16},{20,24},{8,4},{16,12},{24,20},{5,9},{13,17},{21,25},... | collective-permute-start | bytes 841736 | tf_op jit(solution)/shard_map/ppermute | solution.py:458
  132.6 14.4 %collective-permute-start.14 = (f32[24,4,548]{2,1,0:T(4,128)S(1)}, f32[24,4,548]{2,1,0:T(4,128)S(1)}, u32[]{:S(2)}, u32[]{:S(2)}) collective-permute-start(f32[24,4,548]{2,1,0:T(4,128)S(1)} %get-tuple-element.69), channel_id=1, source_target_pairs={{0,1},{2,3},{1,0},{3,2},{4,5},{6,7},{5,4},{7,6},{8,9},{10,11},{9,8... | collective-permute-start | bytes 631304 | tf_op jit(solution)/shard_map/ppermute | solution.py:458
  132.7 14.3 %collective-permute-start.15 = (f32[24,4,548]{2,1,0:T(4,128)S(1)}, f32[24,4,548]{2,1,0:T(4,128)S(1)}, u32[]{:S(2)}, u32[]{:S(2)}) collective-permute-start(f32[24,4,548]{2,1,0:T(4,128)S(1)} %get-tuple-element.70), channel_id=1, source_target_pairs={{1,2},{2,1},{5,6},{6,5},{9,10},{10,9},{13,14},{14,13},{17,18},{18,... | collective-permute-start | bytes 631304 | tf_op jit(solution)/shard_map/ppermute | solution.py:458
  144.9 7.1 %collective-permute-start.10 = (f32[24,4,548]{2,1,0:T(4,128)S(1)}, f32[24,4,548]{2,1,0:T(4,128)S(1)}, u32[]{:S(2)}, u32[]{:S(2)}) collective-permute-start(f32[24,4,548]{2,1,0:T(4,128)S(1)} %get-tuple-element.61), channel_id=1, source_target_pairs={{0,1},{2,3},{1,0},{3,2},{4,5},{6,7},{5,4},{7,6},{8,9},{10,11},{9,8... | collective-permute-start | bytes 631304 | tf_op jit(solution)/shard_map/ppermute | solution.py:458
  145.0 7.5 %collective-permute-start.11 = (f32[24,4,548]{2,1,0:T(4,128)S(1)}, f32[24,4,548]{2,1,0:T(4,128)S(1)}, u32[]{:S(2)}, u32[]{:S(2)}) collective-permute-start(f32[24,4,548]{2,1,0:T(4,128)S(1)} %get-tuple-element.62), channel_id=1, source_target_pairs={{1,2},{2,1},{5,6},{6,5},{9,10},{10,9},{13,14},{14,13},{17,18},{18,... | collective-permute-start | bytes 631304 | tf_op jit(solution)/shard_map/ppermute | solution.py:458

commit v5 on v4

--- a/solution.py
+++ b/solution.py
@@ -213,16 +213,40 @@
     fill(ext, side_ref, tile, *strips, part)
 
 
+def sweeps(load, cb_ref, work, emit, wide):
+    tall, around = cb_ref.shape[1:3]
+
+    def put(buffer, i, value):
+        work[buffer, i, 8 : 8 + around] = value
+        work[buffer, i, :8] = value[around - 8 :]
+        work[buffer, i, 8 + around :] = value[:8]
+
+    for i in range(tall):
+        put(0, i, load(i))
+    for sweep in range(SWEEPS):
+        source = sweep % 2
+        last = sweep == SWEEPS - 1
+        size = wide if last else around
+        for i in range(sweep + 1, tall - 1 - sweep):
+
+            def near(row, by):
+                return work[source, row, 8 + by : 8 + by + size]
+
+            beside = (near(i - 1, 0) + near(i + 1, 0)) + (near(i, -1) + near(i, 1))
+            new = cb_ref[1, i, :size] * near(i, 0) + cb_ref[0, i, :size] * beside
+            if last:
+                emit(i - SWEEPS, new)
+            else:
+                put(1 - source, i, new)
+
+
 def diffuse_kernel(v, side_ref, tile_ref, coeff_ref, *refs):
     strips, stack_ref, refs = refs[:4], refs[4], refs[5:]
     ext, work, high_ref, low_ref, both, sem = refs[-6:]
     out_ref = refs[0]
     fetch = pltpu.make_async_copy(stack_ref.at[3], both, sem)
     fetch.start()
-    w = SWEEPS
     rows, wide, levels = tile_ref.shape[1:]
-    tall = rows + 2 * w
-    around = wide + 2 * w
     fill_levels(ext, side_ref, tile_ref[v], *strips)
     if v > 0:
         cb_ref = coeff_ref
@@ -238,24 +262,16 @@
         )
         fill(cb_ref.at[0], side_ref, own, *strips, (pl.ds(0, LANES), spread))
         cb_ref[1] = 1.0 - 4.0 * cb_ref[0]
+        cb_ref[2] = 1.0 / jnp.where(cb_ref[0] == 0.0, 1.0, cb_ref[0])
 
     def chunk(j, _):
         lanes = pl.ds(pl.multiple_of(j * LANES, LANES), LANES)
-        for sweep in range(SWEEPS):
-            for i in range(sweep + 1, tall - 1 - sweep):
-                if sweep == 0:
-                    above, mid, below = (ext[k, :, lanes] for k in (i - 1, i, i + 1))
-                else:
-                    above, mid, below = (work[(sweep + 1) % 2, k] for k in (i - 1, i, i + 1))
-                beside = above + below + pltpu.roll(mid, 1, 0) + pltpu.roll(mid, around - 1, 0)
-                new = cb_ref[1, i] * mid + cb_ref[0, i] * beside
-                if sweep == SWEEPS - 1:
-                    high, low = split(new[:wide])
-                    here = pl.ds((i - w) * wide, wide)
-                    high_ref[here, lanes] = high
-                    low_ref[here, lanes] = low
-                else:
-                    work[sweep % 2, i] = new
+
+        def emit(row, value):
+            here = pl.ds(row * wide, wide)
+            high_ref[here, lanes], low_ref[here, lanes] = split(value)
+
+        sweeps(lambda i: ext[i, :, lanes], cb_ref, work, emit, wide)
         return 0
 
     lax.fori_loop(0, ext.shape[2] // LANES, chunk, 0)
@@ -413,33 +429,15 @@
     out_ref, ext, work, total, result, sems = refs[-6:]
     w = SWEEPS
     rows, wide, levels = field_ref.shape
-    tall = rows + 2 * w
     fill_levels(ext, side_ref, field_ref[...], *refs[:4])
-    around = wide + 2 * w
 
     def chunk(j, _):
         lanes = pl.ds(pl.multiple_of(j * LANES, LANES), LANES)
-        for sweep in range(SWEEPS):
-
-            def read(k):
-                value = ext[k, :, lanes] if sweep == 0 else work[(sweep + 1) % 2, k]
-                return value, cb_ref[0, k] * value
-
-            above = read(sweep)
-            mid = read(sweep + 1)
-            for i in range(sweep + 1, tall - 1 - sweep):
-                below = read(i + 1)
-                scaled = mid[1]
-                beside = (
-                    above[1] + below[1]
-                    + pltpu.roll(scaled, 1, 0) + pltpu.roll(scaled, around - 1, 0)
-                )
-                new = cb_ref[1, i] * mid[0] + beside
-                if sweep == SWEEPS - 1:
-                    total[i - w, :, lanes] = new[:wide]
-                else:
-                    work[sweep % 2, i] = new
-                above, mid = mid, below
+
+        def emit(row, value):
+            total[row, :, lanes] = cb_ref[2, row + w, :wide] * value
+
+        sweeps(lambda i: cb_ref[0, i] * ext[i, :, lanes], cb_ref, work, emit, wide)
         return 0
 
     lax.fori_loop(0, ext.shape[2] // LANES, chunk, 0)
@@ -565,12 +563,12 @@
     for v in range(pairs):
         got = call(
             functools.partial(diffuse_kernel, v),
-            [shaped((cells, side))] + [shaped((2, tall, around, LANES))] * (v == 0),
+            [shaped((cells, side))] + [shaped((3, tall, around, LANES))] * (v == 0),
             flops=6 * cells * deep * full_u,
             moved=8 * tall * around * deep,
             scratch=[
                 pltpu.VMEM((tall, around, deep), F32),
-                pltpu.VMEM((2, tall, around, LANES), F32),
+                pltpu.VMEM((2, tall, around + 16, LANES), F32),
                 pltpu.VMEM((cells, deep), BF),
                 pltpu.VMEM((cells, deep), BF),
                 pltpu.VMEM((2, side, side), BF),
@@ -632,7 +630,7 @@
             moved=12 * cells * deep,
             scratch=[
                 pltpu.VMEM((tall, around, deep), F32),
-                pltpu.VMEM((2, tall, around, LANES), F32),
+                pltpu.VMEM((2, tall, around + 16, LANES), F32),
                 pltpu.VMEM((tile_x, tile_y, deep), F32),
                 pltpu.VMEM((tile_x, tile_y, levels), F32),
                 pltpu.SemaphoreType.DMA((2,)),

time: 159 us -> 157 us (0.987)
  Pallas kernels: 78.4 us -> 75.9 us
where the time goes in v5:
time: 157 us; the launch traced here: 156 us
  Pallas kernels  75.9 us (48%)
  waiting for transfers between devices  40 us (25%)
  starting transfers between devices  33.3 us (21%)
  local copies, waits for them, and re-layouts  4.74 us (3%)
    ppermute x16, waiting for transfers between devices, swap(): return lax.ppermute(value, axis, pairs + [(j, i) for i, j in pairs])  40 us
    pallas_call x2, Pallas kernels, body(): call(net_kernel, [shaped((tile_x, tile_y, levels))] + [shaped((SWEEPS, ti...  33.6 us
    ppermute x16, starting transfers between devices, swap(): return lax.ppermute(value, axis, pairs + [(j, i) for i, j in pairs])  26.9 us
    pallas_call x2, Pallas kernels, body(): call(functools.partial(diffuse_kernel, v), [shaped((cells, side))] + [sha...  10.5 us
    pallas_call x2, Pallas kernels, body(): call(functools.partial(finish_kernel, v), pltpu.HBM(vectors.shape, F32),...  8.66 us
    pallas_call x1, Pallas kernels, body(): call(prep_kernel, [pltpu.HBM((2, full_l, side), BF), pltpu.HBM((4, 2, sid...  8.29 us
    all_to_all x1, starting transfers between devices, body(): lax.all_to_all(packed if tight else packed.reshape(devices, bucket, deep)...  6.38 us
    pallas_call x1, Pallas kernels, body(): call(functools.partial(hidden_kernel, mark, bucket), [shaped((3, slots, s...  6.2 us
  transfers between devices with their start and end apart: 17, of which 3 were waited for; matrix products, arithmetic and copies ran while one was open for 0% of the time, Pallas kernels for 30%

profile of v5, /device:TPU:9, one launch (start us, length us, event | category | flops | bytes accessed | tf_op | source)
XLA Modules:
  0.0 155.9 jit_solution(8883376001372309716)
XLA Ops:
  0.7 0.7 fusion.6
  1.4 1.2 copy-done.8
  2.6 2.3 %shard_map.134 = f32[32,72,128]{2,1,0:T(8,128)} custom-call(s32[1,512]{1,0:T(1,128)S(1)} %bitcast.9, f32[1,512]{1,0:T(1,128)S(1)} %bitcast.8, f32[548,512]{1,0:T(8,128)S(1)} %bitcast.10), custom_call_target="tpu_custom_call" | custom-call | flops 1006632960 | bytes 2621440 | tf_op jit(solution)/shard_map/pallas_call | solution.py:527
  4.9 6.4 %all-to-all-start = ((f32[32,72,128]{2,1,0:T(8,128)}), f32[32,72,128]{2,1,0:T(8,128)}, u32[]{:S(2)}, u32[]{:S(2)}) async-start(f32[32,72,128]{2,1,0:T(8,128)} %shard_map.134), calls=%async_computation | async-start | bytes 2359296 | tf_op jit(solution)/shard_map/all_to_all | solution.py:535
  11.4 1.9 %shard_map.127 = (f32[4,32,549]{2,1,0:T(8,128)S(1)}, f32[4,32,549]{2,1,0:T(8,128)S(1)}, f32[16,4,549]{2,1,0:T(4,128)S(1)}, f32[16,4,549]{2,1,0:T(4,128)S(1)}) custom-call(s32[2]{0:T(128)S(1)} %pad_add_fusion.side_ref, f32[2,16,32,548]{3,2,1,0:T(8,128)} %base_ref.3, f32[16,32]{1,0:T(8,128)S(1)} %copy-done.5), custom_call_target="tpu_custom_call" | custom-call | bytes 2244608 | tf_op jit(solution)/shard_map/pallas_call | solution.py:504
  13.3 1.2 collective-permute-start
  14.6 2.0 %collective-permute-start.1 = (f32[4,32,549]{2,1,0:T(8,128)S(1)}, f32[4,32,549]{2,1,0:T(8,128)S(1)}, u32[]{:S(2)}, u32[]{:S(2)}) collective-permute-start(f32[4,32,549]{2,1,0:T(8,128)S(1)} %get-tuple-element.39), channel_id=1, source_target_pairs={{4,8},{12,16},{20,24},{8,4},{16,12},{24,20},{5,9},{13,17},{21,25},... | collective-permute-start | bytes 843272 | tf_op jit(solution)/shard_map/ppermute | solution.py:456
  16.6 1.9 %shard_map.131 = (f32[4,32,548]{2,1,0:T(8,128)S(1)}, f32[4,32,548]{2,1,0:T(8,128)S(1)}, f32[16,4,548]{2,1,0:T(4,128)S(1)}, f32[16,4,548]{2,1,0:T(4,128)S(1)}) custom-call(s32[2]{0:T(128)S(1)} %pad_add_fusion.side_ref, f32[2,16,32,548]{3,2,1,0:T(8,128)} %base_ref.3, f32[16,32]{1,0:T(8,128)S(1)} %copy-done.5), custom_call_target="tpu_custom_call" | custom-call | bytes 2244608 | tf_op jit(solution)/shard_map/pallas_call | solution.py:504
  18.5 2.3 %collective-permute-start.4 = (f32[4,32,548]{2,1,0:T(8,128)S(1)}, f32[4,32,548]{2,1,0:T(8,128)S(1)}, u32[]{:S(2)}, u32[]{:S(2)}) collective-permute-start(f32[4,32,548]{2,1,0:T(8,128)S(1)} %get-tuple-element.46), channel_id=1, source_target_pairs={{0,4},{8,12},{16,20},{24,28},{4,0},{12,8},{20,16},{28,24},{1,5},{9... | collective-permute-start | bytes 841736 | tf_op jit(solution)/shard_map/ppermute | solution.py:456
  20.8 1.9 %collective-permute-start.5 = (f32[4,32,548]{2,1,0:T(8,128)S(1)}, f32[4,32,548]{2,1,0:T(8,128)S(1)}, u32[]{:S(2)}, u32[]{:S(2)}) collective-permute-start(f32[4,32,548]{2,1,0:T(8,128)S(1)} %get-tuple-element.47), channel_id=1, source_target_pairs={{4,8},{12,16},{20,24},{8,4},{16,12},{24,20},{5,9},{13,17},{21,25},... | collective-permute-start | bytes 841736 | tf_op jit(solution)/shard_map/ppermute | solution.py:456
  22.8 31.1 %collective-permute-done.4.ra.refs_0_ = f32[4,32,548]{2,1,0:T(8,128)S(1)} collective-permute-done((f32[4,32,548]{2,1,0:T(8,128)S(1)}, f32[4,32,548]{2,1,0:T(8,128)S(1)}, u32[]{:S(2)}, u32[]{:S(2)}) %collective-permute-start.4) | collective-permute-done | bytes 280608 | tf_op jit(solution)/shard_map/ppermute | solution.py:456
  54.5 1.0 collective-permute-start.6
  55.6 3.0 %collective-permute-start.7 = (f32[24,4,548]{2,1,0:T(4,128)S(1)}, f32[24,4,548]{2,1,0:T(4,128)S(1)}, u32[]{:S(2)}, u32[]{:S(2)}) collective-permute-start(f32[24,4,548]{2,1,0:T(4,128)S(1)} %get-tuple-element.51), channel_id=1, source_target_pairs={{1,2},{2,1},{5,6},{6,5},{9,10},{10,9},{13,14},{14,13},{17,18},{18,... | collective-permute-start | bytes 631304 | tf_op jit(solution)/shard_map/ppermute | solution.py:456
  59.3 2.6 %collective-permute-start.3 = (f32[24,4,549]{2,1,0:T(4,128)S(1)}, f32[24,4,549]{2,1,0:T(4,128)S(1)}, u32[]{:S(2)}, u32[]{:S(2)}) collective-permute-start(f32[24,4,549]{2,1,0:T(4,128)S(1)} %get-tuple-element.43), channel_id=1, source_target_pairs={{1,2},{2,1},{5,6},{6,5},{9,10},{10,9},{13,14},{14,13},{17,18},{18,... | collective-permute-start | bytes 632456 | tf_op jit(solution)/shard_map/ppermute | solution.py:456
  61.9 8.3 %shard_map.129 = (bf16[2,768,768]{2,1,0:T(8,128)(2,1)}, bf16[4,2,768,768]{3,2,1,0:T(8,128)(2,1)}) custom-call(f32[548,548]{1,0:T(8,128)} %refs_0_.1, f32[548,768]{1,0:T(8,128)} %refs_1_.1, f32[768,768]{1,0:T(8,128)} %refs_2_.1, f32[616,768]{1,0:T(8,128)} %bitcast.11, f32[616,616]{1,0:T(8,128)} %refs_4_.1), custom_call_target="tpu_custom_call" | custom-call | flops 2717908992 | bytes 23592960 | tf_op jit(solution)/shard_map/pallas_call | solution.py:542
  70.3 5.5 %shard_map.130 = (f32[512,768]{1,0:T(8,128)S(1)}, f32[3,24,40,128]{3,2,1,0:T(8,128)S(1)}) custom-call(s32[2]{0:T(128)S(1)} %pad_add_fusion.side_ref, f32[2,16,32,548]{3,2,1,0:T(8,128)S(1)} %copy-done, f32[16,32]{1,0:T(8,128)S(1)} %copy-done.5, f32[4,32,549]{2,1,0:T(8,128)S(1)} %collective-permute-done.ra.refs_0_, ...), custom_call_target="tpu_custom_call" | custom-call | flops 1509949440 | bytes 4915200 | tf_op jit(solution)/shard_map/pallas_call | solution.py:564
  75.8 1.1 copy-done.6
  77.0 5.0 %shard_map.133.q_ref = f32[512,768]{1,0:T(8,128)S(1)} custom-call(s32[2]{0:T(128)S(1)} %pad_add_fusion.side_ref, f32[2,16,32,548]{3,2,1,0:T(8,128)S(1)} %copy-done, f32[3,24,40,128]{3,2,1,0:T(8,128)S(1)} %get-tuple-element.45.coeff_ref.cb_ref, f32[4,32,548]{2,1,0:T(8,128)S(1)} %collective-permute-done.4.ra.refs_0_, ...), custom_call_target="tpu_custom_call" | custom-call | flops 1509949440 | bytes 4915200 | tf_op jit(solution)/shard_map/pallas_call | solution.py:564
  82.0 1.1 copy-done.1
  83.1 1.2 copy-done.3
  84.3 6.2 %shard_map.135 = (f32[3,512,768]{2,1,0:T(8,128)S(1)}, bf16[512,512]{1,0:T(8,128)(2,1)S(1)}, bf16[512,512]{1,0:T(8,128)(2,1)S(1)}) custom-call(f32[32,72,128]{2,1,0:T(8,128)} %all-to-all-done.x_ref, bf16[2,768,768]{2,1,0:T(8,128)(2,1)} %get-tuple-element.52.first_ref, f32[1,768]{1,0:T(1,128)S(1)} %broadcast_in_dim.16.b1_ref, ...), custom_call_target="tpu_custom_call" | custom-call | flops 3623878656 | bytes 3145728 | tf_op jit(solution)/shard_map/pallas_call | solution.py:585
  90.6 16.9 %shard_map.138 = (f32[16,32,548]{2,1,0:T(8,128)S(1)}, f32[4,32,548]{2,1,0:T(8,128)S(1)}, f32[4,32,548]{2,1,0:T(8,128)S(1)}, f32[16,4,548]{2,1,0:T(4,128)S(1)}, f32[16,4,548]{2,1,0:T(4,128)S(1)}) custom-call(s32[2]{0:T(128)S(1)} %pad_add_fusion.side_ref, f32[512,768]{1,0:T(8,128)S(1)} %copy-done.7, bf16[512,512]{1,0:T(8,128)(2,1)S(1)} %get-tuple-element.53.one_ref, ...), custom_call_target="tpu_custom_call" | custom-call | flops 10871635968 | bytes 11796480 | tf_op jit(solution)/shard_map/pallas_call | solution.py:603
  107.8 1.9 %collective-permute-start.13 = (f32[4,32,548]{2,1,0:T(8,128)S(1)}, f32[4,32,548]{2,1,0:T(8,128)S(1)}, u32[]{:S(2)}, u32[]{:S(2)}) collective-permute-start(f32[4,32,548]{2,1,0:T(8,128)S(1)} %get-tuple-element.66), channel_id=1, source_target_pairs={{4,8},{12,16},{20,24},{8,4},{16,12},{24,20},{5,9},{13,17},{21,25},... | collective-permute-start | bytes 841736 | tf_op jit(solution)/shard_map/ppermute | solution.py:456
  109.7 16.7 %shard_map.136 = (f32[16,32,548]{2,1,0:T(8,128)S(1)}, f32[4,32,548]{2,1,0:T(8,128)S(1)}, f32[4,32,548]{2,1,0:T(8,128)S(1)}, f32[16,4,548]{2,1,0:T(4,128)S(1)}, f32[16,4,548]{2,1,0:T(4,128)S(1)}) custom-call(s32[2]{0:T(128)S(1)} %pad_add_fusion.side_ref, f32[512,768]{1,0:T(8,128)S(1)} %copy-done.4, bf16[512,512]{1,0:T(8,128)(2,1)S(1)} %get-tuple-element.53.one_ref, ...), custom_call_target="tpu_custom_call" | custom-call | flops 10871635968 | bytes 11796480 | tf_op jit(solution)/shard_map/pallas_call | solution.py:603
  126.4 2.4 %collective-permute-start.8 = (f32[4,32,548]{2,1,0:T(8,128)S(1)}, f32[4,32,548]{2,1,0:T(8,128)S(1)}, u32[]{:S(2)}, u32[]{:S(2)}) collective-permute-start(f32[4,32,548]{2,1,0:T(8,128)S(1)} %get-tuple-element.57), channel_id=1, source_target_pairs={{0,4},{8,12},{16,20},{24,28},{4,0},{12,8},{20,16},{28,24},{1,5},{9... | collective-permute-start | bytes 841736 | tf_op jit(solution)/shard_map/ppermute | solution.py:456
  128.9 2.0 %collective-permute-start.9 = (f32[4,32,548]{2,1,0:T(8,128)S(1)}, f32[4,32,548]{2,1,0:T(8,128)S(1)}, u32[]{:S(2)}, u32[]{:S(2)}) collective-permute-start(f32[4,32,548]{2,1,0:T(8,128)S(1)} %get-tuple-element.58), channel_id=1, source_target_pairs={{4,8},{12,16},{20,24},{8,4},{16,12},{24,20},{5,9},{13,17},{21,25},... | collective-permute-start | bytes 841736 | tf_op jit(solution)/shard_map/ppermute | solution.py:456
  131.7 3.8 %collective-permute-start.15 = (f32[24,4,548]{2,1,0:T(4,128)S(1)}, f32[24,4,548]{2,1,0:T(4,128)S(1)}, u32[]{:S(2)}, u32[]{:S(2)}) collective-permute-start(f32[24,4,548]{2,1,0:T(4,128)S(1)} %get-tuple-element.70), channel_id=1, source_target_pairs={{1,2},{2,1},{5,6},{6,5},{9,10},{10,9},{13,14},{14,13},{17,18},{18,... | collective-permute-start | bytes 631304 | tf_op jit(solution)/shard_map/ppermute | solution.py:456
  135.5 7.7 %collective-permute-done.8.ra.refs_0_ = f32[4,32,548]{2,1,0:T(8,128)S(1)} collective-permute-done((f32[4,32,548]{2,1,0:T(8,128)S(1)}, f32[4,32,548]{2,1,0:T(8,128)S(1)}, u32[]{:S(2)}, u32[]{:S(2)}) %collective-permute-start.8) | collective-permute-done | bytes 280608 | tf_op jit(solution)/shard_map/ppermute | solution.py:456
  143.9 2.0 %collective-permute-start.11 = (f32[24,4,548]{2,1,0:T(4,128)S(1)}, f32[24,4,548]{2,1,0:T(4,128)S(1)}, u32[]{:S(2)}, u32[]{:S(2)}) collective-permute-start(f32[24,4,548]{2,1,0:T(4,128)S(1)} %get-tuple-element.62), channel_id=1, source_target_pairs={{1,2},{2,1},{5,6},{6,5},{9,10},{10,9},{13,14},{14,13},{17,18},{18,... | collective-permute-start | bytes 631304 | tf_op jit(solution)/shard_map/ppermute | solution.py:456
  146.0 4.3 %shard_map.140.refs_4_ = f32[2,16,32,548]{3,2,1,0:T(8,128)} custom-call(s32[2]{0:T(128)S(1)} %pad_add_fusion.side_ref, f32[16,32,548]{2,1,0:T(8,128)S(1)} %get-tuple-element.64.field_ref, f32[2,16,32,548]{3,2,1,0:T(8,128)S(1)} %copy-done, f32[3,24,40,128]{3,2,1,0:T(8,128)S(1)} %copy-done.2, f32[4,32,548]{2,1,0:T(8,128)S(1)} %collective-permute-done.12.ra.refs_0_, ...), custom_call_target="tpu_custom_call" | custom-call | flops 24576000 | bytes 3932160 | tf_op jit(solution)/shard_map/pallas_call | solution.py:626
  150.3 1.1 collective-permute-done.11.refs_3_
  151.4 4.3 %shard_map.141 = f32[2,16,32,548]{3,2,1,0:T(8,128)} custom-call(s32[2]{0:T(128)S(1)} %pad_add_fusion.side_ref, f32[16,32,548]{2,1,0:T(8,128)S(1)} %get-tuple-element.56.field_ref, f32[2,16,32,548]{3,2,1,0:T(8,128)S(1)} %copy-done, f32[3,24,40,128]{3,2,1,0:T(8,128)S(1)} %copy-done.2, ...), custom_call_target="tpu_custom_call", output_to_operand_aliasing={{}: (8, {})} | custom-call | flops 24576000 | bytes 3932160 | tf_op jit(solution)/shard_map/pallas_call | solution.py:626
  (45 shorter events, 3.3 us)
Async XLA Ops:
  1.4 1.3 copy-start.8
  4.9 6.5 %copy-start.5 = (f32[16,32]{1,0:T(8,128)S(1)}, f32[16,32]{1,0:T(8,128)}, u32[]{:S(2)}) copy-start(f32[16,32]{1,0:T(8,128)} %coeff_ref.5) | copy-start | bytes 6148
  4.9 79.4 %all-to-all-start = ((f32[32,72,128]{2,1,0:T(8,128)}), f32[32,72,128]{2,1,0:T(8,128)}, u32[]{:S(2)}, u32[]{:S(2)}) async-start(f32[32,72,128]{2,1,0:T(8,128)} %shard_map.134), calls=%async_computation | async-start | bytes 2359296 | tf_op jit(solution)/shard_map/all_to_all | solution.py:535
  13.3 45.3 %collective-permute-start = (f32[4,32,549]{2,1,0:T(8,128)S(1)}, f32[4,32,549]{2,1,0:T(8,128)S(1)}, u32[]{:S(2)}, u32[]{:S(2)}) collective-permute-start(f32[4,32,549]{2,1,0:T(8,128)S(1)} %get-tuple-element.38), channel_id=1, source_target_pairs={{0,4},{8,12},{16,20},{24,28},{4,0},{12,8},{20,16},{28,24},{1,5},{9... | collective-permute-start | bytes 843272 | tf_op jit(solution)/shard_map/ppermute | solution.py:456
  14.6 44.0 %collective-permute-start.1 = (f32[4,32,549]{2,1,0:T(8,128)S(1)}, f32[4,32,549]{2,1,0:T(8,128)S(1)}, u32[]{:S(2)}, u32[]{:S(2)}) collective-permute-start(f32[4,32,549]{2,1,0:T(8,128)S(1)} %get-tuple-element.39), channel_id=1, source_target_pairs={{4,8},{12,16},{20,24},{8,4},{16,12},{24,20},{5,9},{13,17},{21,25},... | collective-permute-start | bytes 843272 | tf_op jit(solution)/shard_map/ppermute | solution.py:456
  18.5 35.4 %collective-permute-start.4 = (f32[4,32,548]{2,1,0:T(8,128)S(1)}, f32[4,32,548]{2,1,0:T(8,128)S(1)}, u32[]{:S(2)}, u32[]{:S(2)}) collective-permute-start(f32[4,32,548]{2,1,0:T(8,128)S(1)} %get-tuple-element.46), channel_id=1, source_target_pairs={{0,4},{8,12},{16,20},{24,28},{4,0},{12,8},{20,16},{28,24},{1,5},{9... | collective-permute-start | bytes 841736 | tf_op jit(solution)/shard_map/ppermute | solution.py:456
  20.8 33.1 %collective-permute-start.5 = (f32[4,32,548]{2,1,0:T(8,128)S(1)}, f32[4,32,548]{2,1,0:T(8,128)S(1)}, u32[]{:S(2)}, u32[]{:S(2)}) collective-permute-start(f32[4,32,548]{2,1,0:T(8,128)S(1)} %get-tuple-element.47), channel_id=1, source_target_pairs={{4,8},{12,16},{20,24},{8,4},{16,12},{24,20},{5,9},{13,17},{21,25},... | collective-permute-start | bytes 841736 | tf_op jit(solution)/shard_map/ppermute | solution.py:456
  54.5 22.4 %collective-permute-start.6 = (f32[24,4,548]{2,1,0:T(4,128)S(1)}, f32[24,4,548]{2,1,0:T(4,128)S(1)}, u32[]{:S(2)}, u32[]{:S(2)}) collective-permute-start(f32[24,4,548]{2,1,0:T(4,128)S(1)} %get-tuple-element.50), channel_id=1, source_target_pairs={{0,1},{2,3},{1,0},{3,2},{4,5},{6,7},{5,4},{7,6},{8,9},{10,11},{9,8... | collective-permute-start | bytes 631304 | tf_op jit(solution)/shard_map/ppermute | solution.py:456
  55.6 21.4 %collective-permute-start.7 = (f32[24,4,548]{2,1,0:T(4,128)S(1)}, f32[24,4,548]{2,1,0:T(4,128)S(1)}, u32[]{:S(2)}, u32[]{:S(2)}) collective-permute-start(f32[24,4,548]{2,1,0:T(4,128)S(1)} %get-tuple-element.51), channel_id=1, source_target_pairs={{1,2},{2,1},{5,6},{6,5},{9,10},{10,9},{13,14},{14,13},{17,18},{18,... | collective-permute-start | bytes 631304 | tf_op jit(solution)/shard_map/ppermute | solution.py:456
  59.2 11.0 %collective-permute-start.2 = (f32[24,4,549]{2,1,0:T(4,128)S(1)}, f32[24,4,549]{2,1,0:T(4,128)S(1)}, u32[]{:S(2)}, u32[]{:S(2)}) collective-permute-start(f32[24,4,549]{2,1,0:T(4,128)S(1)} %get-tuple-element.42), channel_id=1, source_target_pairs={{0,1},{2,3},{1,0},{3,2},{4,5},{6,7},{5,4},{7,6},{8,9},{10,11},{9,8... | collective-permute-start | bytes 632456 | tf_op jit(solution)/shard_map/ppermute | solution.py:456
  59.3 11.0 %collective-permute-start.3 = (f32[24,4,549]{2,1,0:T(4,128)S(1)}, f32[24,4,549]{2,1,0:T(4,128)S(1)}, u32[]{:S(2)}, u32[]{:S(2)}) collective-permute-start(f32[24,4,549]{2,1,0:T(4,128)S(1)} %get-tuple-element.43), channel_id=1, source_target_pairs={{1,2},{2,1},{5,6},{6,5},{9,10},{10,9},{13,14},{14,13},{17,18},{18,... | collective-permute-start | bytes 632456 | tf_op jit(solution)/shard_map/ppermute | solution.py:456
  61.9 8.3 %copy-start.10 = (f32[768]{0:T(1024)S(1)}, f32[768]{0:T(1024)}, u32[]{:S(2)}) copy-start(f32[768]{0:T(1024)} %param.17) | copy-start | bytes 9220
  61.9 8.3 %copy-start.11 = (f32[768]{0:T(1024)S(1)}, f32[768]{0:T(1024)}, u32[]{:S(2)}) copy-start(f32[768]{0:T(1024)} %param.19) | copy-start | bytes 9220
  61.9 8.4 %copy-start = (f32[2,16,32,548]{3,2,1,0:T(8,128)S(1)}, f32[2,16,32,548]{3,2,1,0:T(8,128)}, u32[]{:S(2)}) copy-start(f32[2,16,32,548]{3,2,1,0:T(8,128)} %base_ref.3) | copy-start | bytes 6733828
  75.8 1.1 copy-start.6
  77.0 7.4 %copy-start.9 = (s32[32,616]{1,0:T(8,128)S(1)}, s32[32,616]{1,0:T(8,128)}, u32[]{:S(2)}) copy-start(s32[32,616]{1,0:T(8,128)} %mask_ref.1) | copy-start | bytes 236548
  82.0 1.1 copy-start.1
  83.1 1.2 copy-start.3
  84.3 6.2 %copy-start.7 = (f32[512,768]{1,0:T(8,128)S(1)}, f32[512,768]{1,0:T(8,128)}, u32[]{:S(2)}) copy-start(f32[512,768]{1,0:T(8,128)} %copy-done.6) | copy-start | bytes 4718596
  90.5 19.2 %copy-start.4 = (f32[512,768]{1,0:T(8,128)S(1)}, f32[512,768]{1,0:T(8,128)}, u32[]{:S(2)}) copy-start(f32[512,768]{1,0:T(8,128)} %copy-done.3) | copy-start | bytes 4718596
  107.5 23.5 %collective-permute-start.12 = (f32[4,32,548]{2,1,0:T(8,128)S(1)}, f32[4,32,548]{2,1,0:T(8,128)S(1)}, u32[]{:S(2)}, u32[]{:S(2)}) collective-permute-start(f32[4,32,548]{2,1,0:T(8,128)S(1)} %get-tuple-element.65), channel_id=1, source_target_pairs={{0,4},{8,12},{16,20},{24,28},{4,0},{12,8},{20,16},{28,24},{1,5},{9... | collective-permute-start | bytes 841736 | tf_op jit(solution)/shard_map/ppermute | solution.py:456
  107.8 23.1 %collective-permute-start.13 = (f32[4,32,548]{2,1,0:T(8,128)S(1)}, f32[4,32,548]{2,1,0:T(8,128)S(1)}, u32[]{:S(2)}, u32[]{:S(2)}) collective-permute-start(f32[4,32,548]{2,1,0:T(8,128)S(1)} %get-tuple-element.66), channel_id=1, source_target_pairs={{4,8},{12,16},{20,24},{8,4},{16,12},{24,20},{5,9},{13,17},{21,25},... | collective-permute-start | bytes 841736 | tf_op jit(solution)/shard_map/ppermute | solution.py:456
  126.4 19.5 %copy-start.2 = (f32[3,24,40,128]{3,2,1,0:T(8,128)S(1)}, f32[3,24,40,128]{3,2,1,0:T(8,128)}, u32[]{:S(2)}) copy-start(f32[3,24,40,128]{3,2,1,0:T(8,128)} %copy-done.1) | copy-start | bytes 4423684
  126.4 16.8 %collective-permute-start.8 = (f32[4,32,548]{2,1,0:T(8,128)S(1)}, f32[4,32,548]{2,1,0:T(8,128)S(1)}, u32[]{:S(2)}, u32[]{:S(2)}) collective-permute-start(f32[4,32,548]{2,1,0:T(8,128)S(1)} %get-tuple-element.57), channel_id=1, source_target_pairs={{0,4},{8,12},{16,20},{24,28},{4,0},{12,8},{20,16},{28,24},{1,5},{9... | collective-permute-start | bytes 841736 | tf_op jit(solution)/shard_map/ppermute | solution.py:456
  128.9 14.3 %collective-permute-start.9 = (f32[4,32,548]{2,1,0:T(8,128)S(1)}, f32[4,32,548]{2,1,0:T(8,128)S(1)}, u32[]{:S(2)}, u32[]{:S(2)}) collective-permute-start(f32[4,32,548]{2,1,0:T(8,128)S(1)} %get-tuple-element.58), channel_id=1, source_target_pairs={{4,8},{12,16},{20,24},{8,4},{16,12},{24,20},{5,9},{13,17},{21,25},... | collective-permute-start | bytes 841736 | tf_op jit(solution)/shard_map/ppermute | solution.py:456
  131.6 14.4 %collective-permute-start.14 = (f32[24,4,548]{2,1,0:T(4,128)S(1)}, f32[24,4,548]{2,1,0:T(4,128)S(1)}, u32[]{:S(2)}, u32[]{:S(2)}) collective-permute-start(f32[24,4,548]{2,1,0:T(4,128)S(1)} %get-tuple-element.69), channel_id=1, source_target_pairs={{0,1},{2,3},{1,0},{3,2},{4,5},{6,7},{5,4},{7,6},{8,9},{10,11},{9,8... | collective-permute-start | bytes 631304 | tf_op jit(solution)/shard_map/ppermute | solution.py:456
  131.7 14.3 %collective-permute-start.15 = (f32[24,4,548]{2,1,0:T(4,128)S(1)}, f32[24,4,548]{2,1,0:T(4,128)S(1)}, u32[]{:S(2)}, u32[]{:S(2)}) collective-permute-start(f32[24,4,548]{2,1,0:T(4,128)S(1)} %get-tuple-element.70), channel_id=1, source_target_pairs={{1,2},{2,1},{5,6},{6,5},{9,10},{10,9},{13,14},{14,13},{17,18},{18,... | collective-permute-start | bytes 631304 | tf_op jit(solution)/shard_map/ppermute | solution.py:456
  143.8 6.5 %collective-permute-start.10 = (f32[24,4,548]{2,1,0:T(4,128)S(1)}, f32[24,4,548]{2,1,0:T(4,128)S(1)}, u32[]{:S(2)}, u32[]{:S(2)}) collective-permute-start(f32[24,4,548]{2,1,0:T(4,128)S(1)} %get-tuple-element.61), channel_id=1, source_target_pairs={{0,1},{2,3},{1,0},{3,2},{4,5},{6,7},{5,4},{7,6},{8,9},{10,11},{9,8... | collective-permute-start | bytes 631304 | tf_op jit(solution)/shard_map/ppermute | solution.py:456
  143.9 7.5 %collective-permute-start.11 = (f32[24,4,548]{2,1,0:T(4,128)S(1)}, f32[24,4,548]{2,1,0:T(4,128)S(1)}, u32[]{:S(2)}, u32[]{:S(2)}) collective-permute-start(f32[24,4,548]{2,1,0:T(4,128)S(1)} %get-tuple-element.62), channel_id=1, source_target_pairs={{1,2},{2,1},{5,6},{6,5},{9,10},{10,9},{13,14},{14,13},{17,18},{18,... | collective-permute-start | bytes 631304 | tf_op jit(solution)/shard_map/ppermute | solution.py:456

commit v6 on v5

--- a/solution.py
+++ b/solution.py
@@ -38,6 +38,17 @@
 def halves(size):
     half = size // 2
     return [pl.ds(0, half), pl.ds(half, half)] if half % 16 == 0 else [pl.ds(0, size)]
+
+
+def each_half(size, work):
+    parts = halves(size)
+    step = parts[0].size
+
+    def run(k, _):
+        work(pl.ds(pl.multiple_of(k * step, step), step))
+        return 0
+
+    lax.fori_loop(0, len(parts), run, 0)
 
 
 def iota(shape, axis):
@@ -121,9 +132,12 @@
     send(first, first_out)
     rows = up(raw[0].shape[1], LANES)
     stack[3, :, rows:, :] = jnp.zeros((2,) + (stack.shape[2] - rows, stack.shape[3]), BF)
-    for part in halves(rows):
+
+    def half(part):
         got = mm3(turned[0, part, :], turned[1, part, :], first[0], first[1])
         stack[3, 0, part, :], stack[3, 1, part, :] = split(got)
+
+    each_half(rows, half)
     send(stack.at[3], stack_out.at[3])
     for k in range(3):
         fetch[k + 2].wait()
@@ -277,10 +291,13 @@
     lax.fori_loop(0, ext.shape[2] // LANES, chunk, 0)
     deep = ext.shape[2]
     fetch.wait()
-    for part in halves(out_ref.shape[0]):
+
+    def half(part):
         out_ref[part, :] = mm3(
             high_ref[part, :], low_ref[part, :], both[0, :deep], both[1, :deep]
         )
+
+    each_half(out_ref.shape[0], half)
 
 
 def hidden_kernel(
@@ -324,30 +341,22 @@
     for k, piece in enumerate(pieces):
         here = pl.ds(k * LANES, LANES)
         high_ref[:, here], low_ref[:, here] = split(piece)
-    parts = halves(slots)
     fetch_first.wait()
-    for part in parts:
+    fetch_second.wait()
+
+    def both_layers(part):
         got = mm3(high_ref[part, :deep], low_ref[part, :deep], first[0, :deep], first[1, :deep])
         hidden = jnp.tanh(got + b1_ref[...])
         s1_ref[part, :] = 1.0 - hidden * hidden
         high, low = split(hidden)
-        high_ref[part, :] = high
-        low_ref[part, :] = low
-    fetch_second.wait()
-    for part in parts:
-        got = mm3(high_ref[part, :], low_ref[part, :], second[0], second[1])
+        got = mm3(high, low, second[0], second[1])
         hidden = jnp.tanh(got + b2_ref[...])
         s2_ref[part, :] = 1.0 - hidden * hidden
 
-
-LAYERS = ((0, 0, 1), (1, 1, 2), (2, 0, 2), (1, 0, 1), (0, 1, 0))
-
-
-def table(values, layer):
-    value = jnp.int32(values[0])
-    for k in range(1, len(values)):
-        value = jnp.where(layer == k, values[k], value)
-    return value
+    each_half(slots, both_layers)
+
+
+LAYERS = ((0, NN, 1), (1, NT, 2), (2, NN, 2), (1, NN, 1), (0, NT, 0))
 
 
 def net_kernel(
@@ -374,51 +383,40 @@
     acc_low[...] = pick(one_ref[second, :])
     close(acc_top, 0, first, top)
     fetch[0].wait()
-    scales = [0] + [entry[2] for entry in LAYERS]
-
-    def step(layer, _):
-        for k in (1, 2):
-
-            @pl.when(layer == k)
-            def _():
-                fetch[k].wait()
-
-        weight = table([entry[0] for entry in LAYERS], layer)
-        turned = table([entry[1] for entry in LAYERS], layer)
-        before, after = table(scales[:-1], layer), table(scales[1:], layer)
-
-        def run(dims):
-            acc_top[...] = mm3(top[0], top[1], stack[weight, 0], stack[weight, 1], dims)
-            close(acc_low, before, second, low)
-            acc_low[...] = mm3(low[0], low[1], stack[weight, 0], stack[weight, 1], dims)
-            close(acc_top, after, first, top)
-
-        @pl.when(turned == 0)
-        def _():
-            run(NN)
-
-        @pl.when(turned == 1)
-        def _():
-            run(NT)
-
-        return 0
-
-    lax.fori_loop(0, len(LAYERS), step, 0)
-    close(acc_low, scales[-1], second, low)
-    for part in halves(one_t_ref.shape[0]):
+    before = 0
+    for layer, (weight, dims, scale) in enumerate(LAYERS):
+        if layer in (1, 2):
+            fetch[layer].wait()
+        acc_top[...] = mm3(top[0], top[1], stack[weight, 0], stack[weight, 1], dims)
+        close(acc_low, before, second, low)
+        acc_low[...] = mm3(low[0], low[1], stack[weight, 0], stack[weight, 1], dims)
+        close(acc_top, scale, first, top)
+        before = scale
+    close(acc_low, before, second, low)
+
+    def scatter(part):
         got = mm(one_t_ref[part, :half], top[0]) + mm(one_t_ref[part, :half], top[1])
         got = got + mm(one_t_ref[part, half:], low[0]) + mm(one_t_ref[part, half:], low[1])
         x1[0, part, :], x1[1, part, :] = split(got)
+
+    each_half(one_t_ref.shape[0], scatter)
     fetch[3].wait()
     rows, wide, levels = out_ref.shape
-    for k, part in enumerate(halves(rows * wide)):
+    parts = halves(rows * wide)
+    size = parts[0].size
+    tall = size // wide
+
+    def place(k, _):
+        part = pl.ds(pl.multiple_of(k * size, size), size)
         got = mm3(x1[0, part, :], x1[1, part, :], stack[3, 0], stack[3, 1], NT)
-        tall = got.shape[0] // wide
         got = got.reshape(tall, wide, got.shape[1])[:, :, :levels]
         here = pl.ds(k * tall, tall)
         out_ref[here] = got
         yhead[here] = got[:, :SWEEPS]
         ytail[here] = got[:, wide - SWEEPS :]
+        return 0
+
+    lax.fori_loop(0, len(parts), place, 0)
     even = side_ref[0] == 0
     head, tail = out_ref[:SWEEPS], out_ref[rows - SWEEPS :]
     xa[...] = jnp.where(even, tail, head)

time: 157 us -> 159 us (1.013)
  Pallas kernels: 75.9 us -> 77.8 us
    pallas_call x1, Pallas kernels: 6.2 us -> 7.95 us  [body(): call(functools.partial(hidden_kernel, mark, bucket), [shaped((3, slots, s...]
where the time goes in v6:
time: 159 us; the launch traced here: 158 us
  Pallas kernels  77.8 us (49%)
  waiting for transfers between devices  40 us (25%)
  starting transfers between devices  33.5 us (21%)
  local copies, waits for them, and re-layouts  4.74 us (3%)
    ppermute x16, waiting for transfers between devices, swap(): return lax.ppermute(value, axis, pairs + [(j, i) for i, j in pairs])  40 us
    pallas_call x2, Pallas kernels, body(): call(net_kernel, [shaped((tile_x, tile_y, levels))] + [shaped((SWEEPS, ti...  33.2 us
    ppermute x16, starting transfers between devices, swap(): return lax.ppermute(value, axis, pairs + [(j, i) for i, j in pairs])  27.1 us
    pallas_call x2, Pallas kernels, body(): call(functools.partial(diffuse_kernel, v), [shaped((cells, side))] + [sha...  10.7 us
    pallas_call x2, Pallas kernels, body(): call(functools.partial(finish_kernel, v), pltpu.HBM(vectors.shape, F32),...  8.66 us
    pallas_call x1, Pallas kernels, body(): call(prep_kernel, [pltpu.HBM((2, full_l, side), BF), pltpu.HBM((4, 2, sid...  8.62 us
    pallas_call x1, Pallas kernels, body(): call(functools.partial(hidden_kernel, mark, bucket), [shaped((3, slots, s...  7.95 us
    all_to_all x1, starting transfers between devices, body(): lax.all_to_all(packed if tight else packed.reshape(devices, bucket, deep)...  6.38 us
  transfers between devices with their start and end apart: 17, of which 3 were waited for; matrix products, arithmetic and copies ran while one was open for 0% of the time, Pallas kernels for 30%

profile of v6, /device:TPU:9, one launch (start us, length us, event | category | flops | bytes accessed | tf_op | source)
XLA Modules:
  0.0 158.1 jit_solution(9948862268363864412)
XLA Ops:
  0.7 0.7 fusion.6
  1.4 1.2 copy-done.8
  2.6 2.3 %shard_map.134 = f32[32,72,128]{2,1,0:T(8,128)} custom-call(s32[1,512]{1,0:T(1,128)S(1)} %bitcast.9, f32[1,512]{1,0:T(1,128)S(1)} %bitcast.8, f32[548,512]{1,0:T(8,128)S(1)} %bitcast.10), custom_call_target="tpu_custom_call" | custom-call | flops 1006632960 | bytes 2621440 | tf_op jit(solution)/shard_map/pallas_call | solution.py:525
  4.9 6.4 %all-to-all-start = ((f32[32,72,128]{2,1,0:T(8,128)}), f32[32,72,128]{2,1,0:T(8,128)}, u32[]{:S(2)}, u32[]{:S(2)}) async-start(f32[32,72,128]{2,1,0:T(8,128)} %shard_map.134), calls=%async_computation | async-start | bytes 2359296 | tf_op jit(solution)/shard_map/all_to_all | solution.py:533
  11.4 1.9 %shard_map.127 = (f32[4,32,549]{2,1,0:T(8,128)S(1)}, f32[4,32,549]{2,1,0:T(8,128)S(1)}, f32[16,4,549]{2,1,0:T(4,128)S(1)}, f32[16,4,549]{2,1,0:T(4,128)S(1)}) custom-call(s32[2]{0:T(128)S(1)} %pad_add_fusion.side_ref, f32[2,16,32,548]{3,2,1,0:T(8,128)} %base_ref.3, f32[16,32]{1,0:T(8,128)S(1)} %copy-done.5), custom_call_target="tpu_custom_call" | custom-call | bytes 2244608 | tf_op jit(solution)/shard_map/pallas_call | solution.py:502
  13.3 1.2 collective-permute-start
  14.6 2.0 %collective-permute-start.1 = (f32[4,32,549]{2,1,0:T(8,128)S(1)}, f32[4,32,549]{2,1,0:T(8,128)S(1)}, u32[]{:S(2)}, u32[]{:S(2)}) collective-permute-start(f32[4,32,549]{2,1,0:T(8,128)S(1)} %get-tuple-element.39), channel_id=1, source_target_pairs={{4,8},{12,16},{20,24},{8,4},{16,12},{24,20},{5,9},{13,17},{21,25},... | collective-permute-start | bytes 843272 | tf_op jit(solution)/shard_map/ppermute | solution.py:454
  16.6 1.9 %shard_map.131 = (f32[4,32,548]{2,1,0:T(8,128)S(1)}, f32[4,32,548]{2,1,0:T(8,128)S(1)}, f32[16,4,548]{2,1,0:T(4,128)S(1)}, f32[16,4,548]{2,1,0:T(4,128)S(1)}) custom-call(s32[2]{0:T(128)S(1)} %pad_add_fusion.side_ref, f32[2,16,32,548]{3,2,1,0:T(8,128)} %base_ref.3, f32[16,32]{1,0:T(8,128)S(1)} %copy-done.5), custom_call_target="tpu_custom_call" | custom-call | bytes 2244608 | tf_op jit(solution)/shard_map/pallas_call | solution.py:502
  18.5 2.3 %collective-permute-start.4 = (f32[4,32,548]{2,1,0:T(8,128)S(1)}, f32[4,32,548]{2,1,0:T(8,128)S(1)}, u32[]{:S(2)}, u32[]{:S(2)}) collective-permute-start(f32[4,32,548]{2,1,0:T(8,128)S(1)} %get-tuple-element.46), channel_id=1, source_target_pairs={{0,4},{8,12},{16,20},{24,28},{4,0},{12,8},{20,16},{28,24},{1,5},{9... | collective-permute-start | bytes 841736 | tf_op jit(solution)/shard_map/ppermute | solution.py:454
  20.8 1.9 %collective-permute-start.5 = (f32[4,32,548]{2,1,0:T(8,128)S(1)}, f32[4,32,548]{2,1,0:T(8,128)S(1)}, u32[]{:S(2)}, u32[]{:S(2)}) collective-permute-start(f32[4,32,548]{2,1,0:T(8,128)S(1)} %get-tuple-element.47), channel_id=1, source_target_pairs={{4,8},{12,16},{20,24},{8,4},{16,12},{24,20},{5,9},{13,17},{21,25},... | collective-permute-start | bytes 841736 | tf_op jit(solution)/shard_map/ppermute | solution.py:454
  22.8 31.1 %collective-permute-done.4.ra.refs_0_ = f32[4,32,548]{2,1,0:T(8,128)S(1)} collective-permute-done((f32[4,32,548]{2,1,0:T(8,128)S(1)}, f32[4,32,548]{2,1,0:T(8,128)S(1)}, u32[]{:S(2)}, u32[]{:S(2)}) %collective-permute-start.4) | collective-permute-done | bytes 280608 | tf_op jit(solution)/shard_map/ppermute | solution.py:454
  54.5 1.0 collective-permute-start.6
  55.6 3.0 %collective-permute-start.7 = (f32[24,4,548]{2,1,0:T(4,128)S(1)}, f32[24,4,548]{2,1,0:T(4,128)S(1)}, u32[]{:S(2)}, u32[]{:S(2)}) collective-permute-start(f32[24,4,548]{2,1,0:T(4,128)S(1)} %get-tuple-element.51), channel_id=1, source_target_pairs={{1,2},{2,1},{5,6},{6,5},{9,10},{10,9},{13,14},{14,13},{17,18},{18,... | collective-permute-start | bytes 631304 | tf_op jit(solution)/shard_map/ppermute | solution.py:454
  59.3 2.6 %collective-permute-start.3 = (f32[24,4,549]{2,1,0:T(4,128)S(1)}, f32[24,4,549]{2,1,0:T(4,128)S(1)}, u32[]{:S(2)}, u32[]{:S(2)}) collective-permute-start(f32[24,4,549]{2,1,0:T(4,128)S(1)} %get-tuple-element.43), channel_id=1, source_target_pairs={{1,2},{2,1},{5,6},{6,5},{9,10},{10,9},{13,14},{14,13},{17,18},{18,... | collective-permute-start | bytes 632456 | tf_op jit(solution)/shard_map/ppermute | solution.py:454
  61.9 8.6 %shard_map.129 = (bf16[2,768,768]{2,1,0:T(8,128)(2,1)}, bf16[4,2,768,768]{3,2,1,0:T(8,128)(2,1)}) custom-call(f32[548,548]{1,0:T(8,128)} %refs_0_.1, f32[548,768]{1,0:T(8,128)} %refs_1_.1, f32[768,768]{1,0:T(8,128)} %refs_2_.1, f32[616,768]{1,0:T(8,128)} %bitcast.11, f32[616,616]{1,0:T(8,128)} %refs_4_.1), custom_call_target="tpu_custom_call" | custom-call | flops 2717908992 | bytes 23592960 | tf_op jit(solution)/shard_map/pallas_call | solution.py:540
  70.6 5.5 %shard_map.130 = (f32[512,768]{1,0:T(8,128)S(1)}, f32[3,24,40,128]{3,2,1,0:T(8,128)S(1)}) custom-call(s32[2]{0:T(128)S(1)} %pad_add_fusion.side_ref, f32[2,16,32,548]{3,2,1,0:T(8,128)S(1)} %copy-done, f32[16,32]{1,0:T(8,128)S(1)} %copy-done.5, f32[4,32,549]{2,1,0:T(8,128)S(1)} %collective-permute-done.ra.refs_0_, ...), custom_call_target="tpu_custom_call" | custom-call | flops 1509949440 | bytes 4915200 | tf_op jit(solution)/shard_map/pallas_call | solution.py:562
  76.2 1.1 copy-done.6
  77.3 5.2 %shard_map.133.q_ref = f32[512,768]{1,0:T(8,128)S(1)} custom-call(s32[2]{0:T(128)S(1)} %pad_add_fusion.side_ref, f32[2,16,32,548]{3,2,1,0:T(8,128)S(1)} %copy-done, f32[3,24,40,128]{3,2,1,0:T(8,128)S(1)} %get-tuple-element.45.coeff_ref.cb_ref, f32[4,32,548]{2,1,0:T(8,128)S(1)} %collective-permute-done.4.ra.refs_0_, ...), custom_call_target="tpu_custom_call" | custom-call | flops 1509949440 | bytes 4915200 | tf_op jit(solution)/shard_map/pallas_call | solution.py:562
  82.5 1.1 copy-done.1
  83.6 1.2 copy-done.3
  84.8 8.0 %shard_map.135 = (f32[3,512,768]{2,1,0:T(8,128)S(1)}, bf16[512,512]{1,0:T(8,128)(2,1)S(1)}, bf16[512,512]{1,0:T(8,128)(2,1)S(1)}) custom-call(f32[32,72,128]{2,1,0:T(8,128)} %all-to-all-done.x_ref, bf16[2,768,768]{2,1,0:T(8,128)(2,1)} %get-tuple-element.52.first_ref, f32[1,768]{1,0:T(1,128)S(1)} %broadcast_in_dim.16.b1_ref, ...), custom_call_target="tpu_custom_call" | custom-call | flops 3623878656 | bytes 3145728 | tf_op jit(solution)/shard_map/pallas_call | solution.py:583
  92.8 16.6 %shard_map.138 = (f32[16,32,548]{2,1,0:T(8,128)S(1)}, f32[4,32,548]{2,1,0:T(8,128)S(1)}, f32[4,32,548]{2,1,0:T(8,128)S(1)}, f32[16,4,548]{2,1,0:T(4,128)S(1)}, f32[16,4,548]{2,1,0:T(4,128)S(1)}) custom-call(s32[2]{0:T(128)S(1)} %pad_add_fusion.side_ref, f32[512,768]{1,0:T(8,128)S(1)} %copy-done.7, bf16[512,512]{1,0:T(8,128)(2,1)S(1)} %get-tuple-element.53.one_ref, ...), custom_call_target="tpu_custom_call" | custom-call | flops 10871635968 | bytes 11796480 | tf_op jit(solution)/shard_map/pallas_call | solution.py:601
  109.8 2.1 %collective-permute-start.13 = (f32[4,32,548]{2,1,0:T(8,128)S(1)}, f32[4,32,548]{2,1,0:T(8,128)S(1)}, u32[]{:S(2)}, u32[]{:S(2)}) collective-permute-start(f32[4,32,548]{2,1,0:T(8,128)S(1)} %get-tuple-element.66), channel_id=1, source_target_pairs={{4,8},{12,16},{20,24},{8,4},{16,12},{24,20},{5,9},{13,17},{21,25},... | collective-permute-start | bytes 841736 | tf_op jit(solution)/shard_map/ppermute | solution.py:454
  111.9 16.6 %shard_map.136 = (f32[16,32,548]{2,1,0:T(8,128)S(1)}, f32[4,32,548]{2,1,0:T(8,128)S(1)}, f32[4,32,548]{2,1,0:T(8,128)S(1)}, f32[16,4,548]{2,1,0:T(4,128)S(1)}, f32[16,4,548]{2,1,0:T(4,128)S(1)}) custom-call(s32[2]{0:T(128)S(1)} %pad_add_fusion.side_ref, f32[512,768]{1,0:T(8,128)S(1)} %copy-done.4, bf16[512,512]{1,0:T(8,128)(2,1)S(1)} %get-tuple-element.53.one_ref, ...), custom_call_target="tpu_custom_call" | custom-call | flops 10871635968 | bytes 11796480 | tf_op jit(solution)/shard_map/pallas_call | solution.py:601
  128.5 2.4 %collective-permute-start.8 = (f32[4,32,548]{2,1,0:T(8,128)S(1)}, f32[4,32,548]{2,1,0:T(8,128)S(1)}, u32[]{:S(2)}, u32[]{:S(2)}) collective-permute-start(f32[4,32,548]{2,1,0:T(8,128)S(1)} %get-tuple-element.57), channel_id=1, source_target_pairs={{0,4},{8,12},{16,20},{24,28},{4,0},{12,8},{20,16},{28,24},{1,5},{9... | collective-permute-start | bytes 841736 | tf_op jit(solution)/shard_map/ppermute | solution.py:454
  131.0 2.0 %collective-permute-start.9 = (f32[4,32,548]{2,1,0:T(8,128)S(1)}, f32[4,32,548]{2,1,0:T(8,128)S(1)}, u32[]{:S(2)}, u32[]{:S(2)}) collective-permute-start(f32[4,32,548]{2,1,0:T(8,128)S(1)} %get-tuple-element.58), channel_id=1, source_target_pairs={{4,8},{12,16},{20,24},{8,4},{16,12},{24,20},{5,9},{13,17},{21,25},... | collective-permute-start | bytes 841736 | tf_op jit(solution)/shard_map/ppermute | solution.py:454
  133.8 3.8 %collective-permute-start.15 = (f32[24,4,548]{2,1,0:T(4,128)S(1)}, f32[24,4,548]{2,1,0:T(4,128)S(1)}, u32[]{:S(2)}, u32[]{:S(2)}) collective-permute-start(f32[24,4,548]{2,1,0:T(4,128)S(1)} %get-tuple-element.70), channel_id=1, source_target_pairs={{1,2},{2,1},{5,6},{6,5},{9,10},{10,9},{13,14},{14,13},{17,18},{18,... | collective-permute-start | bytes 631304 | tf_op jit(solution)/shard_map/ppermute | solution.py:454
  137.6 7.7 %collective-permute-done.8.ra.refs_0_ = f32[4,32,548]{2,1,0:T(8,128)S(1)} collective-permute-done((f32[4,32,548]{2,1,0:T(8,128)S(1)}, f32[4,32,548]{2,1,0:T(8,128)S(1)}, u32[]{:S(2)}, u32[]{:S(2)}) %collective-permute-start.8) | collective-permute-done | bytes 280608 | tf_op jit(solution)/shard_map/ppermute | solution.py:454
  146.0 2.0 %collective-permute-start.11 = (f32[24,4,548]{2,1,0:T(4,128)S(1)}, f32[24,4,548]{2,1,0:T(4,128)S(1)}, u32[]{:S(2)}, u32[]{:S(2)}) collective-permute-start(f32[24,4,548]{2,1,0:T(4,128)S(1)} %get-tuple-element.62), channel_id=1, source_target_pairs={{1,2},{2,1},{5,6},{6,5},{9,10},{10,9},{13,14},{14,13},{17,18},{18,... | collective-permute-start | bytes 631304 | tf_op jit(solution)/shard_map/ppermute | solution.py:454
  148.1 4.3 %shard_map.140.refs_4_ = f32[2,16,32,548]{3,2,1,0:T(8,128)} custom-call(s32[2]{0:T(128)S(1)} %pad_add_fusion.side_ref, f32[16,32,548]{2,1,0:T(8,128)S(1)} %get-tuple-element.64.field_ref, f32[2,16,32,548]{3,2,1,0:T(8,128)S(1)} %copy-done, f32[3,24,40,128]{3,2,1,0:T(8,128)S(1)} %copy-done.2, f32[4,32,548]{2,1,0:T(8,128)S(1)} %collective-permute-done.12.ra.refs_0_, ...), custom_call_target="tpu_custom_call" | custom-call | flops 24576000 | bytes 3932160 | tf_op jit(solution)/shard_map/pallas_call | solution.py:624
  152.4 1.1 collective-permute-done.11.refs_3_
  153.5 4.3 %shard_map.141 = f32[2,16,32,548]{3,2,1,0:T(8,128)} custom-call(s32[2]{0:T(128)S(1)} %pad_add_fusion.side_ref, f32[16,32,548]{2,1,0:T(8,128)S(1)} %get-tuple-element.56.field_ref, f32[2,16,32,548]{3,2,1,0:T(8,128)S(1)} %copy-done, f32[3,24,40,128]{3,2,1,0:T(8,128)S(1)} %copy-done.2, ...), custom_call_target="tpu_custom_call", output_to_operand_aliasing={{}: (8, {})} | custom-call | flops 24576000 | bytes 3932160 | tf_op jit(solution)/shard_map/pallas_call | solution.py:624
  (45 shorter events, 3.2 us)
Async XLA Ops:
  1.4 1.3 copy-start.8
  4.9 6.5 %copy-start.5 = (f32[16,32]{1,0:T(8,128)S(1)}, f32[16,32]{1,0:T(8,128)}, u32[]{:S(2)}) copy-start(f32[16,32]{1,0:T(8,128)} %coeff_ref.5) | copy-start | bytes 6148
  4.9 79.9 %all-to-all-start = ((f32[32,72,128]{2,1,0:T(8,128)}), f32[32,72,128]{2,1,0:T(8,128)}, u32[]{:S(2)}, u32[]{:S(2)}) async-start(f32[32,72,128]{2,1,0:T(8,128)} %shard_map.134), calls=%async_computation | async-start | bytes 2359296 | tf_op jit(solution)/shard_map/all_to_all | solution.py:533
  13.3 45.3 %collective-permute-start = (f32[4,32,549]{2,1,0:T(8,128)S(1)}, f32[4,32,549]{2,1,0:T(8,128)S(1)}, u32[]{:S(2)}, u32[]{:S(2)}) collective-permute-start(f32[4,32,549]{2,1,0:T(8,128)S(1)} %get-tuple-element.38), channel_id=1, source_target_pairs={{0,4},{8,12},{16,20},{24,28},{4,0},{12,8},{20,16},{28,24},{1,5},{9... | collective-permute-start | bytes 843272 | tf_op jit(solution)/shard_map/ppermute | solution.py:454
  14.6 44.0 %collective-permute-start.1 = (f32[4,32,549]{2,1,0:T(8,128)S(1)}, f32[4,32,549]{2,1,0:T(8,128)S(1)}, u32[]{:S(2)}, u32[]{:S(2)}) collective-permute-start(f32[4,32,549]{2,1,0:T(8,128)S(1)} %get-tuple-element.39), channel_id=1, source_target_pairs={{4,8},{12,16},{20,24},{8,4},{16,12},{24,20},{5,9},{13,17},{21,25},... | collective-permute-start | bytes 843272 | tf_op jit(solution)/shard_map/ppermute | solution.py:454
  18.5 35.4 %collective-permute-start.4 = (f32[4,32,548]{2,1,0:T(8,128)S(1)}, f32[4,32,548]{2,1,0:T(8,128)S(1)}, u32[]{:S(2)}, u32[]{:S(2)}) collective-permute-start(f32[4,32,548]{2,1,0:T(8,128)S(1)} %get-tuple-element.46), channel_id=1, source_target_pairs={{0,4},{8,12},{16,20},{24,28},{4,0},{12,8},{20,16},{28,24},{1,5},{9... | collective-permute-start | bytes 841736 | tf_op jit(solution)/shard_map/ppermute | solution.py:454
  20.8 33.1 %collective-permute-start.5 = (f32[4,32,548]{2,1,0:T(8,128)S(1)}, f32[4,32,548]{2,1,0:T(8,128)S(1)}, u32[]{:S(2)}, u32[]{:S(2)}) collective-permute-start(f32[4,32,548]{2,1,0:T(8,128)S(1)} %get-tuple-element.47), channel_id=1, source_target_pairs={{4,8},{12,16},{20,24},{8,4},{16,12},{24,20},{5,9},{13,17},{21,25},... | collective-permute-start | bytes 841736 | tf_op jit(solution)/shard_map/ppermute | solution.py:454
  54.5 22.7 %collective-permute-start.6 = (f32[24,4,548]{2,1,0:T(4,128)S(1)}, f32[24,4,548]{2,1,0:T(4,128)S(1)}, u32[]{:S(2)}, u32[]{:S(2)}) collective-permute-start(f32[24,4,548]{2,1,0:T(4,128)S(1)} %get-tuple-element.50), channel_id=1, source_target_pairs={{0,1},{2,3},{1,0},{3,2},{4,5},{6,7},{5,4},{7,6},{8,9},{10,11},{9,8... | collective-permute-start | bytes 631304 | tf_op jit(solution)/shard_map/ppermute | solution.py:454
  55.6 21.7 %collective-permute-start.7 = (f32[24,4,548]{2,1,0:T(4,128)S(1)}, f32[24,4,548]{2,1,0:T(4,128)S(1)}, u32[]{:S(2)}, u32[]{:S(2)}) collective-permute-start(f32[24,4,548]{2,1,0:T(4,128)S(1)} %get-tuple-element.51), channel_id=1, source_target_pairs={{1,2},{2,1},{5,6},{6,5},{9,10},{10,9},{13,14},{14,13},{17,18},{18,... | collective-permute-start | bytes 631304 | tf_op jit(solution)/shard_map/ppermute | solution.py:454
  59.2 11.4 %collective-permute-start.2 = (f32[24,4,549]{2,1,0:T(4,128)S(1)}, f32[24,4,549]{2,1,0:T(4,128)S(1)}, u32[]{:S(2)}, u32[]{:S(2)}) collective-permute-start(f32[24,4,549]{2,1,0:T(4,128)S(1)} %get-tuple-element.42), channel_id=1, source_target_pairs={{0,1},{2,3},{1,0},{3,2},{4,5},{6,7},{5,4},{7,6},{8,9},{10,11},{9,8... | collective-permute-start | bytes 632456 | tf_op jit(solution)/shard_map/ppermute | solution.py:454
  59.3 11.3 %collective-permute-start.3 = (f32[24,4,549]{2,1,0:T(4,128)S(1)}, f32[24,4,549]{2,1,0:T(4,128)S(1)}, u32[]{:S(2)}, u32[]{:S(2)}) collective-permute-start(f32[24,4,549]{2,1,0:T(4,128)S(1)} %get-tuple-element.43), channel_id=1, source_target_pairs={{1,2},{2,1},{5,6},{6,5},{9,10},{10,9},{13,14},{14,13},{17,18},{18,... | collective-permute-start | bytes 632456 | tf_op jit(solution)/shard_map/ppermute | solution.py:454
  61.9 8.7 %copy-start.10 = (f32[768]{0:T(1024)S(1)}, f32[768]{0:T(1024)}, u32[]{:S(2)}) copy-start(f32[768]{0:T(1024)} %param.17) | copy-start | bytes 9220
  61.9 8.7 %copy-start.11 = (f32[768]{0:T(1024)S(1)}, f32[768]{0:T(1024)}, u32[]{:S(2)}) copy-start(f32[768]{0:T(1024)} %param.19) | copy-start | bytes 9220
  61.9 8.7 %copy-start = (f32[2,16,32,548]{3,2,1,0:T(8,128)S(1)}, f32[2,16,32,548]{3,2,1,0:T(8,128)}, u32[]{:S(2)}) copy-start(f32[2,16,32,548]{3,2,1,0:T(8,128)} %base_ref.3) | copy-start | bytes 6733828
  76.2 1.1 copy-start.6
  77.3 7.5 %copy-start.9 = (s32[32,616]{1,0:T(8,128)S(1)}, s32[32,616]{1,0:T(8,128)}, u32[]{:S(2)}) copy-start(s32[32,616]{1,0:T(8,128)} %mask_ref.1) | copy-start | bytes 236548
  82.5 1.1 copy-start.1
  83.6 1.2 copy-start.3
  84.8 8.0 %copy-start.7 = (f32[512,768]{1,0:T(8,128)S(1)}, f32[512,768]{1,0:T(8,128)}, u32[]{:S(2)}) copy-start(f32[512,768]{1,0:T(8,128)} %copy-done.6) | copy-start | bytes 4718596
  92.8 19.1 %copy-start.4 = (f32[512,768]{1,0:T(8,128)S(1)}, f32[512,768]{1,0:T(8,128)}, u32[]{:S(2)}) copy-start(f32[512,768]{1,0:T(8,128)} %copy-done.3) | copy-start | bytes 4718596
  109.4 23.6 %collective-permute-start.12 = (f32[4,32,548]{2,1,0:T(8,128)S(1)}, f32[4,32,548]{2,1,0:T(8,128)S(1)}, u32[]{:S(2)}, u32[]{:S(2)}) collective-permute-start(f32[4,32,548]{2,1,0:T(8,128)S(1)} %get-tuple-element.65), channel_id=1, source_target_pairs={{0,4},{8,12},{16,20},{24,28},{4,0},{12,8},{20,16},{28,24},{1,5},{9... | collective-permute-start | bytes 841736 | tf_op jit(solution)/shard_map/ppermute | solution.py:454
  109.8 23.3 %collective-permute-start.13 = (f32[4,32,548]{2,1,0:T(8,128)S(1)}, f32[4,32,548]{2,1,0:T(8,128)S(1)}, u32[]{:S(2)}, u32[]{:S(2)}) collective-permute-start(f32[4,32,548]{2,1,0:T(8,128)S(1)} %get-tuple-element.66), channel_id=1, source_target_pairs={{4,8},{12,16},{20,24},{8,4},{16,12},{24,20},{5,9},{13,17},{21,25},... | collective-permute-start | bytes 841736 | tf_op jit(solution)/shard_map/ppermute | solution.py:454
  128.5 19.5 %copy-start.2 = (f32[3,24,40,128]{3,2,1,0:T(8,128)S(1)}, f32[3,24,40,128]{3,2,1,0:T(8,128)}, u32[]{:S(2)}) copy-start(f32[3,24,40,128]{3,2,1,0:T(8,128)} %copy-done.1) | copy-start | bytes 4423684
  128.5 16.8 %collective-permute-start.8 = (f32[4,32,548]{2,1,0:T(8,128)S(1)}, f32[4,32,548]{2,1,0:T(8,128)S(1)}, u32[]{:S(2)}, u32[]{:S(2)}) collective-permute-start(f32[4,32,548]{2,1,0:T(8,128)S(1)} %get-tuple-element.57), channel_id=1, source_target_pairs={{0,4},{8,12},{16,20},{24,28},{4,0},{12,8},{20,16},{28,24},{1,5},{9... | collective-permute-start | bytes 841736 | tf_op jit(solution)/shard_map/ppermute | solution.py:454
  131.0 14.3 %collective-permute-start.9 = (f32[4,32,548]{2,1,0:T(8,128)S(1)}, f32[4,32,548]{2,1,0:T(8,128)S(1)}, u32[]{:S(2)}, u32[]{:S(2)}) collective-permute-start(f32[4,32,548]{2,1,0:T(8,128)S(1)} %get-tuple-element.58), channel_id=1, source_target_pairs={{4,8},{12,16},{20,24},{8,4},{16,12},{24,20},{5,9},{13,17},{21,25},... | collective-permute-start | bytes 841736 | tf_op jit(solution)/shard_map/ppermute | solution.py:454
  133.7 14.4 %collective-permute-start.14 = (f32[24,4,548]{2,1,0:T(4,128)S(1)}, f32[24,4,548]{2,1,0:T(4,128)S(1)}, u32[]{:S(2)}, u32[]{:S(2)}) collective-permute-start(f32[24,4,548]{2,1,0:T(4,128)S(1)} %get-tuple-element.69), channel_id=1, source_target_pairs={{0,1},{2,3},{1,0},{3,2},{4,5},{6,7},{5,4},{7,6},{8,9},{10,11},{9,8... | collective-permute-start | bytes 631304 | tf_op jit(solution)/shard_map/ppermute | solution.py:454
  133.8 14.3 %collective-permute-start.15 = (f32[24,4,548]{2,1,0:T(4,128)S(1)}, f32[24,4,548]{2,1,0:T(4,128)S(1)}, u32[]{:S(2)}, u32[]{:S(2)}) collective-permute-start(f32[24,4,548]{2,1,0:T(4,128)S(1)} %get-tuple-element.70), channel_id=1, source_target_pairs={{1,2},{2,1},{5,6},{6,5},{9,10},{10,9},{13,14},{14,13},{17,18},{18,... | collective-permute-start | bytes 631304 | tf_op jit(solution)/shard_map/ppermute | solution.py:454
  145.9 6.5 %collective-permute-start.10 = (f32[24,4,548]{2,1,0:T(4,128)S(1)}, f32[24,4,548]{2,1,0:T(4,128)S(1)}, u32[]{:S(2)}, u32[]{:S(2)}) collective-permute-start(f32[24,4,548]{2,1,0:T(4,128)S(1)} %get-tuple-element.61), channel_id=1, source_target_pairs={{0,1},{2,3},{1,0},{3,2},{4,5},{6,7},{5,4},{7,6},{8,9},{10,11},{9,8... | collective-permute-start | bytes 631304 | tf_op jit(solution)/shard_map/ppermute | solution.py:454
  146.0 7.5 %collective-permute-start.11 = (f32[24,4,548]{2,1,0:T(4,128)S(1)}, f32[24,4,548]{2,1,0:T(4,128)S(1)}, u32[]{:S(2)}, u32[]{:S(2)}) collective-permute-start(f32[24,4,548]{2,1,0:T(4,128)S(1)} %get-tuple-element.62), channel_id=1, source_target_pairs={{1,2},{2,1},{5,6},{6,5},{9,10},{10,9},{13,14},{14,13},{17,18},{18,... | collective-permute-start | bytes 631304 | tf_op jit(solution)/shard_map/ppermute | solution.py:454

commit v7 on v5

--- a/solution.py
+++ b/solution.py
@@ -38,6 +38,28 @@
 def halves(size):
     half = size // 2
     return [pl.ds(0, half), pl.ds(half, half)] if half % 16 == 0 else [pl.ds(0, size)]
+
+
+class Fetch:
+    def __init__(self, source, target, sems):
+        half = target.shape[1] // 2
+        self.copies = [
+            pltpu.make_async_copy(
+                source.at[term, pl.ds(k * half, half)],
+                target.at[term, pl.ds(k * half, half)],
+                sems.at[2 * term + k],
+            )
+            for term in range(2)
+            for k in range(2)
+        ]
+
+    def start(self):
+        for copy in self.copies:
+            copy.start()
+
+    def wait(self):
+        for copy in self.copies:
+            copy.wait()
 
 
 def iota(shape, axis):
@@ -244,7 +266,7 @@
     strips, stack_ref, refs = refs[:4], refs[4], refs[5:]
     ext, work, high_ref, low_ref, both, sem = refs[-6:]
     out_ref = refs[0]
-    fetch = pltpu.make_async_copy(stack_ref.at[3], both, sem)
+    fetch = Fetch(stack_ref.at[3], both, sem)
     fetch.start()
     rows, wide, levels = tile_ref.shape[1:]
     fill_levels(ext, side_ref, tile_ref[v], *strips)
@@ -287,12 +309,11 @@
     mark, bucket, x_ref, first_ref, b1_ref, stack_ref, b2_ref, mask_ref,
     scale_ref, one_ref, one_t_ref, high_ref, low_ref, x_buf, first, second, sems,
 ):
-    fetch_x = pltpu.make_async_copy(x_ref, x_buf, sems.at[2])
+    fetch_x = pltpu.make_async_copy(x_ref, x_buf, sems.at[2, 0])
     fetch_x.start()
-    fetch_first = pltpu.make_async_copy(first_ref, first, sems.at[0])
-    fetch_second = pltpu.make_async_copy(stack_ref.at[0], second, sems.at[1])
+    fetch_first = Fetch(first_ref, first, sems.at[0])
+    fetch_second = Fetch(stack_ref.at[0], second, sems.at[1])
     fetch_first.start()
-    fetch_second.start()
     s1_ref, s2_ref, gate_ref = (scale_ref.at[k] for k in range(3))
     slots, cells = one_ref.shape
     devices, channels = mask_ref.shape
@@ -326,6 +347,7 @@
         high_ref[:, here], low_ref[:, here] = split(piece)
     parts = halves(slots)
     fetch_first.wait()
+    fetch_second.start()
     for part in parts:
         got = mm3(high_ref[part, :deep], low_ref[part, :deep], first[0, :deep], first[1, :deep])
         hidden = jnp.tanh(got + b1_ref[...])
@@ -354,11 +376,8 @@
     side_ref, q_ref, one_ref, one_t_ref, scale_ref, stack_ref,
     out_ref, xa, xb, yhead, ytail, x1, top, low, acc_top, acc_low, stack, sems,
 ):
-    fetch = [
-        pltpu.make_async_copy(stack_ref.at[k], stack.at[k], sems.at[k]) for k in range(4)
-    ]
-    for copy in fetch:
-        copy.start()
+    fetch = [Fetch(stack_ref.at[k], stack.at[k], sems.at[k]) for k in range(4)]
+    fetch[0].start()
     slots = q_ref.shape[0]
     half = slots // 2
     first, second = pl.ds(0, half), pl.ds(half, half)
@@ -374,6 +393,7 @@
     acc_low[...] = pick(one_ref[second, :])
     close(acc_top, 0, first, top)
     fetch[0].wait()
+    fetch[1].start()
     scales = [0] + [entry[2] for entry in LAYERS]
 
     def step(layer, _):
@@ -382,6 +402,7 @@
             @pl.when(layer == k)
             def _():
                 fetch[k].wait()
+                fetch[k + 1].start()
 
         weight = table([entry[0] for entry in LAYERS], layer)
         turned = table([entry[1] for entry in LAYERS], layer)
@@ -572,7 +593,7 @@
                 pltpu.VMEM((cells, deep), BF),
                 pltpu.VMEM((cells, deep), BF),
                 pltpu.VMEM((2, side, side), BF),
-                pltpu.SemaphoreType.DMA,
+                pltpu.SemaphoreType.DMA((4,)),
             ],
             vmem=16,
             in_specs=[scalars, whole] + [whole] * 5 + [far],
@@ -591,7 +612,7 @@
         + [
             pltpu.VMEM(packed_shape, F32),
             pltpu.VMEM((2, full_l, side), BF), pltpu.VMEM((2, side, side), BF),
-            pltpu.SemaphoreType.DMA((3,)),
+            pltpu.SemaphoreType.DMA((3, 4)),
         ],
         vmem=18,
         in_specs=[far, far, whole, far, whole, whole],
@@ -612,7 +633,7 @@
                 + [pltpu.VMEM((slots // 2, side), F32)] * 2
                 + [
                     pltpu.VMEM((4, 2, side, side), BF),
-                    pltpu.SemaphoreType.DMA((4,)),
+                    pltpu.SemaphoreType.DMA((4, 4)),
                 ],
                 vmem=22,
                 in_specs=[scalars] + [whole] * 4 + [far],

time: 157 us -> 158 us (level)
  no operation moved by 1% of the time
where the time goes in v7:
time: 158 us; the launch traced here: 156 us
  Pallas kernels  76.3 us (48%)
  waiting for transfers between devices  40 us (25%)
  starting transfers between devices  33.3 us (21%)
  local copies, waits for them, and re-layouts  4.74 us (3%)
    ppermute x16, waiting for transfers between devices, swap(): return lax.ppermute(value, axis, pairs + [(j, i) for i, j in pairs])  40 us
    pallas_call x2, Pallas kernels, body(): call(net_kernel, [shaped((tile_x, tile_y, levels))] + [shaped((SWEEPS, ti...  33.8 us
    ppermute x16, starting transfers between devices, swap(): return lax.ppermute(value, axis, pairs + [(j, i) for i, j in pairs])  26.9 us
    pallas_call x2, Pallas kernels, body(): call(functools.partial(diffuse_kernel, v), [shaped((cells, side))] + [sha...  10.6 us
    pallas_call x2, Pallas kernels, body(): call(functools.partial(finish_kernel, v), pltpu.HBM(vectors.shape, F32),...  8.66 us
    pallas_call x1, Pallas kernels, body(): call(prep_kernel, [pltpu.HBM((2, full_l, side), BF), pltpu.HBM((4, 2, sid...  8.29 us
    all_to_all x1, starting transfers between devices, body(): lax.all_to_all(packed if tight else packed.reshape(devices, bucket, deep)...  6.38 us
    pallas_call x1, Pallas kernels, body(): call(functools.partial(hidden_kernel, mark, bucket), [shaped((3, slots, s...  6.29 us
  transfers between devices with their start and end apart: 17, of which 3 were waited for; matrix products, arithmetic and copies ran while one was open for 0% of the time, Pallas kernels for 30%

profile of v7, /device:TPU:9, one launch (start us, length us, event | category | flops | bytes accessed | tf_op | source)
XLA Modules:
  0.0 156.3 jit_solution(3792155293999721264)
XLA Ops:
  0.7 0.7 fusion.6
  1.4 1.2 copy-done.8
  2.6 2.3 %shard_map.134 = f32[32,72,128]{2,1,0:T(8,128)} custom-call(s32[1,512]{1,0:T(1,128)S(1)} %bitcast.9, f32[1,512]{1,0:T(1,128)S(1)} %bitcast.8, f32[548,512]{1,0:T(8,128)S(1)} %bitcast.10), custom_call_target="tpu_custom_call" | custom-call | flops 1006632960 | bytes 2621440 | tf_op jit(solution)/shard_map/pallas_call | solution.py:548
  4.9 6.4 %all-to-all-start = ((f32[32,72,128]{2,1,0:T(8,128)}), f32[32,72,128]{2,1,0:T(8,128)}, u32[]{:S(2)}, u32[]{:S(2)}) async-start(f32[32,72,128]{2,1,0:T(8,128)} %shard_map.134), calls=%async_computation | async-start | bytes 2359296 | tf_op jit(solution)/shard_map/all_to_all | solution.py:556
  11.4 1.9 %shard_map.127 = (f32[4,32,549]{2,1,0:T(8,128)S(1)}, f32[4,32,549]{2,1,0:T(8,128)S(1)}, f32[16,4,549]{2,1,0:T(4,128)S(1)}, f32[16,4,549]{2,1,0:T(4,128)S(1)}) custom-call(s32[2]{0:T(128)S(1)} %pad_add_fusion.side_ref, f32[2,16,32,548]{3,2,1,0:T(8,128)} %base_ref.3, f32[16,32]{1,0:T(8,128)S(1)} %copy-done.5), custom_call_target="tpu_custom_call" | custom-call | bytes 2244608 | tf_op jit(solution)/shard_map/pallas_call | solution.py:525
  13.3 1.2 collective-permute-start
  14.6 2.0 %collective-permute-start.1 = (f32[4,32,549]{2,1,0:T(8,128)S(1)}, f32[4,32,549]{2,1,0:T(8,128)S(1)}, u32[]{:S(2)}, u32[]{:S(2)}) collective-permute-start(f32[4,32,549]{2,1,0:T(8,128)S(1)} %get-tuple-element.39), channel_id=1, source_target_pairs={{4,8},{12,16},{20,24},{8,4},{16,12},{24,20},{5,9},{13,17},{21,25},... | collective-permute-start | bytes 843272 | tf_op jit(solution)/shard_map/ppermute | solution.py:477
  16.6 1.9 %shard_map.131 = (f32[4,32,548]{2,1,0:T(8,128)S(1)}, f32[4,32,548]{2,1,0:T(8,128)S(1)}, f32[16,4,548]{2,1,0:T(4,128)S(1)}, f32[16,4,548]{2,1,0:T(4,128)S(1)}) custom-call(s32[2]{0:T(128)S(1)} %pad_add_fusion.side_ref, f32[2,16,32,548]{3,2,1,0:T(8,128)} %base_ref.3, f32[16,32]{1,0:T(8,128)S(1)} %copy-done.5), custom_call_target="tpu_custom_call" | custom-call | bytes 2244608 | tf_op jit(solution)/shard_map/pallas_call | solution.py:525
  18.5 2.3 %collective-permute-start.4 = (f32[4,32,548]{2,1,0:T(8,128)S(1)}, f32[4,32,548]{2,1,0:T(8,128)S(1)}, u32[]{:S(2)}, u32[]{:S(2)}) collective-permute-start(f32[4,32,548]{2,1,0:T(8,128)S(1)} %get-tuple-element.46), channel_id=1, source_target_pairs={{0,4},{8,12},{16,20},{24,28},{4,0},{12,8},{20,16},{28,24},{1,5},{9... | collective-permute-start | bytes 841736 | tf_op jit(solution)/shard_map/ppermute | solution.py:477
  20.8 1.9 %collective-permute-start.5 = (f32[4,32,548]{2,1,0:T(8,128)S(1)}, f32[4,32,548]{2,1,0:T(8,128)S(1)}, u32[]{:S(2)}, u32[]{:S(2)}) collective-permute-start(f32[4,32,548]{2,1,0:T(8,128)S(1)} %get-tuple-element.47), channel_id=1, source_target_pairs={{4,8},{12,16},{20,24},{8,4},{16,12},{24,20},{5,9},{13,17},{21,25},... | collective-permute-start | bytes 841736 | tf_op jit(solution)/shard_map/ppermute | solution.py:477
  22.8 31.1 %collective-permute-done.4.ra.refs_0_ = f32[4,32,548]{2,1,0:T(8,128)S(1)} collective-permute-done((f32[4,32,548]{2,1,0:T(8,128)S(1)}, f32[4,32,548]{2,1,0:T(8,128)S(1)}, u32[]{:S(2)}, u32[]{:S(2)}) %collective-permute-start.4) | collective-permute-done | bytes 280608 | tf_op jit(solution)/shard_map/ppermute | solution.py:477
  54.5 1.0 collective-permute-start.6
  55.6 3.0 %collective-permute-start.7 = (f32[24,4,548]{2,1,0:T(4,128)S(1)}, f32[24,4,548]{2,1,0:T(4,128)S(1)}, u32[]{:S(2)}, u32[]{:S(2)}) collective-permute-start(f32[24,4,548]{2,1,0:T(4,128)S(1)} %get-tuple-element.51), channel_id=1, source_target_pairs={{1,2},{2,1},{5,6},{6,5},{9,10},{10,9},{13,14},{14,13},{17,18},{18,... | collective-permute-start | bytes 631304 | tf_op jit(solution)/shard_map/ppermute | solution.py:477
  59.3 2.6 %collective-permute-start.3 = (f32[24,4,549]{2,1,0:T(4,128)S(1)}, f32[24,4,549]{2,1,0:T(4,128)S(1)}, u32[]{:S(2)}, u32[]{:S(2)}) collective-permute-start(f32[24,4,549]{2,1,0:T(4,128)S(1)} %get-tuple-element.43), channel_id=1, source_target_pairs={{1,2},{2,1},{5,6},{6,5},{9,10},{10,9},{13,14},{14,13},{17,18},{18,... | collective-permute-start | bytes 632456 | tf_op jit(solution)/shard_map/ppermute | solution.py:477
  61.9 8.3 %shard_map.129 = (bf16[2,768,768]{2,1,0:T(8,128)(2,1)}, bf16[4,2,768,768]{3,2,1,0:T(8,128)(2,1)}) custom-call(f32[548,548]{1,0:T(8,128)} %refs_0_.1, f32[548,768]{1,0:T(8,128)} %refs_1_.1, f32[768,768]{1,0:T(8,128)} %refs_2_.1, f32[616,768]{1,0:T(8,128)} %bitcast.11, f32[616,616]{1,0:T(8,128)} %refs_4_.1), custom_call_target="tpu_custom_call" | custom-call | flops 2717908992 | bytes 23592960 | tf_op jit(solution)/shard_map/pallas_call | solution.py:563
  70.3 5.6 %shard_map.130 = (f32[512,768]{1,0:T(8,128)S(1)}, f32[3,24,40,128]{3,2,1,0:T(8,128)S(1)}) custom-call(s32[2]{0:T(128)S(1)} %pad_add_fusion.side_ref, f32[2,16,32,548]{3,2,1,0:T(8,128)S(1)} %copy-done, f32[16,32]{1,0:T(8,128)S(1)} %copy-done.5, f32[4,32,549]{2,1,0:T(8,128)S(1)} %collective-permute-done.ra.refs_0_, ...), custom_call_target="tpu_custom_call" | custom-call | flops 1509949440 | bytes 4915200 | tf_op jit(solution)/shard_map/pallas_call | solution.py:585
  75.9 1.1 copy-done.6
  77.0 5.0 %shard_map.133.q_ref = f32[512,768]{1,0:T(8,128)S(1)} custom-call(s32[2]{0:T(128)S(1)} %pad_add_fusion.side_ref, f32[2,16,32,548]{3,2,1,0:T(8,128)S(1)} %copy-done, f32[3,24,40,128]{3,2,1,0:T(8,128)S(1)} %get-tuple-element.45.coeff_ref.cb_ref, f32[4,32,548]{2,1,0:T(8,128)S(1)} %collective-permute-done.4.ra.refs_0_, ...), custom_call_target="tpu_custom_call" | custom-call | flops 1509949440 | bytes 4915200 | tf_op jit(solution)/shard_map/pallas_call | solution.py:585
  82.1 1.1 copy-done.1
  83.2 1.2 copy-done.3
  84.4 6.3 %shard_map.135 = (f32[3,512,768]{2,1,0:T(8,128)S(1)}, bf16[512,512]{1,0:T(8,128)(2,1)S(1)}, bf16[512,512]{1,0:T(8,128)(2,1)S(1)}) custom-call(f32[32,72,128]{2,1,0:T(8,128)} %all-to-all-done.x_ref, bf16[2,768,768]{2,1,0:T(8,128)(2,1)} %get-tuple-element.52.first_ref, f32[1,768]{1,0:T(1,128)S(1)} %broadcast_in_dim.16.b1_ref, ...), custom_call_target="tpu_custom_call" | custom-call | flops 3623878656 | bytes 3145728 | tf_op jit(solution)/shard_map/pallas_call | solution.py:606
  90.7 17.0 %shard_map.138 = (f32[16,32,548]{2,1,0:T(8,128)S(1)}, f32[4,32,548]{2,1,0:T(8,128)S(1)}, f32[4,32,548]{2,1,0:T(8,128)S(1)}, f32[16,4,548]{2,1,0:T(4,128)S(1)}, f32[16,4,548]{2,1,0:T(4,128)S(1)}) custom-call(s32[2]{0:T(128)S(1)} %pad_add_fusion.side_ref, f32[512,768]{1,0:T(8,128)S(1)} %copy-done.7, bf16[512,512]{1,0:T(8,128)(2,1)S(1)} %get-tuple-element.53.one_ref, ...), custom_call_target="tpu_custom_call" | custom-call | flops 10871635968 | bytes 11796480 | tf_op jit(solution)/shard_map/pallas_call | solution.py:624
  108.1 1.9 %collective-permute-start.13 = (f32[4,32,548]{2,1,0:T(8,128)S(1)}, f32[4,32,548]{2,1,0:T(8,128)S(1)}, u32[]{:S(2)}, u32[]{:S(2)}) collective-permute-start(f32[4,32,548]{2,1,0:T(8,128)S(1)} %get-tuple-element.66), channel_id=1, source_target_pairs={{4,8},{12,16},{20,24},{8,4},{16,12},{24,20},{5,9},{13,17},{21,25},... | collective-permute-start | bytes 841736 | tf_op jit(solution)/shard_map/ppermute | solution.py:477
  110.0 16.8 %shard_map.136 = (f32[16,32,548]{2,1,0:T(8,128)S(1)}, f32[4,32,548]{2,1,0:T(8,128)S(1)}, f32[4,32,548]{2,1,0:T(8,128)S(1)}, f32[16,4,548]{2,1,0:T(4,128)S(1)}, f32[16,4,548]{2,1,0:T(4,128)S(1)}) custom-call(s32[2]{0:T(128)S(1)} %pad_add_fusion.side_ref, f32[512,768]{1,0:T(8,128)S(1)} %copy-done.4, bf16[512,512]{1,0:T(8,128)(2,1)S(1)} %get-tuple-element.53.one_ref, ...), custom_call_target="tpu_custom_call" | custom-call | flops 10871635968 | bytes 11796480 | tf_op jit(solution)/shard_map/pallas_call | solution.py:624
  126.8 2.4 %collective-permute-start.8 = (f32[4,32,548]{2,1,0:T(8,128)S(1)}, f32[4,32,548]{2,1,0:T(8,128)S(1)}, u32[]{:S(2)}, u32[]{:S(2)}) collective-permute-start(f32[4,32,548]{2,1,0:T(8,128)S(1)} %get-tuple-element.57), channel_id=1, source_target_pairs={{0,4},{8,12},{16,20},{24,28},{4,0},{12,8},{20,16},{28,24},{1,5},{9... | collective-permute-start | bytes 841736 | tf_op jit(solution)/shard_map/ppermute | solution.py:477
  129.2 2.0 %collective-permute-start.9 = (f32[4,32,548]{2,1,0:T(8,128)S(1)}, f32[4,32,548]{2,1,0:T(8,128)S(1)}, u32[]{:S(2)}, u32[]{:S(2)}) collective-permute-start(f32[4,32,548]{2,1,0:T(8,128)S(1)} %get-tuple-element.58), channel_id=1, source_target_pairs={{4,8},{12,16},{20,24},{8,4},{16,12},{24,20},{5,9},{13,17},{21,25},... | collective-permute-start | bytes 841736 | tf_op jit(solution)/shard_map/ppermute | solution.py:477
  132.0 3.8 %collective-permute-start.15 = (f32[24,4,548]{2,1,0:T(4,128)S(1)}, f32[24,4,548]{2,1,0:T(4,128)S(1)}, u32[]{:S(2)}, u32[]{:S(2)}) collective-permute-start(f32[24,4,548]{2,1,0:T(4,128)S(1)} %get-tuple-element.70), channel_id=1, source_target_pairs={{1,2},{2,1},{5,6},{6,5},{9,10},{10,9},{13,14},{14,13},{17,18},{18,... | collective-permute-start | bytes 631304 | tf_op jit(solution)/shard_map/ppermute | solution.py:477
  135.9 7.7 %collective-permute-done.8.ra.refs_0_ = f32[4,32,548]{2,1,0:T(8,128)S(1)} collective-permute-done((f32[4,32,548]{2,1,0:T(8,128)S(1)}, f32[4,32,548]{2,1,0:T(8,128)S(1)}, u32[]{:S(2)}, u32[]{:S(2)}) %collective-permute-start.8) | collective-permute-done | bytes 280608 | tf_op jit(solution)/shard_map/ppermute | solution.py:477
  144.3 2.0 %collective-permute-start.11 = (f32[24,4,548]{2,1,0:T(4,128)S(1)}, f32[24,4,548]{2,1,0:T(4,128)S(1)}, u32[]{:S(2)}, u32[]{:S(2)}) collective-permute-start(f32[24,4,548]{2,1,0:T(4,128)S(1)} %get-tuple-element.62), channel_id=1, source_target_pairs={{1,2},{2,1},{5,6},{6,5},{9,10},{10,9},{13,14},{14,13},{17,18},{18,... | collective-permute-start | bytes 631304 | tf_op jit(solution)/shard_map/ppermute | solution.py:477
  146.3 4.3 %shard_map.140.refs_4_ = f32[2,16,32,548]{3,2,1,0:T(8,128)} custom-call(s32[2]{0:T(128)S(1)} %pad_add_fusion.side_ref, f32[16,32,548]{2,1,0:T(8,128)S(1)} %get-tuple-element.64.field_ref, f32[2,16,32,548]{3,2,1,0:T(8,128)S(1)} %copy-done, f32[3,24,40,128]{3,2,1,0:T(8,128)S(1)} %copy-done.2, f32[4,32,548]{2,1,0:T(8,128)S(1)} %collective-permute-done.12.ra.refs_0_, ...), custom_call_target="tpu_custom_call" | custom-call | flops 24576000 | bytes 3932160 | tf_op jit(solution)/shard_map/pallas_call | solution.py:647
  150.7 1.1 collective-permute-done.11.refs_3_
  151.8 4.3 %shard_map.141 = f32[2,16,32,548]{3,2,1,0:T(8,128)} custom-call(s32[2]{0:T(128)S(1)} %pad_add_fusion.side_ref, f32[16,32,548]{2,1,0:T(8,128)S(1)} %get-tuple-element.56.field_ref, f32[2,16,32,548]{3,2,1,0:T(8,128)S(1)} %copy-done, f32[3,24,40,128]{3,2,1,0:T(8,128)S(1)} %copy-done.2, ...), custom_call_target="tpu_custom_call", output_to_operand_aliasing={{}: (8, {})} | custom-call | flops 24576000 | bytes 3932160 | tf_op jit(solution)/shard_map/pallas_call | solution.py:647
  (45 shorter events, 3.3 us)
Async XLA Ops:
  1.4 1.3 copy-start.8
  4.9 6.5 %copy-start.5 = (f32[16,32]{1,0:T(8,128)S(1)}, f32[16,32]{1,0:T(8,128)}, u32[]{:S(2)}) copy-start(f32[16,32]{1,0:T(8,128)} %coeff_ref.5) | copy-start | bytes 6148
  4.9 79.5 %all-to-all-start = ((f32[32,72,128]{2,1,0:T(8,128)}), f32[32,72,128]{2,1,0:T(8,128)}, u32[]{:S(2)}, u32[]{:S(2)}) async-start(f32[32,72,128]{2,1,0:T(8,128)} %shard_map.134), calls=%async_computation | async-start | bytes 2359296 | tf_op jit(solution)/shard_map/all_to_all | solution.py:556
  13.3 45.3 %collective-permute-start = (f32[4,32,549]{2,1,0:T(8,128)S(1)}, f32[4,32,549]{2,1,0:T(8,128)S(1)}, u32[]{:S(2)}, u32[]{:S(2)}) collective-permute-start(f32[4,32,549]{2,1,0:T(8,128)S(1)} %get-tuple-element.38), channel_id=1, source_target_pairs={{0,4},{8,12},{16,20},{24,28},{4,0},{12,8},{20,16},{28,24},{1,5},{9... | collective-permute-start | bytes 843272 | tf_op jit(solution)/shard_map/ppermute | solution.py:477
  14.6 44.0 %collective-permute-start.1 = (f32[4,32,549]{2,1,0:T(8,128)S(1)}, f32[4,32,549]{2,1,0:T(8,128)S(1)}, u32[]{:S(2)}, u32[]{:S(2)}) collective-permute-start(f32[4,32,549]{2,1,0:T(8,128)S(1)} %get-tuple-element.39), channel_id=1, source_target_pairs={{4,8},{12,16},{20,24},{8,4},{16,12},{24,20},{5,9},{13,17},{21,25},... | collective-permute-start | bytes 843272 | tf_op jit(solution)/shard_map/ppermute | solution.py:477
  18.5 35.4 %collective-permute-start.4 = (f32[4,32,548]{2,1,0:T(8,128)S(1)}, f32[4,32,548]{2,1,0:T(8,128)S(1)}, u32[]{:S(2)}, u32[]{:S(2)}) collective-permute-start(f32[4,32,548]{2,1,0:T(8,128)S(1)} %get-tuple-element.46), channel_id=1, source_target_pairs={{0,4},{8,12},{16,20},{24,28},{4,0},{12,8},{20,16},{28,24},{1,5},{9... | collective-permute-start | bytes 841736 | tf_op jit(solution)/shard_map/ppermute | solution.py:477
  20.8 33.1 %collective-permute-start.5 = (f32[4,32,548]{2,1,0:T(8,128)S(1)}, f32[4,32,548]{2,1,0:T(8,128)S(1)}, u32[]{:S(2)}, u32[]{:S(2)}) collective-permute-start(f32[4,32,548]{2,1,0:T(8,128)S(1)} %get-tuple-element.47), channel_id=1, source_target_pairs={{4,8},{12,16},{20,24},{8,4},{16,12},{24,20},{5,9},{13,17},{21,25},... | collective-permute-start | bytes 841736 | tf_op jit(solution)/shard_map/ppermute | solution.py:477
  54.5 22.5 %collective-permute-start.6 = (f32[24,4,548]{2,1,0:T(4,128)S(1)}, f32[24,4,548]{2,1,0:T(4,128)S(1)}, u32[]{:S(2)}, u32[]{:S(2)}) collective-permute-start(f32[24,4,548]{2,1,0:T(4,128)S(1)} %get-tuple-element.50), channel_id=1, source_target_pairs={{0,1},{2,3},{1,0},{3,2},{4,5},{6,7},{5,4},{7,6},{8,9},{10,11},{9,8... | collective-permute-start | bytes 631304 | tf_op jit(solution)/shard_map/ppermute | solution.py:477
  55.6 21.4 %collective-permute-start.7 = (f32[24,4,548]{2,1,0:T(4,128)S(1)}, f32[24,4,548]{2,1,0:T(4,128)S(1)}, u32[]{:S(2)}, u32[]{:S(2)}) collective-permute-start(f32[24,4,548]{2,1,0:T(4,128)S(1)} %get-tuple-element.51), channel_id=1, source_target_pairs={{1,2},{2,1},{5,6},{6,5},{9,10},{10,9},{13,14},{14,13},{17,18},{18,... | collective-permute-start | bytes 631304 | tf_op jit(solution)/shard_map/ppermute | solution.py:477
  59.2 11.0 %collective-permute-start.2 = (f32[24,4,549]{2,1,0:T(4,128)S(1)}, f32[24,4,549]{2,1,0:T(4,128)S(1)}, u32[]{:S(2)}, u32[]{:S(2)}) collective-permute-start(f32[24,4,549]{2,1,0:T(4,128)S(1)} %get-tuple-element.42), channel_id=1, source_target_pairs={{0,1},{2,3},{1,0},{3,2},{4,5},{6,7},{5,4},{7,6},{8,9},{10,11},{9,8... | collective-permute-start | bytes 632456 | tf_op jit(solution)/shard_map/ppermute | solution.py:477
  59.3 11.0 %collective-permute-start.3 = (f32[24,4,549]{2,1,0:T(4,128)S(1)}, f32[24,4,549]{2,1,0:T(4,128)S(1)}, u32[]{:S(2)}, u32[]{:S(2)}) collective-permute-start(f32[24,4,549]{2,1,0:T(4,128)S(1)} %get-tuple-element.43), channel_id=1, source_target_pairs={{1,2},{2,1},{5,6},{6,5},{9,10},{10,9},{13,14},{14,13},{17,18},{18,... | collective-permute-start | bytes 632456 | tf_op jit(solution)/shard_map/ppermute | solution.py:477
  61.9 8.3 %copy-start.10 = (f32[768]{0:T(1024)S(1)}, f32[768]{0:T(1024)}, u32[]{:S(2)}) copy-start(f32[768]{0:T(1024)} %param.17) | copy-start | bytes 9220
  61.9 8.3 %copy-start.11 = (f32[768]{0:T(1024)S(1)}, f32[768]{0:T(1024)}, u32[]{:S(2)}) copy-start(f32[768]{0:T(1024)} %param.19) | copy-start | bytes 9220
  61.9 8.4 %copy-start = (f32[2,16,32,548]{3,2,1,0:T(8,128)S(1)}, f32[2,16,32,548]{3,2,1,0:T(8,128)}, u32[]{:S(2)}) copy-start(f32[2,16,32,548]{3,2,1,0:T(8,128)} %base_ref.3) | copy-start | bytes 6733828
  75.9 1.1 copy-start.6
  77.0 7.4 %copy-start.9 = (s32[32,616]{1,0:T(8,128)S(1)}, s32[32,616]{1,0:T(8,128)}, u32[]{:S(2)}) copy-start(s32[32,616]{1,0:T(8,128)} %mask_ref.1) | copy-start | bytes 236548
  82.1 1.1 copy-start.1
  83.2 1.2 copy-start.3
  84.4 6.3 %copy-start.7 = (f32[512,768]{1,0:T(8,128)S(1)}, f32[512,768]{1,0:T(8,128)}, u32[]{:S(2)}) copy-start(f32[512,768]{1,0:T(8,128)} %copy-done.6) | copy-start | bytes 4718596
  90.7 19.3 %copy-start.4 = (f32[512,768]{1,0:T(8,128)S(1)}, f32[512,768]{1,0:T(8,128)}, u32[]{:S(2)}) copy-start(f32[512,768]{1,0:T(8,128)} %copy-done.3) | copy-start | bytes 4718596
  107.7 23.6 %collective-permute-start.12 = (f32[4,32,548]{2,1,0:T(8,128)S(1)}, f32[4,32,548]{2,1,0:T(8,128)S(1)}, u32[]{:S(2)}, u32[]{:S(2)}) collective-permute-start(f32[4,32,548]{2,1,0:T(8,128)S(1)} %get-tuple-element.65), channel_id=1, source_target_pairs={{0,4},{8,12},{16,20},{24,28},{4,0},{12,8},{20,16},{28,24},{1,5},{9... | collective-permute-start | bytes 841736 | tf_op jit(solution)/shard_map/ppermute | solution.py:477
  108.1 23.2 %collective-permute-start.13 = (f32[4,32,548]{2,1,0:T(8,128)S(1)}, f32[4,32,548]{2,1,0:T(8,128)S(1)}, u32[]{:S(2)}, u32[]{:S(2)}) collective-permute-start(f32[4,32,548]{2,1,0:T(8,128)S(1)} %get-tuple-element.66), channel_id=1, source_target_pairs={{4,8},{12,16},{20,24},{8,4},{16,12},{24,20},{5,9},{13,17},{21,25},... | collective-permute-start | bytes 841736 | tf_op jit(solution)/shard_map/ppermute | solution.py:477
  126.8 19.5 %copy-start.2 = (f32[3,24,40,128]{3,2,1,0:T(8,128)S(1)}, f32[3,24,40,128]{3,2,1,0:T(8,128)}, u32[]{:S(2)}) copy-start(f32[3,24,40,128]{3,2,1,0:T(8,128)} %copy-done.1) | copy-start | bytes 4423684
  126.8 16.8 %collective-permute-start.8 = (f32[4,32,548]{2,1,0:T(8,128)S(1)}, f32[4,32,548]{2,1,0:T(8,128)S(1)}, u32[]{:S(2)}, u32[]{:S(2)}) collective-permute-start(f32[4,32,548]{2,1,0:T(8,128)S(1)} %get-tuple-element.57), channel_id=1, source_target_pairs={{0,4},{8,12},{16,20},{24,28},{4,0},{12,8},{20,16},{28,24},{1,5},{9... | collective-permute-start | bytes 841736 | tf_op jit(solution)/shard_map/ppermute | solution.py:477
  129.2 14.3 %collective-permute-start.9 = (f32[4,32,548]{2,1,0:T(8,128)S(1)}, f32[4,32,548]{2,1,0:T(8,128)S(1)}, u32[]{:S(2)}, u32[]{:S(2)}) collective-permute-start(f32[4,32,548]{2,1,0:T(8,128)S(1)} %get-tuple-element.58), channel_id=1, source_target_pairs={{4,8},{12,16},{20,24},{8,4},{16,12},{24,20},{5,9},{13,17},{21,25},... | collective-permute-start | bytes 841736 | tf_op jit(solution)/shard_map/ppermute | solution.py:477
  132.0 14.4 %collective-permute-start.14 = (f32[24,4,548]{2,1,0:T(4,128)S(1)}, f32[24,4,548]{2,1,0:T(4,128)S(1)}, u32[]{:S(2)}, u32[]{:S(2)}) collective-permute-start(f32[24,4,548]{2,1,0:T(4,128)S(1)} %get-tuple-element.69), channel_id=1, source_target_pairs={{0,1},{2,3},{1,0},{3,2},{4,5},{6,7},{5,4},{7,6},{8,9},{10,11},{9,8... | collective-permute-start | bytes 631304 | tf_op jit(solution)/shard_map/ppermute | solution.py:477
  132.0 14.3 %collective-permute-start.15 = (f32[24,4,548]{2,1,0:T(4,128)S(1)}, f32[24,4,548]{2,1,0:T(4,128)S(1)}, u32[]{:S(2)}, u32[]{:S(2)}) collective-permute-start(f32[24,4,548]{2,1,0:T(4,128)S(1)} %get-tuple-element.70), channel_id=1, source_target_pairs={{1,2},{2,1},{5,6},{6,5},{9,10},{10,9},{13,14},{14,13},{17,18},{18,... | collective-permute-start | bytes 631304 | tf_op jit(solution)/shard_map/ppermute | solution.py:477
  144.2 6.5 %collective-permute-start.10 = (f32[24,4,548]{2,1,0:T(4,128)S(1)}, f32[24,4,548]{2,1,0:T(4,128)S(1)}, u32[]{:S(2)}, u32[]{:S(2)}) collective-permute-start(f32[24,4,548]{2,1,0:T(4,128)S(1)} %get-tuple-element.61), channel_id=1, source_target_pairs={{0,1},{2,3},{1,0},{3,2},{4,5},{6,7},{5,4},{7,6},{8,9},{10,11},{9,8... | collective-permute-start | bytes 631304 | tf_op jit(solution)/shard_map/ppermute | solution.py:477
  144.3 7.5 %collective-permute-start.11 = (f32[24,4,548]{2,1,0:T(4,128)S(1)}, f32[24,4,548]{2,1,0:T(4,128)S(1)}, u32[]{:S(2)}, u32[]{:S(2)}) collective-permute-start(f32[24,4,548]{2,1,0:T(4,128)S(1)} %get-tuple-element.62), channel_id=1, source_target_pairs={{1,2},{2,1},{5,6},{6,5},{9,10},{10,9},{13,14},{14,13},{17,18},{18,... | collective-permute-start | bytes 631304 | tf_op jit(solution)/shard_map/ppermute | solution.py:477

commit v8 on v6

--- a/solution.py
+++ b/solution.py
@@ -30,6 +30,10 @@
 
 
 def mm3(left_high, left_low, right_high, right_low, dims=NN):
+    if left_high.shape[dims[0][0]] % WIDE == 0:
+        return mm(left_high, right_high, dims) + (
+            mm(left_high, right_low, dims) + mm(left_low, right_high, dims)
+        )
     left = jnp.concatenate([left_high, left_low, left_high], axis=dims[0][0])
     right = jnp.concatenate([right_high, right_high, right_low], axis=dims[1][0])
     return mm(left, right, dims)
@@ -40,15 +44,14 @@
     return [pl.ds(0, half), pl.ds(half, half)] if half % 16 == 0 else [pl.ds(0, size)]
 
 
-def each_half(size, work):
-    parts = halves(size)
-    step = parts[0].size
+def each_part(size, work, count=2):
+    step = size // count if size % (16 * count) == 0 else size
 
     def run(k, _):
         work(pl.ds(pl.multiple_of(k * step, step), step))
         return 0
 
-    lax.fori_loop(0, len(parts), run, 0)
+    lax.fori_loop(0, size // step, run, 0)
 
 
 def iota(shape, axis):
@@ -137,11 +140,18 @@
         got = mm3(turned[0, part, :], turned[1, part, :], first[0], first[1])
         stack[3, 0, part, :], stack[3, 1, part, :] = split(got)
 
-    each_half(rows, half)
+    each_part(rows, half)
     send(stack.at[3], stack_out.at[3])
     for k in range(3):
         fetch[k + 2].wait()
-        put(raw[k + 2][...], stack.at[k])
+        if raw[k + 2].shape == stack.shape[2:]:
+
+            def rows_of(part, k=k):
+                stack[k, 0, part, :], stack[k, 1, part, :] = split(raw[k + 2][part, :])
+
+            each_part(stack.shape[2], rows_of, 4)
+        else:
+            put(raw[k + 2][...], stack.at[k])
         send(stack.at[k], stack_out.at[k])
     for copy in sends:
         copy.wait()
@@ -297,7 +307,7 @@
             high_ref[part, :], low_ref[part, :], both[0, :deep], both[1, :deep]
         )
 
-    each_half(out_ref.shape[0], half)
+    each_part(out_ref.shape[0], half)
 
 
 def hidden_kernel(
@@ -342,18 +352,17 @@
         here = pl.ds(k * LANES, LANES)
         high_ref[:, here], low_ref[:, here] = split(piece)
     fetch_first.wait()
-    fetch_second.wait()
-
-    def both_layers(part):
+    parts = halves(slots)
+    for part in parts:
         got = mm3(high_ref[part, :deep], low_ref[part, :deep], first[0, :deep], first[1, :deep])
         hidden = jnp.tanh(got + b1_ref[...])
         s1_ref[part, :] = 1.0 - hidden * hidden
-        high, low = split(hidden)
-        got = mm3(high, low, second[0], second[1])
+        high_ref[part, :], low_ref[part, :] = split(hidden)
+    fetch_second.wait()
+    for part in parts:
+        got = mm3(high_ref[part, :], low_ref[part, :], second[0], second[1])
         hidden = jnp.tanh(got + b2_ref[...])
         s2_ref[part, :] = 1.0 - hidden * hidden
-
-    each_half(slots, both_layers)
 
 
 LAYERS = ((0, NN, 1), (1, NT, 2), (2, NN, 2), (1, NN, 1), (0, NT, 0))
@@ -378,7 +387,11 @@
     def close(acc, scale, part, target):
         target[0], target[1] = split(acc[...] * scale_ref[scale, part, :])
 
-    x1[0], x1[1] = split(q_ref[...])
+
+    def take(part):
+        x1[0, part, :], x1[1, part, :] = split(q_ref[part, :])
+
+    each_part(slots, take, 4)
     acc_top[...] = pick(one_ref[first, :])
     acc_low[...] = pick(one_ref[second, :])
     close(acc_top, 0, first, top)
@@ -399,7 +412,7 @@
         got = got + mm(one_t_ref[part, half:], low[0]) + mm(one_t_ref[part, half:], low[1])
         x1[0, part, :], x1[1, part, :] = split(got)
 
-    each_half(one_t_ref.shape[0], scatter)
+    each_part(one_t_ref.shape[0], scatter)
     fetch[3].wait()
     rows, wide, levels = out_ref.shape
     parts = halves(rows * wide)

time: 159 us -> 159 us (level)
  no operation moved by 1% of the time
where the time goes in v8:
time: 159 us; the launch traced here: 157 us
  Pallas kernels  77.2 us (49%)
  waiting for transfers between devices  40 us (25%)
  starting transfers between devices  33.4 us (21%)
  local copies, waits for them, and re-layouts  4.74 us (3%)
    ppermute x16, waiting for transfers between devices, swap(): return lax.ppermute(value, axis, pairs + [(j, i) for i, j in pairs])  40 us
    pallas_call x2, Pallas kernels, body(): call(net_kernel, [shaped((tile_x, tile_y, levels))] + [shaped((SWEEPS, ti...  33.3 us
    ppermute x16, starting transfers between devices, swap(): return lax.ppermute(value, axis, pairs + [(j, i) for i, j in pairs])  27.1 us
    pallas_call x2, Pallas kernels, body(): call(functools.partial(diffuse_kernel, v), [shaped((cells, side))] + [sha...  10.7 us
    pallas_call x2, Pallas kernels, body(): call(functools.partial(finish_kernel, v), pltpu.HBM(vectors.shape, F32),...  8.66 us
    pallas_call x1, Pallas kernels, body(): call(prep_kernel, [pltpu.HBM((2, full_l, side), BF), pltpu.HBM((4, 2, sid...  8.64 us
    pallas_call x1, Pallas kernels, body(): call(functools.partial(hidden_kernel, mark, bucket), [shaped((3, slots, s...  7.23 us
    all_to_all x1, starting transfers between devices, body(): lax.all_to_all(packed if tight else packed.reshape(devices, bucket, deep)...  6.38 us
  transfers between devices with their start and end apart: 17, of which 3 were waited for; matrix products, arithmetic and copies ran while one was open for 0% of the time, Pallas kernels for 30%

profile of v8, /device:TPU:9, one launch (start us, length us, event | category | flops | bytes accessed | tf_op | source)
XLA Modules:
  0.0 157.4 jit_solution(5314398146929515508)
XLA Ops:
  0.7 0.7 fusion.6
  1.4 1.2 copy-done.8
  2.6 2.3 %shard_map.134 = f32[32,72,128]{2,1,0:T(8,128)} custom-call(s32[1,512]{1,0:T(1,128)S(1)} %bitcast.9, f32[1,512]{1,0:T(1,128)S(1)} %bitcast.8, f32[548,512]{1,0:T(8,128)S(1)} %bitcast.10), custom_call_target="tpu_custom_call" | custom-call | flops 1006632960 | bytes 2621440 | tf_op jit(solution)/shard_map/pallas_call | solution.py:538
  4.9 6.4 %all-to-all-start = ((f32[32,72,128]{2,1,0:T(8,128)}), f32[32,72,128]{2,1,0:T(8,128)}, u32[]{:S(2)}, u32[]{:S(2)}) async-start(f32[32,72,128]{2,1,0:T(8,128)} %shard_map.134), calls=%async_computation | async-start | bytes 2359296 | tf_op jit(solution)/shard_map/all_to_all | solution.py:546
  11.4 1.9 %shard_map.127 = (f32[4,32,549]{2,1,0:T(8,128)S(1)}, f32[4,32,549]{2,1,0:T(8,128)S(1)}, f32[16,4,549]{2,1,0:T(4,128)S(1)}, f32[16,4,549]{2,1,0:T(4,128)S(1)}) custom-call(s32[2]{0:T(128)S(1)} %pad_add_fusion.side_ref, f32[2,16,32,548]{3,2,1,0:T(8,128)} %base_ref.3, f32[16,32]{1,0:T(8,128)S(1)} %copy-done.5), custom_call_target="tpu_custom_call" | custom-call | bytes 2244608 | tf_op jit(solution)/shard_map/pallas_call | solution.py:515
  13.3 1.2 collective-permute-start
  14.6 2.0 %collective-permute-start.1 = (f32[4,32,549]{2,1,0:T(8,128)S(1)}, f32[4,32,549]{2,1,0:T(8,128)S(1)}, u32[]{:S(2)}, u32[]{:S(2)}) collective-permute-start(f32[4,32,549]{2,1,0:T(8,128)S(1)} %get-tuple-element.39), channel_id=1, source_target_pairs={{4,8},{12,16},{20,24},{8,4},{16,12},{24,20},{5,9},{13,17},{21,25},... | collective-permute-start | bytes 843272 | tf_op jit(solution)/shard_map/ppermute | solution.py:467
  16.6 1.9 %shard_map.131 = (f32[4,32,548]{2,1,0:T(8,128)S(1)}, f32[4,32,548]{2,1,0:T(8,128)S(1)}, f32[16,4,548]{2,1,0:T(4,128)S(1)}, f32[16,4,548]{2,1,0:T(4,128)S(1)}) custom-call(s32[2]{0:T(128)S(1)} %pad_add_fusion.side_ref, f32[2,16,32,548]{3,2,1,0:T(8,128)} %base_ref.3, f32[16,32]{1,0:T(8,128)S(1)} %copy-done.5), custom_call_target="tpu_custom_call" | custom-call | bytes 2244608 | tf_op jit(solution)/shard_map/pallas_call | solution.py:515
  18.5 2.3 %collective-permute-start.4 = (f32[4,32,548]{2,1,0:T(8,128)S(1)}, f32[4,32,548]{2,1,0:T(8,128)S(1)}, u32[]{:S(2)}, u32[]{:S(2)}) collective-permute-start(f32[4,32,548]{2,1,0:T(8,128)S(1)} %get-tuple-element.46), channel_id=1, source_target_pairs={{0,4},{8,12},{16,20},{24,28},{4,0},{12,8},{20,16},{28,24},{1,5},{9... | collective-permute-start | bytes 841736 | tf_op jit(solution)/shard_map/ppermute | solution.py:467
  20.8 1.9 %collective-permute-start.5 = (f32[4,32,548]{2,1,0:T(8,128)S(1)}, f32[4,32,548]{2,1,0:T(8,128)S(1)}, u32[]{:S(2)}, u32[]{:S(2)}) collective-permute-start(f32[4,32,548]{2,1,0:T(8,128)S(1)} %get-tuple-element.47), channel_id=1, source_target_pairs={{4,8},{12,16},{20,24},{8,4},{16,12},{24,20},{5,9},{13,17},{21,25},... | collective-permute-start | bytes 841736 | tf_op jit(solution)/shard_map/ppermute | solution.py:467
  22.8 31.1 %collective-permute-done.4.ra.refs_0_ = f32[4,32,548]{2,1,0:T(8,128)S(1)} collective-permute-done((f32[4,32,548]{2,1,0:T(8,128)S(1)}, f32[4,32,548]{2,1,0:T(8,128)S(1)}, u32[]{:S(2)}, u32[]{:S(2)}) %collective-permute-start.4) | collective-permute-done | bytes 280608 | tf_op jit(solution)/shard_map/ppermute | solution.py:467
  54.5 1.0 collective-permute-start.6
  55.6 3.0 %collective-permute-start.7 = (f32[24,4,548]{2,1,0:T(4,128)S(1)}, f32[24,4,548]{2,1,0:T(4,128)S(1)}, u32[]{:S(2)}, u32[]{:S(2)}) collective-permute-start(f32[24,4,548]{2,1,0:T(4,128)S(1)} %get-tuple-element.51), channel_id=1, source_target_pairs={{1,2},{2,1},{5,6},{6,5},{9,10},{10,9},{13,14},{14,13},{17,18},{18,... | collective-permute-start | bytes 631304 | tf_op jit(solution)/shard_map/ppermute | solution.py:467
  59.3 2.7 %collective-permute-start.3 = (f32[24,4,549]{2,1,0:T(4,128)S(1)}, f32[24,4,549]{2,1,0:T(4,128)S(1)}, u32[]{:S(2)}, u32[]{:S(2)}) collective-permute-start(f32[24,4,549]{2,1,0:T(4,128)S(1)} %get-tuple-element.43), channel_id=1, source_target_pairs={{1,2},{2,1},{5,6},{6,5},{9,10},{10,9},{13,14},{14,13},{17,18},{18,... | collective-permute-start | bytes 632456 | tf_op jit(solution)/shard_map/ppermute | solution.py:467
  62.1 8.6 %shard_map.129 = (bf16[2,768,768]{2,1,0:T(8,128)(2,1)}, bf16[4,2,768,768]{3,2,1,0:T(8,128)(2,1)}) custom-call(f32[548,548]{1,0:T(8,128)} %refs_0_.1, f32[548,768]{1,0:T(8,128)} %refs_1_.1, f32[768,768]{1,0:T(8,128)} %refs_2_.1, f32[616,768]{1,0:T(8,128)} %bitcast.11, f32[616,616]{1,0:T(8,128)} %refs_4_.1), custom_call_target="tpu_custom_call" | custom-call | flops 2717908992 | bytes 23592960 | tf_op jit(solution)/shard_map/pallas_call | solution.py:553
  70.8 5.5 %shard_map.130 = (f32[512,768]{1,0:T(8,128)S(1)}, f32[3,24,40,128]{3,2,1,0:T(8,128)S(1)}) custom-call(s32[2]{0:T(128)S(1)} %pad_add_fusion.side_ref, f32[2,16,32,548]{3,2,1,0:T(8,128)S(1)} %copy-done, f32[16,32]{1,0:T(8,128)S(1)} %copy-done.5, f32[4,32,549]{2,1,0:T(8,128)S(1)} %collective-permute-done.ra.refs_0_, ...), custom_call_target="tpu_custom_call" | custom-call | flops 1509949440 | bytes 4915200 | tf_op jit(solution)/shard_map/pallas_call | solution.py:575
  76.4 1.1 copy-done.6
  77.5 5.2 %shard_map.133.q_ref = f32[512,768]{1,0:T(8,128)S(1)} custom-call(s32[2]{0:T(128)S(1)} %pad_add_fusion.side_ref, f32[2,16,32,548]{3,2,1,0:T(8,128)S(1)} %copy-done, f32[3,24,40,128]{3,2,1,0:T(8,128)S(1)} %get-tuple-element.45.coeff_ref.cb_ref, f32[4,32,548]{2,1,0:T(8,128)S(1)} %collective-permute-done.4.ra.refs_0_, ...), custom_call_target="tpu_custom_call" | custom-call | flops 1509949440 | bytes 4915200 | tf_op jit(solution)/shard_map/pallas_call | solution.py:575
  82.7 1.1 copy-done.1
  83.8 1.2 copy-done.3
  85.0 7.2 %shard_map.135 = (f32[3,512,768]{2,1,0:T(8,128)S(1)}, bf16[512,512]{1,0:T(8,128)(2,1)S(1)}, bf16[512,512]{1,0:T(8,128)(2,1)S(1)}) custom-call(f32[32,72,128]{2,1,0:T(8,128)} %all-to-all-done.x_ref, bf16[2,768,768]{2,1,0:T(8,128)(2,1)} %get-tuple-element.52.first_ref, f32[1,768]{1,0:T(1,128)S(1)} %broadcast_in_dim.16.b1_ref, ...), custom_call_target="tpu_custom_call" | custom-call | flops 3623878656 | bytes 3145728 | tf_op jit(solution)/shard_map/pallas_call | solution.py:596
  92.3 16.6 %shard_map.138 = (f32[16,32,548]{2,1,0:T(8,128)S(1)}, f32[4,32,548]{2,1,0:T(8,128)S(1)}, f32[4,32,548]{2,1,0:T(8,128)S(1)}, f32[16,4,548]{2,1,0:T(4,128)S(1)}, f32[16,4,548]{2,1,0:T(4,128)S(1)}) custom-call(s32[2]{0:T(128)S(1)} %pad_add_fusion.side_ref, f32[512,768]{1,0:T(8,128)S(1)} %copy-done.7, bf16[512,512]{1,0:T(8,128)(2,1)S(1)} %get-tuple-element.53.one_ref, ...), custom_call_target="tpu_custom_call" | custom-call | flops 10871635968 | bytes 11796480 | tf_op jit(solution)/shard_map/pallas_call | solution.py:614
  109.3 1.9 %collective-permute-start.13 = (f32[4,32,548]{2,1,0:T(8,128)S(1)}, f32[4,32,548]{2,1,0:T(8,128)S(1)}, u32[]{:S(2)}, u32[]{:S(2)}) collective-permute-start(f32[4,32,548]{2,1,0:T(8,128)S(1)} %get-tuple-element.66), channel_id=1, source_target_pairs={{4,8},{12,16},{20,24},{8,4},{16,12},{24,20},{5,9},{13,17},{21,25},... | collective-permute-start | bytes 841736 | tf_op jit(solution)/shard_map/ppermute | solution.py:467
  111.2 16.7 %shard_map.136 = (f32[16,32,548]{2,1,0:T(8,128)S(1)}, f32[4,32,548]{2,1,0:T(8,128)S(1)}, f32[4,32,548]{2,1,0:T(8,128)S(1)}, f32[16,4,548]{2,1,0:T(4,128)S(1)}, f32[16,4,548]{2,1,0:T(4,128)S(1)}) custom-call(s32[2]{0:T(128)S(1)} %pad_add_fusion.side_ref, f32[512,768]{1,0:T(8,128)S(1)} %copy-done.4, bf16[512,512]{1,0:T(8,128)(2,1)S(1)} %get-tuple-element.53.one_ref, ...), custom_call_target="tpu_custom_call" | custom-call | flops 10871635968 | bytes 11796480 | tf_op jit(solution)/shard_map/pallas_call | solution.py:614
  127.9 2.4 %collective-permute-start.8 = (f32[4,32,548]{2,1,0:T(8,128)S(1)}, f32[4,32,548]{2,1,0:T(8,128)S(1)}, u32[]{:S(2)}, u32[]{:S(2)}) collective-permute-start(f32[4,32,548]{2,1,0:T(8,128)S(1)} %get-tuple-element.57), channel_id=1, source_target_pairs={{0,4},{8,12},{16,20},{24,28},{4,0},{12,8},{20,16},{28,24},{1,5},{9... | collective-permute-start | bytes 841736 | tf_op jit(solution)/shard_map/ppermute | solution.py:467
  130.3 2.0 %collective-permute-start.9 = (f32[4,32,548]{2,1,0:T(8,128)S(1)}, f32[4,32,548]{2,1,0:T(8,128)S(1)}, u32[]{:S(2)}, u32[]{:S(2)}) collective-permute-start(f32[4,32,548]{2,1,0:T(8,128)S(1)} %get-tuple-element.58), channel_id=1, source_target_pairs={{4,8},{12,16},{20,24},{8,4},{16,12},{24,20},{5,9},{13,17},{21,25},... | collective-permute-start | bytes 841736 | tf_op jit(solution)/shard_map/ppermute | solution.py:467
  133.1 3.8 %collective-permute-start.15 = (f32[24,4,548]{2,1,0:T(4,128)S(1)}, f32[24,4,548]{2,1,0:T(4,128)S(1)}, u32[]{:S(2)}, u32[]{:S(2)}) collective-permute-start(f32[24,4,548]{2,1,0:T(4,128)S(1)} %get-tuple-element.70), channel_id=1, source_target_pairs={{1,2},{2,1},{5,6},{6,5},{9,10},{10,9},{13,14},{14,13},{17,18},{18,... | collective-permute-start | bytes 631304 | tf_op jit(solution)/shard_map/ppermute | solution.py:467
  137.0 7.7 %collective-permute-done.8.ra.refs_0_ = f32[4,32,548]{2,1,0:T(8,128)S(1)} collective-permute-done((f32[4,32,548]{2,1,0:T(8,128)S(1)}, f32[4,32,548]{2,1,0:T(8,128)S(1)}, u32[]{:S(2)}, u32[]{:S(2)}) %collective-permute-start.8) | collective-permute-done | bytes 280608 | tf_op jit(solution)/shard_map/ppermute | solution.py:467
  145.4 2.0 %collective-permute-start.11 = (f32[24,4,548]{2,1,0:T(4,128)S(1)}, f32[24,4,548]{2,1,0:T(4,128)S(1)}, u32[]{:S(2)}, u32[]{:S(2)}) collective-permute-start(f32[24,4,548]{2,1,0:T(4,128)S(1)} %get-tuple-element.62), channel_id=1, source_target_pairs={{1,2},{2,1},{5,6},{6,5},{9,10},{10,9},{13,14},{14,13},{17,18},{18,... | collective-permute-start | bytes 631304 | tf_op jit(solution)/shard_map/ppermute | solution.py:467
  147.4 4.3 %shard_map.140.refs_4_ = f32[2,16,32,548]{3,2,1,0:T(8,128)} custom-call(s32[2]{0:T(128)S(1)} %pad_add_fusion.side_ref, f32[16,32,548]{2,1,0:T(8,128)S(1)} %get-tuple-element.64.field_ref, f32[2,16,32,548]{3,2,1,0:T(8,128)S(1)} %copy-done, f32[3,24,40,128]{3,2,1,0:T(8,128)S(1)} %copy-done.2, f32[4,32,548]{2,1,0:T(8,128)S(1)} %collective-permute-done.12.ra.refs_0_, ...), custom_call_target="tpu_custom_call" | custom-call | flops 24576000 | bytes 3932160 | tf_op jit(solution)/shard_map/pallas_call | solution.py:637
  151.7 1.1 collective-permute-done.11.refs_3_
  152.9 4.3 %shard_map.141 = f32[2,16,32,548]{3,2,1,0:T(8,128)} custom-call(s32[2]{0:T(128)S(1)} %pad_add_fusion.side_ref, f32[16,32,548]{2,1,0:T(8,128)S(1)} %get-tuple-element.56.field_ref, f32[2,16,32,548]{3,2,1,0:T(8,128)S(1)} %copy-done, f32[3,24,40,128]{3,2,1,0:T(8,128)S(1)} %copy-done.2, ...), custom_call_target="tpu_custom_call", output_to_operand_aliasing={{}: (8, {})} | custom-call | flops 24576000 | bytes 3932160 | tf_op jit(solution)/shard_map/pallas_call | solution.py:637
  (45 shorter events, 3.3 us)
Async XLA Ops:
  1.4 1.3 copy-start.8
  4.9 6.5 %copy-start.5 = (f32[16,32]{1,0:T(8,128)S(1)}, f32[16,32]{1,0:T(8,128)}, u32[]{:S(2)}) copy-start(f32[16,32]{1,0:T(8,128)} %coeff_ref.5) | copy-start | bytes 6148
  4.9 80.1 %all-to-all-start = ((f32[32,72,128]{2,1,0:T(8,128)}), f32[32,72,128]{2,1,0:T(8,128)}, u32[]{:S(2)}, u32[]{:S(2)}) async-start(f32[32,72,128]{2,1,0:T(8,128)} %shard_map.134), calls=%async_computation | async-start | bytes 2359296 | tf_op jit(solution)/shard_map/all_to_all | solution.py:546
  13.3 45.3 %collective-permute-start = (f32[4,32,549]{2,1,0:T(8,128)S(1)}, f32[4,32,549]{2,1,0:T(8,128)S(1)}, u32[]{:S(2)}, u32[]{:S(2)}) collective-permute-start(f32[4,32,549]{2,1,0:T(8,128)S(1)} %get-tuple-element.38), channel_id=1, source_target_pairs={{0,4},{8,12},{16,20},{24,28},{4,0},{12,8},{20,16},{28,24},{1,5},{9... | collective-permute-start | bytes 843272 | tf_op jit(solution)/shard_map/ppermute | solution.py:467
  14.6 44.0 %collective-permute-start.1 = (f32[4,32,549]{2,1,0:T(8,128)S(1)}, f32[4,32,549]{2,1,0:T(8,128)S(1)}, u32[]{:S(2)}, u32[]{:S(2)}) collective-permute-start(f32[4,32,549]{2,1,0:T(8,128)S(1)} %get-tuple-element.39), channel_id=1, source_target_pairs={{4,8},{12,16},{20,24},{8,4},{16,12},{24,20},{5,9},{13,17},{21,25},... | collective-permute-start | bytes 843272 | tf_op jit(solution)/shard_map/ppermute | solution.py:467
  18.5 35.4 %collective-permute-start.4 = (f32[4,32,548]{2,1,0:T(8,128)S(1)}, f32[4,32,548]{2,1,0:T(8,128)S(1)}, u32[]{:S(2)}, u32[]{:S(2)}) collective-permute-start(f32[4,32,548]{2,1,0:T(8,128)S(1)} %get-tuple-element.46), channel_id=1, source_target_pairs={{0,4},{8,12},{16,20},{24,28},{4,0},{12,8},{20,16},{28,24},{1,5},{9... | collective-permute-start | bytes 841736 | tf_op jit(solution)/shard_map/ppermute | solution.py:467
  20.8 33.1 %collective-permute-start.5 = (f32[4,32,548]{2,1,0:T(8,128)S(1)}, f32[4,32,548]{2,1,0:T(8,128)S(1)}, u32[]{:S(2)}, u32[]{:S(2)}) collective-permute-start(f32[4,32,548]{2,1,0:T(8,128)S(1)} %get-tuple-element.47), channel_id=1, source_target_pairs={{4,8},{12,16},{20,24},{8,4},{16,12},{24,20},{5,9},{13,17},{21,25},... | collective-permute-start | bytes 841736 | tf_op jit(solution)/shard_map/ppermute | solution.py:467
  54.5 22.9 %collective-permute-start.6 = (f32[24,4,548]{2,1,0:T(4,128)S(1)}, f32[24,4,548]{2,1,0:T(4,128)S(1)}, u32[]{:S(2)}, u32[]{:S(2)}) collective-permute-start(f32[24,4,548]{2,1,0:T(4,128)S(1)} %get-tuple-element.50), channel_id=1, source_target_pairs={{0,1},{2,3},{1,0},{3,2},{4,5},{6,7},{5,4},{7,6},{8,9},{10,11},{9,8... | collective-permute-start | bytes 631304 | tf_op jit(solution)/shard_map/ppermute | solution.py:467
  55.6 21.9 %collective-permute-start.7 = (f32[24,4,548]{2,1,0:T(4,128)S(1)}, f32[24,4,548]{2,1,0:T(4,128)S(1)}, u32[]{:S(2)}, u32[]{:S(2)}) collective-permute-start(f32[24,4,548]{2,1,0:T(4,128)S(1)} %get-tuple-element.51), channel_id=1, source_target_pairs={{1,2},{2,1},{5,6},{6,5},{9,10},{10,9},{13,14},{14,13},{17,18},{18,... | collective-permute-start | bytes 631304 | tf_op jit(solution)/shard_map/ppermute | solution.py:467
  59.2 11.6 %collective-permute-start.2 = (f32[24,4,549]{2,1,0:T(4,128)S(1)}, f32[24,4,549]{2,1,0:T(4,128)S(1)}, u32[]{:S(2)}, u32[]{:S(2)}) collective-permute-start(f32[24,4,549]{2,1,0:T(4,128)S(1)} %get-tuple-element.42), channel_id=1, source_target_pairs={{0,1},{2,3},{1,0},{3,2},{4,5},{6,7},{5,4},{7,6},{8,9},{10,11},{9,8... | collective-permute-start | bytes 632456 | tf_op jit(solution)/shard_map/ppermute | solution.py:467
  59.3 11.5 %collective-permute-start.3 = (f32[24,4,549]{2,1,0:T(4,128)S(1)}, f32[24,4,549]{2,1,0:T(4,128)S(1)}, u32[]{:S(2)}, u32[]{:S(2)}) collective-permute-start(f32[24,4,549]{2,1,0:T(4,128)S(1)} %get-tuple-element.43), channel_id=1, source_target_pairs={{1,2},{2,1},{5,6},{6,5},{9,10},{10,9},{13,14},{14,13},{17,18},{18,... | collective-permute-start | bytes 632456 | tf_op jit(solution)/shard_map/ppermute | solution.py:467
  62.1 8.7 %copy-start.10 = (f32[768]{0:T(1024)S(1)}, f32[768]{0:T(1024)}, u32[]{:S(2)}) copy-start(f32[768]{0:T(1024)} %param.17) | copy-start | bytes 9220
  62.1 8.7 %copy-start.11 = (f32[768]{0:T(1024)S(1)}, f32[768]{0:T(1024)}, u32[]{:S(2)}) copy-start(f32[768]{0:T(1024)} %param.19) | copy-start | bytes 9220
  62.1 8.7 %copy-start = (f32[2,16,32,548]{3,2,1,0:T(8,128)S(1)}, f32[2,16,32,548]{3,2,1,0:T(8,128)}, u32[]{:S(2)}) copy-start(f32[2,16,32,548]{3,2,1,0:T(8,128)} %base_ref.3) | copy-start | bytes 6733828
  76.4 1.1 copy-start.6
  77.5 7.5 %copy-start.9 = (s32[32,616]{1,0:T(8,128)S(1)}, s32[32,616]{1,0:T(8,128)}, u32[]{:S(2)}) copy-start(s32[32,616]{1,0:T(8,128)} %mask_ref.1) | copy-start | bytes 236548
  82.7 1.1 copy-start.1
  83.8 1.2 copy-start.3
  85.0 7.2 %copy-start.7 = (f32[512,768]{1,0:T(8,128)S(1)}, f32[512,768]{1,0:T(8,128)}, u32[]{:S(2)}) copy-start(f32[512,768]{1,0:T(8,128)} %copy-done.6) | copy-start | bytes 4718596
  92.3 18.9 %copy-start.4 = (f32[512,768]{1,0:T(8,128)S(1)}, f32[512,768]{1,0:T(8,128)}, u32[]{:S(2)}) copy-start(f32[512,768]{1,0:T(8,128)} %copy-done.3) | copy-start | bytes 4718596
  108.9 23.4 %collective-permute-start.12 = (f32[4,32,548]{2,1,0:T(8,128)S(1)}, f32[4,32,548]{2,1,0:T(8,128)S(1)}, u32[]{:S(2)}, u32[]{:S(2)}) collective-permute-start(f32[4,32,548]{2,1,0:T(8,128)S(1)} %get-tuple-element.65), channel_id=1, source_target_pairs={{0,4},{8,12},{16,20},{24,28},{4,0},{12,8},{20,16},{28,24},{1,5},{9... | collective-permute-start | bytes 841736 | tf_op jit(solution)/shard_map/ppermute | solution.py:467
  109.3 23.1 %collective-permute-start.13 = (f32[4,32,548]{2,1,0:T(8,128)S(1)}, f32[4,32,548]{2,1,0:T(8,128)S(1)}, u32[]{:S(2)}, u32[]{:S(2)}) collective-permute-start(f32[4,32,548]{2,1,0:T(8,128)S(1)} %get-tuple-element.66), channel_id=1, source_target_pairs={{4,8},{12,16},{20,24},{8,4},{16,12},{24,20},{5,9},{13,17},{21,25},... | collective-permute-start | bytes 841736 | tf_op jit(solution)/shard_map/ppermute | solution.py:467
  127.9 19.5 %copy-start.2 = (f32[3,24,40,128]{3,2,1,0:T(8,128)S(1)}, f32[3,24,40,128]{3,2,1,0:T(8,128)}, u32[]{:S(2)}) copy-start(f32[3,24,40,128]{3,2,1,0:T(8,128)} %copy-done.1) | copy-start | bytes 4423684
  127.9 16.7 %collective-permute-start.8 = (f32[4,32,548]{2,1,0:T(8,128)S(1)}, f32[4,32,548]{2,1,0:T(8,128)S(1)}, u32[]{:S(2)}, u32[]{:S(2)}) collective-permute-start(f32[4,32,548]{2,1,0:T(8,128)S(1)} %get-tuple-element.57), channel_id=1, source_target_pairs={{0,4},{8,12},{16,20},{24,28},{4,0},{12,8},{20,16},{28,24},{1,5},{9... | collective-permute-start | bytes 841736 | tf_op jit(solution)/shard_map/ppermute | solution.py:467
  130.3 14.3 %collective-permute-start.9 = (f32[4,32,548]{2,1,0:T(8,128)S(1)}, f32[4,32,548]{2,1,0:T(8,128)S(1)}, u32[]{:S(2)}, u32[]{:S(2)}) collective-permute-start(f32[4,32,548]{2,1,0:T(8,128)S(1)} %get-tuple-element.58), channel_id=1, source_target_pairs={{4,8},{12,16},{20,24},{8,4},{16,12},{24,20},{5,9},{13,17},{21,25},... | collective-permute-start | bytes 841736 | tf_op jit(solution)/shard_map/ppermute | solution.py:467
  133.0 14.3 %collective-permute-start.14 = (f32[24,4,548]{2,1,0:T(4,128)S(1)}, f32[24,4,548]{2,1,0:T(4,128)S(1)}, u32[]{:S(2)}, u32[]{:S(2)}) collective-permute-start(f32[24,4,548]{2,1,0:T(4,128)S(1)} %get-tuple-element.69), channel_id=1, source_target_pairs={{0,1},{2,3},{1,0},{3,2},{4,5},{6,7},{5,4},{7,6},{8,9},{10,11},{9,8... | collective-permute-start | bytes 631304 | tf_op jit(solution)/shard_map/ppermute | solution.py:467
  133.1 14.3 %collective-permute-start.15 = (f32[24,4,548]{2,1,0:T(4,128)S(1)}, f32[24,4,548]{2,1,0:T(4,128)S(1)}, u32[]{:S(2)}, u32[]{:S(2)}) collective-permute-start(f32[24,4,548]{2,1,0:T(4,128)S(1)} %get-tuple-element.70), channel_id=1, source_target_pairs={{1,2},{2,1},{5,6},{6,5},{9,10},{10,9},{13,14},{14,13},{17,18},{18,... | collective-permute-start | bytes 631304 | tf_op jit(solution)/shard_map/ppermute | solution.py:467
  145.3 6.5 %collective-permute-start.10 = (f32[24,4,548]{2,1,0:T(4,128)S(1)}, f32[24,4,548]{2,1,0:T(4,128)S(1)}, u32[]{:S(2)}, u32[]{:S(2)}) collective-permute-start(f32[24,4,548]{2,1,0:T(4,128)S(1)} %get-tuple-element.61), channel_id=1, source_target_pairs={{0,1},{2,3},{1,0},{3,2},{4,5},{6,7},{5,4},{7,6},{8,9},{10,11},{9,8... | collective-permute-start | bytes 631304 | tf_op jit(solution)/shard_map/ppermute | solution.py:467
  145.4 7.5 %collective-permute-start.11 = (f32[24,4,548]{2,1,0:T(4,128)S(1)}, f32[24,4,548]{2,1,0:T(4,128)S(1)}, u32[]{:S(2)}, u32[]{:S(2)}) collective-permute-start(f32[24,4,548]{2,1,0:T(4,128)S(1)} %get-tuple-element.62), channel_id=1, source_target_pairs={{1,2},{2,1},{5,6},{6,5},{9,10},{10,9},{13,14},{14,13},{17,18},{18,... | collective-permute-start | bytes 631304 | tf_op jit(solution)/shard_map/ppermute | solution.py:467

commit v9 on v7

--- a/solution.py
+++ b/solution.py
@@ -162,8 +162,8 @@
     return jnp.sum(jnp.where(diagonal, spread, 0.0), axis=1, keepdims=True)
 
 
-def cut_kernel(v, side_ref, vectors_ref, coeff_ref, xa, xb, yhead, ytail, *refs):
-    bufs, sems = refs[:4], refs[4]
+def cut_kernel(v, side_ref, vectors_ref, coeff_far, xa, xb, yhead, ytail, *refs):
+    bufs, coeff_ref, sems = refs[:4], refs[4], refs[5]
     rows, wide, levels = vectors_ref.shape[1:]
     w = SWEEPS
     parts = (
@@ -173,10 +173,14 @@
         vectors_ref.at[v, :, pl.ds(wide - 8, 8)],
     )
     copies = [pltpu.make_async_copy(parts[k], bufs[k], sems.at[k]) for k in range(4)]
+    if v == 0:
+        fetch = pltpu.make_async_copy(coeff_far, coeff_ref, sems.at[4])
+        fetch.start()
     for copy in copies:
         copy.start()
     even = side_ref[0] == 0
     if v == 0:
+        fetch.wait()
         columns = [coeff_column(coeff_ref, row) for row in range(rows)]
         for row in range(w):
             head, tail = columns[row], columns[rows - w + row]
@@ -530,9 +534,9 @@
             vmem=12,
             scratch=[pltpu.VMEM((SWEEPS, tile_y, levels), F32)] * 2
             + [pltpu.VMEM((tile_x, 8, levels), F32)] * 2
-            + [pltpu.SemaphoreType.DMA((4,))],
-            in_specs=[scalars, far, whole],
-        )(sides, base, diffusivity)
+            + [pltpu.VMEM(diffusivity.shape, F32), pltpu.SemaphoreType.DMA((5,))],
+            in_specs=[scalars, far, far],
+        )(sides, base, pltpu.with_memory_space_constraint(diffusivity, pltpu.HBM))
         strips.append(halo(sides, *cuts))
 
     position = jnp.arange(slots, dtype=jnp.int32)

time: 158 us -> 158 us (level)
  no operation moved by 1% of the time
where the time goes in v9:
time: 158 us; the launch traced here: 156 us
  Pallas kernels  76.3 us (48%)
  waiting for transfers between devices  40 us (25%)
  starting transfers between devices  33.3 us (21%)
  local copies, waits for them, and re-layouts  4.74 us (3%)
    ppermute x16, waiting for transfers between devices, swap(): return lax.ppermute(value, axis, pairs + [(j, i) for i, j in pairs])  40 us
    pallas_call x2, Pallas kernels, body(): call(net_kernel, [shaped((tile_x, tile_y, levels))] + [shaped((SWEEPS, ti...  33.8 us
    ppermute x16, starting transfers between devices, swap(): return lax.ppermute(value, axis, pairs + [(j, i) for i, j in pairs])  26.9 us
    pallas_call x2, Pallas kernels, body(): call(functools.partial(diffuse_kernel, v), [shaped((cells, side))] + [sha...  10.6 us
    pallas_call x2, Pallas kernels, body(): call(functools.partial(finish_kernel, v), pltpu.HBM(vectors.shape, F32),...  8.66 us
    pallas_call x1, Pallas kernels, body(): call(prep_kernel, [pltpu.HBM((2, full_l, side), BF), pltpu.HBM((4, 2, sid...  8.29 us
    all_to_all x1, starting transfers between devices, body(): lax.all_to_all(packed if tight else packed.reshape(devices, bucket, deep)...  6.38 us
    pallas_call x1, Pallas kernels, body(): call(functools.partial(hidden_kernel, mark, bucket), [shaped((3, slots, s...  6.29 us
  transfers between devices with their start and end apart: 17, of which 3 were waited for; matrix products, arithmetic and copies ran while one was open for 0% of the time, Pallas kernels for 30%

profile of v9, /device:TPU:9, one launch (start us, length us, event | category | flops | bytes accessed | tf_op | source)
XLA Modules:
  0.0 156.4 jit_solution(3778295170581476768)
XLA Ops:
  0.7 0.7 fusion.6
  1.4 1.2 copy-done.8
  2.6 2.3 %shard_map.134 = f32[32,72,128]{2,1,0:T(8,128)} custom-call(s32[1,512]{1,0:T(1,128)S(1)} %bitcast.9, f32[1,512]{1,0:T(1,128)S(1)} %bitcast.8, f32[548,512]{1,0:T(8,128)S(1)} %bitcast.10), custom_call_target="tpu_custom_call" | custom-call | flops 1006632960 | bytes 2621440 | tf_op jit(solution)/shard_map/pallas_call | solution.py:552
  4.9 6.4 %all-to-all-start = ((f32[32,72,128]{2,1,0:T(8,128)}), f32[32,72,128]{2,1,0:T(8,128)}, u32[]{:S(2)}, u32[]{:S(2)}) async-start(f32[32,72,128]{2,1,0:T(8,128)} %shard_map.134), calls=%async_computation | async-start | bytes 2359296 | tf_op jit(solution)/shard_map/all_to_all | solution.py:560
  11.4 1.9 %shard_map.127 = (f32[4,32,549]{2,1,0:T(8,128)S(1)}, f32[4,32,549]{2,1,0:T(8,128)S(1)}, f32[16,4,549]{2,1,0:T(4,128)S(1)}, f32[16,4,549]{2,1,0:T(4,128)S(1)}) custom-call(s32[2]{0:T(128)S(1)} %pad_add_fusion.side_ref, f32[2,16,32,548]{3,2,1,0:T(8,128)} %base_ref.3, f32[16,32]{1,0:T(8,128)} %coeff_far.3), custom_call_target="tpu_custom_call" | custom-call | bytes 2244608 | tf_op jit(solution)/shard_map/pallas_call | solution.py:529
  13.3 1.2 collective-permute-start
  14.6 2.0 %collective-permute-start.1 = (f32[4,32,549]{2,1,0:T(8,128)S(1)}, f32[4,32,549]{2,1,0:T(8,128)S(1)}, u32[]{:S(2)}, u32[]{:S(2)}) collective-permute-start(f32[4,32,549]{2,1,0:T(8,128)S(1)} %get-tuple-element.39), channel_id=1, source_target_pairs={{4,8},{12,16},{20,24},{8,4},{16,12},{24,20},{5,9},{13,17},{21,25},... | collective-permute-start | bytes 843272 | tf_op jit(solution)/shard_map/ppermute | solution.py:481
  16.6 1.9 %shard_map.131 = (f32[4,32,548]{2,1,0:T(8,128)S(1)}, f32[4,32,548]{2,1,0:T(8,128)S(1)}, f32[16,4,548]{2,1,0:T(4,128)S(1)}, f32[16,4,548]{2,1,0:T(4,128)S(1)}) custom-call(s32[2]{0:T(128)S(1)} %pad_add_fusion.side_ref, f32[2,16,32,548]{3,2,1,0:T(8,128)} %base_ref.3, f32[16,32]{1,0:T(8,128)} %coeff_far.3), custom_call_target="tpu_custom_call" | custom-call | bytes 2244608 | tf_op jit(solution)/shard_map/pallas_call | solution.py:529
  18.5 2.3 %collective-permute-start.4 = (f32[4,32,548]{2,1,0:T(8,128)S(1)}, f32[4,32,548]{2,1,0:T(8,128)S(1)}, u32[]{:S(2)}, u32[]{:S(2)}) collective-permute-start(f32[4,32,548]{2,1,0:T(8,128)S(1)} %get-tuple-element.46), channel_id=1, source_target_pairs={{0,4},{8,12},{16,20},{24,28},{4,0},{12,8},{20,16},{28,24},{1,5},{9... | collective-permute-start | bytes 841736 | tf_op jit(solution)/shard_map/ppermute | solution.py:481
  20.9 1.9 %collective-permute-start.5 = (f32[4,32,548]{2,1,0:T(8,128)S(1)}, f32[4,32,548]{2,1,0:T(8,128)S(1)}, u32[]{:S(2)}, u32[]{:S(2)}) collective-permute-start(f32[4,32,548]{2,1,0:T(8,128)S(1)} %get-tuple-element.47), channel_id=1, source_target_pairs={{4,8},{12,16},{20,24},{8,4},{16,12},{24,20},{5,9},{13,17},{21,25},... | collective-permute-start | bytes 841736 | tf_op jit(solution)/shard_map/ppermute | solution.py:481
  22.8 31.1 %collective-permute-done.4.ra.refs_0_ = f32[4,32,548]{2,1,0:T(8,128)S(1)} collective-permute-done((f32[4,32,548]{2,1,0:T(8,128)S(1)}, f32[4,32,548]{2,1,0:T(8,128)S(1)}, u32[]{:S(2)}, u32[]{:S(2)}) %collective-permute-start.4) | collective-permute-done | bytes 280608 | tf_op jit(solution)/shard_map/ppermute | solution.py:481
  54.5 1.0 collective-permute-start.6
  55.6 3.0 %collective-permute-start.7 = (f32[24,4,548]{2,1,0:T(4,128)S(1)}, f32[24,4,548]{2,1,0:T(4,128)S(1)}, u32[]{:S(2)}, u32[]{:S(2)}) collective-permute-start(f32[24,4,548]{2,1,0:T(4,128)S(1)} %get-tuple-element.51), channel_id=1, source_target_pairs={{1,2},{2,1},{5,6},{6,5},{9,10},{10,9},{13,14},{14,13},{17,18},{18,... | collective-permute-start | bytes 631304 | tf_op jit(solution)/shard_map/ppermute | solution.py:481
  59.3 2.6 %collective-permute-start.3 = (f32[24,4,549]{2,1,0:T(4,128)S(1)}, f32[24,4,549]{2,1,0:T(4,128)S(1)}, u32[]{:S(2)}, u32[]{:S(2)}) collective-permute-start(f32[24,4,549]{2,1,0:T(4,128)S(1)} %get-tuple-element.43), channel_id=1, source_target_pairs={{1,2},{2,1},{5,6},{6,5},{9,10},{10,9},{13,14},{14,13},{17,18},{18,... | collective-permute-start | bytes 632456 | tf_op jit(solution)/shard_map/ppermute | solution.py:481
  61.9 8.3 %shard_map.129 = (bf16[2,768,768]{2,1,0:T(8,128)(2,1)}, bf16[4,2,768,768]{3,2,1,0:T(8,128)(2,1)}) custom-call(f32[548,548]{1,0:T(8,128)} %refs_0_.1, f32[548,768]{1,0:T(8,128)} %refs_1_.1, f32[768,768]{1,0:T(8,128)} %refs_2_.1, f32[616,768]{1,0:T(8,128)} %bitcast.11, f32[616,616]{1,0:T(8,128)} %refs_4_.1), custom_call_target="tpu_custom_call" | custom-call | flops 2717908992 | bytes 23592960 | tf_op jit(solution)/shard_map/pallas_call | solution.py:567
  70.3 5.6 %shard_map.130 = (f32[512,768]{1,0:T(8,128)S(1)}, f32[3,24,40,128]{3,2,1,0:T(8,128)S(1)}) custom-call(s32[2]{0:T(128)S(1)} %pad_add_fusion.side_ref, f32[2,16,32,548]{3,2,1,0:T(8,128)S(1)} %copy-done, f32[16,32]{1,0:T(8,128)S(1)} %copy-done.5, f32[4,32,549]{2,1,0:T(8,128)S(1)} %collective-permute-done.ra.refs_0_, ...), custom_call_target="tpu_custom_call" | custom-call | flops 1509949440 | bytes 4915200 | tf_op jit(solution)/shard_map/pallas_call | solution.py:589
  75.9 1.1 copy-done.6
  77.0 5.0 %shard_map.133.q_ref = f32[512,768]{1,0:T(8,128)S(1)} custom-call(s32[2]{0:T(128)S(1)} %pad_add_fusion.side_ref, f32[2,16,32,548]{3,2,1,0:T(8,128)S(1)} %copy-done, f32[3,24,40,128]{3,2,1,0:T(8,128)S(1)} %get-tuple-element.45.coeff_ref.cb_ref, f32[4,32,548]{2,1,0:T(8,128)S(1)} %collective-permute-done.4.ra.refs_0_, ...), custom_call_target="tpu_custom_call" | custom-call | flops 1509949440 | bytes 4915200 | tf_op jit(solution)/shard_map/pallas_call | solution.py:589
  82.1 1.1 copy-done.1
  83.2 1.2 copy-done.3
  84.4 6.3 %shard_map.135 = (f32[3,512,768]{2,1,0:T(8,128)S(1)}, bf16[512,512]{1,0:T(8,128)(2,1)S(1)}, bf16[512,512]{1,0:T(8,128)(2,1)S(1)}) custom-call(f32[32,72,128]{2,1,0:T(8,128)} %all-to-all-done.x_ref, bf16[2,768,768]{2,1,0:T(8,128)(2,1)} %get-tuple-element.52.first_ref, f32[1,768]{1,0:T(1,128)S(1)} %broadcast_in_dim.16.b1_ref, ...), custom_call_target="tpu_custom_call" | custom-call | flops 3623878656 | bytes 3145728 | tf_op jit(solution)/shard_map/pallas_call | solution.py:610
  90.7 17.0 %shard_map.138 = (f32[16,32,548]{2,1,0:T(8,128)S(1)}, f32[4,32,548]{2,1,0:T(8,128)S(1)}, f32[4,32,548]{2,1,0:T(8,128)S(1)}, f32[16,4,548]{2,1,0:T(4,128)S(1)}, f32[16,4,548]{2,1,0:T(4,128)S(1)}) custom-call(s32[2]{0:T(128)S(1)} %pad_add_fusion.side_ref, f32[512,768]{1,0:T(8,128)S(1)} %copy-done.7, bf16[512,512]{1,0:T(8,128)(2,1)S(1)} %get-tuple-element.53.one_ref, ...), custom_call_target="tpu_custom_call" | custom-call | flops 10871635968 | bytes 11796480 | tf_op jit(solution)/shard_map/pallas_call | solution.py:628
  108.1 1.9 %collective-permute-start.13 = (f32[4,32,548]{2,1,0:T(8,128)S(1)}, f32[4,32,548]{2,1,0:T(8,128)S(1)}, u32[]{:S(2)}, u32[]{:S(2)}) collective-permute-start(f32[4,32,548]{2,1,0:T(8,128)S(1)} %get-tuple-element.66), channel_id=1, source_target_pairs={{4,8},{12,16},{20,24},{8,4},{16,12},{24,20},{5,9},{13,17},{21,25},... | collective-permute-start | bytes 841736 | tf_op jit(solution)/shard_map/ppermute | solution.py:481
  110.0 16.8 %shard_map.136 = (f32[16,32,548]{2,1,0:T(8,128)S(1)}, f32[4,32,548]{2,1,0:T(8,128)S(1)}, f32[4,32,548]{2,1,0:T(8,128)S(1)}, f32[16,4,548]{2,1,0:T(4,128)S(1)}, f32[16,4,548]{2,1,0:T(4,128)S(1)}) custom-call(s32[2]{0:T(128)S(1)} %pad_add_fusion.side_ref, f32[512,768]{1,0:T(8,128)S(1)} %copy-done.4, bf16[512,512]{1,0:T(8,128)(2,1)S(1)} %get-tuple-element.53.one_ref, ...), custom_call_target="tpu_custom_call" | custom-call | flops 10871635968 | bytes 11796480 | tf_op jit(solution)/shard_map/pallas_call | solution.py:628
  126.8 2.4 %collective-permute-start.8 = (f32[4,32,548]{2,1,0:T(8,128)S(1)}, f32[4,32,548]{2,1,0:T(8,128)S(1)}, u32[]{:S(2)}, u32[]{:S(2)}) collective-permute-start(f32[4,32,548]{2,1,0:T(8,128)S(1)} %get-tuple-element.57), channel_id=1, source_target_pairs={{0,4},{8,12},{16,20},{24,28},{4,0},{12,8},{20,16},{28,24},{1,5},{9... | collective-permute-start | bytes 841736 | tf_op jit(solution)/shard_map/ppermute | solution.py:481
  129.3 2.0 %collective-permute-start.9 = (f32[4,32,548]{2,1,0:T(8,128)S(1)}, f32[4,32,548]{2,1,0:T(8,128)S(1)}, u32[]{:S(2)}, u32[]{:S(2)}) collective-permute-start(f32[4,32,548]{2,1,0:T(8,128)S(1)} %get-tuple-element.58), channel_id=1, source_target_pairs={{4,8},{12,16},{20,24},{8,4},{16,12},{24,20},{5,9},{13,17},{21,25},... | collective-permute-start | bytes 841736 | tf_op jit(solution)/shard_map/ppermute | solution.py:481
  132.0 3.8 %collective-permute-start.15 = (f32[24,4,548]{2,1,0:T(4,128)S(1)}, f32[24,4,548]{2,1,0:T(4,128)S(1)}, u32[]{:S(2)}, u32[]{:S(2)}) collective-permute-start(f32[24,4,548]{2,1,0:T(4,128)S(1)} %get-tuple-element.70), channel_id=1, source_target_pairs={{1,2},{2,1},{5,6},{6,5},{9,10},{10,9},{13,14},{14,13},{17,18},{18,... | collective-permute-start | bytes 631304 | tf_op jit(solution)/shard_map/ppermute | solution.py:481
  135.9 7.7 %collective-permute-done.8.ra.refs_0_ = f32[4,32,548]{2,1,0:T(8,128)S(1)} collective-permute-done((f32[4,32,548]{2,1,0:T(8,128)S(1)}, f32[4,32,548]{2,1,0:T(8,128)S(1)}, u32[]{:S(2)}, u32[]{:S(2)}) %collective-permute-start.8) | collective-permute-done | bytes 280608 | tf_op jit(solution)/shard_map/ppermute | solution.py:481
  144.3 2.0 %collective-permute-start.11 = (f32[24,4,548]{2,1,0:T(4,128)S(1)}, f32[24,4,548]{2,1,0:T(4,128)S(1)}, u32[]{:S(2)}, u32[]{:S(2)}) collective-permute-start(f32[24,4,548]{2,1,0:T(4,128)S(1)} %get-tuple-element.62), channel_id=1, source_target_pairs={{1,2},{2,1},{5,6},{6,5},{9,10},{10,9},{13,14},{14,13},{17,18},{18,... | collective-permute-start | bytes 631304 | tf_op jit(solution)/shard_map/ppermute | solution.py:481
  146.4 4.3 %shard_map.140.refs_4_ = f32[2,16,32,548]{3,2,1,0:T(8,128)} custom-call(s32[2]{0:T(128)S(1)} %pad_add_fusion.side_ref, f32[16,32,548]{2,1,0:T(8,128)S(1)} %get-tuple-element.64.field_ref, f32[2,16,32,548]{3,2,1,0:T(8,128)S(1)} %copy-done, f32[3,24,40,128]{3,2,1,0:T(8,128)S(1)} %copy-done.2, f32[4,32,548]{2,1,0:T(8,128)S(1)} %collective-permute-done.12.ra.refs_0_, ...), custom_call_target="tpu_custom_call" | custom-call | flops 24576000 | bytes 3932160 | tf_op jit(solution)/shard_map/pallas_call | solution.py:651
  150.7 1.1 collective-permute-done.11.refs_3_
  151.8 4.3 %shard_map.141 = f32[2,16,32,548]{3,2,1,0:T(8,128)} custom-call(s32[2]{0:T(128)S(1)} %pad_add_fusion.side_ref, f32[16,32,548]{2,1,0:T(8,128)S(1)} %get-tuple-element.56.field_ref, f32[2,16,32,548]{3,2,1,0:T(8,128)S(1)} %copy-done, f32[3,24,40,128]{3,2,1,0:T(8,128)S(1)} %copy-done.2, ...), custom_call_target="tpu_custom_call", output_to_operand_aliasing={{}: (8, {})} | custom-call | flops 24576000 | bytes 3932160 | tf_op jit(solution)/shard_map/pallas_call | solution.py:651
  (45 shorter events, 3.3 us)
Async XLA Ops:
  1.4 1.3 copy-start.8
  4.9 79.5 %all-to-all-start = ((f32[32,72,128]{2,1,0:T(8,128)}), f32[32,72,128]{2,1,0:T(8,128)}, u32[]{:S(2)}, u32[]{:S(2)}) async-start(f32[32,72,128]{2,1,0:T(8,128)} %shard_map.134), calls=%async_computation | async-start | bytes 2359296 | tf_op jit(solution)/shard_map/all_to_all | solution.py:560
  13.3 45.3 %collective-permute-start = (f32[4,32,549]{2,1,0:T(8,128)S(1)}, f32[4,32,549]{2,1,0:T(8,128)S(1)}, u32[]{:S(2)}, u32[]{:S(2)}) collective-permute-start(f32[4,32,549]{2,1,0:T(8,128)S(1)} %get-tuple-element.38), channel_id=1, source_target_pairs={{0,4},{8,12},{16,20},{24,28},{4,0},{12,8},{20,16},{28,24},{1,5},{9... | collective-permute-start | bytes 843272 | tf_op jit(solution)/shard_map/ppermute | solution.py:481
  14.6 44.0 %collective-permute-start.1 = (f32[4,32,549]{2,1,0:T(8,128)S(1)}, f32[4,32,549]{2,1,0:T(8,128)S(1)}, u32[]{:S(2)}, u32[]{:S(2)}) collective-permute-start(f32[4,32,549]{2,1,0:T(8,128)S(1)} %get-tuple-element.39), channel_id=1, source_target_pairs={{4,8},{12,16},{20,24},{8,4},{16,12},{24,20},{5,9},{13,17},{21,25},... | collective-permute-start | bytes 843272 | tf_op jit(solution)/shard_map/ppermute | solution.py:481
  18.5 35.4 %collective-permute-start.4 = (f32[4,32,548]{2,1,0:T(8,128)S(1)}, f32[4,32,548]{2,1,0:T(8,128)S(1)}, u32[]{:S(2)}, u32[]{:S(2)}) collective-permute-start(f32[4,32,548]{2,1,0:T(8,128)S(1)} %get-tuple-element.46), channel_id=1, source_target_pairs={{0,4},{8,12},{16,20},{24,28},{4,0},{12,8},{20,16},{28,24},{1,5},{9... | collective-permute-start | bytes 841736 | tf_op jit(solution)/shard_map/ppermute | solution.py:481
  20.9 33.0 %collective-permute-start.5 = (f32[4,32,548]{2,1,0:T(8,128)S(1)}, f32[4,32,548]{2,1,0:T(8,128)S(1)}, u32[]{:S(2)}, u32[]{:S(2)}) collective-permute-start(f32[4,32,548]{2,1,0:T(8,128)S(1)} %get-tuple-element.47), channel_id=1, source_target_pairs={{4,8},{12,16},{20,24},{8,4},{16,12},{24,20},{5,9},{13,17},{21,25},... | collective-permute-start | bytes 841736 | tf_op jit(solution)/shard_map/ppermute | solution.py:481
  54.5 22.5 %collective-permute-start.6 = (f32[24,4,548]{2,1,0:T(4,128)S(1)}, f32[24,4,548]{2,1,0:T(4,128)S(1)}, u32[]{:S(2)}, u32[]{:S(2)}) collective-permute-start(f32[24,4,548]{2,1,0:T(4,128)S(1)} %get-tuple-element.50), channel_id=1, source_target_pairs={{0,1},{2,3},{1,0},{3,2},{4,5},{6,7},{5,4},{7,6},{8,9},{10,11},{9,8... | collective-permute-start | bytes 631304 | tf_op jit(solution)/shard_map/ppermute | solution.py:481
  55.6 21.4 %collective-permute-start.7 = (f32[24,4,548]{2,1,0:T(4,128)S(1)}, f32[24,4,548]{2,1,0:T(4,128)S(1)}, u32[]{:S(2)}, u32[]{:S(2)}) collective-permute-start(f32[24,4,548]{2,1,0:T(4,128)S(1)} %get-tuple-element.51), channel_id=1, source_target_pairs={{1,2},{2,1},{5,6},{6,5},{9,10},{10,9},{13,14},{14,13},{17,18},{18,... | collective-permute-start | bytes 631304 | tf_op jit(solution)/shard_map/ppermute | solution.py:481
  59.2 11.0 %collective-permute-start.2 = (f32[24,4,549]{2,1,0:T(4,128)S(1)}, f32[24,4,549]{2,1,0:T(4,128)S(1)}, u32[]{:S(2)}, u32[]{:S(2)}) collective-permute-start(f32[24,4,549]{2,1,0:T(4,128)S(1)} %get-tuple-element.42), channel_id=1, source_target_pairs={{0,1},{2,3},{1,0},{3,2},{4,5},{6,7},{5,4},{7,6},{8,9},{10,11},{9,8... | collective-permute-start | bytes 632456 | tf_op jit(solution)/shard_map/ppermute | solution.py:481
  59.3 11.0 %collective-permute-start.3 = (f32[24,4,549]{2,1,0:T(4,128)S(1)}, f32[24,4,549]{2,1,0:T(4,128)S(1)}, u32[]{:S(2)}, u32[]{:S(2)}) collective-permute-start(f32[24,4,549]{2,1,0:T(4,128)S(1)} %get-tuple-element.43), channel_id=1, source_target_pairs={{1,2},{2,1},{5,6},{6,5},{9,10},{10,9},{13,14},{14,13},{17,18},{18,... | collective-permute-start | bytes 632456 | tf_op jit(solution)/shard_map/ppermute | solution.py:481
  61.9 8.3 %copy-start.10 = (f32[768]{0:T(1024)S(1)}, f32[768]{0:T(1024)}, u32[]{:S(2)}) copy-start(f32[768]{0:T(1024)} %param.17) | copy-start | bytes 9220
  61.9 8.4 %copy-start.11 = (f32[768]{0:T(1024)S(1)}, f32[768]{0:T(1024)}, u32[]{:S(2)}) copy-start(f32[768]{0:T(1024)} %param.19) | copy-start | bytes 9220
  61.9 8.4 %copy-start = (f32[2,16,32,548]{3,2,1,0:T(8,128)S(1)}, f32[2,16,32,548]{3,2,1,0:T(8,128)}, u32[]{:S(2)}) copy-start(f32[2,16,32,548]{3,2,1,0:T(8,128)} %base_ref.3) | copy-start | bytes 6733828
  61.9 8.4 %copy-start.5 = (f32[16,32]{1,0:T(8,128)S(1)}, f32[16,32]{1,0:T(8,128)}, u32[]{:S(2)}) copy-start(f32[16,32]{1,0:T(8,128)} %coeff_far.3) | copy-start | bytes 6148
  75.9 1.1 copy-start.6
  77.0 7.4 %copy-start.9 = (s32[32,616]{1,0:T(8,128)S(1)}, s32[32,616]{1,0:T(8,128)}, u32[]{:S(2)}) copy-start(s32[32,616]{1,0:T(8,128)} %mask_ref.1) | copy-start | bytes 236548
  82.1 1.1 copy-start.1
  83.2 1.2 copy-start.3
  84.4 6.3 %copy-start.7 = (f32[512,768]{1,0:T(8,128)S(1)}, f32[512,768]{1,0:T(8,128)}, u32[]{:S(2)}) copy-start(f32[512,768]{1,0:T(8,128)} %copy-done.6) | copy-start | bytes 4718596
  90.7 19.3 %copy-start.4 = (f32[512,768]{1,0:T(8,128)S(1)}, f32[512,768]{1,0:T(8,128)}, u32[]{:S(2)}) copy-start(f32[512,768]{1,0:T(8,128)} %copy-done.3) | copy-start | bytes 4718596
  107.7 23.6 %collective-permute-start.12 = (f32[4,32,548]{2,1,0:T(8,128)S(1)}, f32[4,32,548]{2,1,0:T(8,128)S(1)}, u32[]{:S(2)}, u32[]{:S(2)}) collective-permute-start(f32[4,32,548]{2,1,0:T(8,128)S(1)} %get-tuple-element.65), channel_id=1, source_target_pairs={{0,4},{8,12},{16,20},{24,28},{4,0},{12,8},{20,16},{28,24},{1,5},{9... | collective-permute-start | bytes 841736 | tf_op jit(solution)/shard_map/ppermute | solution.py:481
  108.1 23.2 %collective-permute-start.13 = (f32[4,32,548]{2,1,0:T(8,128)S(1)}, f32[4,32,548]{2,1,0:T(8,128)S(1)}, u32[]{:S(2)}, u32[]{:S(2)}) collective-permute-start(f32[4,32,548]{2,1,0:T(8,128)S(1)} %get-tuple-element.66), channel_id=1, source_target_pairs={{4,8},{12,16},{20,24},{8,4},{16,12},{24,20},{5,9},{13,17},{21,25},... | collective-permute-start | bytes 841736 | tf_op jit(solution)/shard_map/ppermute | solution.py:481
  126.8 19.5 %copy-start.2 = (f32[3,24,40,128]{3,2,1,0:T(8,128)S(1)}, f32[3,24,40,128]{3,2,1,0:T(8,128)}, u32[]{:S(2)}) copy-start(f32[3,24,40,128]{3,2,1,0:T(8,128)} %copy-done.1) | copy-start | bytes 4423684
  126.8 16.8 %collective-permute-start.8 = (f32[4,32,548]{2,1,0:T(8,128)S(1)}, f32[4,32,548]{2,1,0:T(8,128)S(1)}, u32[]{:S(2)}, u32[]{:S(2)}) collective-permute-start(f32[4,32,548]{2,1,0:T(8,128)S(1)} %get-tuple-element.57), channel_id=1, source_target_pairs={{0,4},{8,12},{16,20},{24,28},{4,0},{12,8},{20,16},{28,24},{1,5},{9... | collective-permute-start | bytes 841736 | tf_op jit(solution)/shard_map/ppermute | solution.py:481
  129.3 14.3 %collective-permute-start.9 = (f32[4,32,548]{2,1,0:T(8,128)S(1)}, f32[4,32,548]{2,1,0:T(8,128)S(1)}, u32[]{:S(2)}, u32[]{:S(2)}) collective-permute-start(f32[4,32,548]{2,1,0:T(8,128)S(1)} %get-tuple-element.58), channel_id=1, source_target_pairs={{4,8},{12,16},{20,24},{8,4},{16,12},{24,20},{5,9},{13,17},{21,25},... | collective-permute-start | bytes 841736 | tf_op jit(solution)/shard_map/ppermute | solution.py:481
  132.0 14.4 %collective-permute-start.14 = (f32[24,4,548]{2,1,0:T(4,128)S(1)}, f32[24,4,548]{2,1,0:T(4,128)S(1)}, u32[]{:S(2)}, u32[]{:S(2)}) collective-permute-start(f32[24,4,548]{2,1,0:T(4,128)S(1)} %get-tuple-element.69), channel_id=1, source_target_pairs={{0,1},{2,3},{1,0},{3,2},{4,5},{6,7},{5,4},{7,6},{8,9},{10,11},{9,8... | collective-permute-start | bytes 631304 | tf_op jit(solution)/shard_map/ppermute | solution.py:481
  132.0 14.3 %collective-permute-start.15 = (f32[24,4,548]{2,1,0:T(4,128)S(1)}, f32[24,4,548]{2,1,0:T(4,128)S(1)}, u32[]{:S(2)}, u32[]{:S(2)}) collective-permute-start(f32[24,4,548]{2,1,0:T(4,128)S(1)} %get-tuple-element.70), channel_id=1, source_target_pairs={{1,2},{2,1},{5,6},{6,5},{9,10},{10,9},{13,14},{14,13},{17,18},{18,... | collective-permute-start | bytes 631304 | tf_op jit(solution)/shard_map/ppermute | solution.py:481
  144.2 6.5 %collective-permute-start.10 = (f32[24,4,548]{2,1,0:T(4,128)S(1)}, f32[24,4,548]{2,1,0:T(4,128)S(1)}, u32[]{:S(2)}, u32[]{:S(2)}) collective-permute-start(f32[24,4,548]{2,1,0:T(4,128)S(1)} %get-tuple-element.61), channel_id=1, source_target_pairs={{0,1},{2,3},{1,0},{3,2},{4,5},{6,7},{5,4},{7,6},{8,9},{10,11},{9,8... | collective-permute-start | bytes 631304 | tf_op jit(solution)/shard_map/ppermute | solution.py:481
  144.3 7.5 %collective-permute-start.11 = (f32[24,4,548]{2,1,0:T(4,128)S(1)}, f32[24,4,548]{2,1,0:T(4,128)S(1)}, u32[]{:S(2)}, u32[]{:S(2)}) collective-permute-start(f32[24,4,548]{2,1,0:T(4,128)S(1)} %get-tuple-element.62), channel_id=1, source_target_pairs={{1,2},{2,1},{5,6},{6,5},{9,10},{10,9},{13,14},{14,13},{17,18},{18,... | collective-permute-start | bytes 631304 | tf_op jit(solution)/shard_map/ppermute | solution.py:481
